TPU v7x, 256 devices: a whole 4x4x8 slice. The times are simulated.
256 devices in a mesh: rows: 64 (over x, z_hi, y), experts: 4 (over z_lo, core).
Axes of the slice: x: 4, y: 4, z: 8 (z_hi: 4, z_lo: 2; z = z_hi * 2 + z_lo), core: 2. Of those that a mesh axis runs over, the one named last changes fastest.
Arguments:
- weight: bfloat16 [4, 64, 2048, 512], P('experts', None, 'rows'), may hold values from -3 to 3
- momentum: bfloat16 [4, 64, 2048, 512], P('experts', None, 'rows'), may hold values from -6 to 6
- gradient: bfloat16 [4, 64, 2048, 512], P('experts', None, 'rows'), may hold values from -32 to 32
- assign: int32 [4, 64], P('experts'), may hold values from 0 to 63, each once within a row
Outputs:
- new_weight: bfloat16 [4, 64, 2048, 512], P('experts', None, 'rows')
- new_momentum: bfloat16 [4, 64, 2048, 512], P('experts', None, 'rows')
Inputs may be any that keep to these rules, and one draw needn't show every extreme that they name: Each row of assign names every slot 0 to 63 exactly once; matrix i of group e keeps its momentum in slot assign[e, i].
All inputs are finite; a program needn't handle non-finite values.
Results may differ from a plain program's by a relative error of at most 0.0075.
Values may be sent and summed in bfloat16 or wider, within the bound.
No kernel may reach another device: no remote copies, remote signals or barrier semaphores. Data moves between devices by JAX's collectives and lax.ppermute only.
A program may use at most 64 MiB of HBM per device.

v0:
```python
import functools
import math

import jax
import jax.numpy as jnp
from jax import lax
from jax.sharding import Mesh
from jax.sharding import PartitionSpec as P

ROWS = 2048
COLS = 512
ITERS = 5
ROWS_AXES = ("rows_0", "rows_1", "rows_2")
EXPERTS = ("experts_0", "experts_1")
ROWS_EXPERTS = ("rows_0", "rows_1", "rows_2", "experts_0", "experts_1")


linear_coef = 3.4445
cubic_coef = -4.775
quintic_coef = 2.0315
beta_decay = 0.95
learn_rate = 0.5
weight_decay = 0.1
norm_epsilon = 1e-07
clip_epsilon = 1e-06


def one_axis_at_a_time(shard, axes):
    return functools.reduce(lax.psum, axes, shard)


def in_blocks(shard, dim, peers):
    lengths = shard.shape
    tiles = shard.reshape(*lengths[:dim], peers, lengths[dim] // peers, *lengths[dim + 1 :])
    return jnp.moveaxis(tiles, dim, 0)


def cut_rows(length, count):
    step = length // count
    if step >= 8:
        step -= step % 8
    return [step * k for k in range(1, count)]


def laid_out(tiles, dim):
    tiles = jnp.moveaxis(tiles, 0, dim)
    lengths = tiles.shape
    return tiles.reshape(*lengths[:dim], lengths[dim] * lengths[dim + 1], *lengths[dim + 2 :])


def cut_exchange(shard, axis, pieces, split_dim, concat_dim):
    tiles = in_blocks(shard, split_dim, lax.axis_size(axis))
    widest = max(range(1, max(2, tiles.ndim - 1)), key=lambda d: tiles.shape[d])
    gathered = []
    for piece in jnp.split(tiles, cut_rows(tiles.shape[widest], pieces), axis=widest):
        if piece.size:
            gathered.append(lax.all_to_all(piece, axis, split_axis=0, concat_axis=0, tiled=True))
    return laid_out(jnp.concatenate(gathered, axis=widest), concat_dim)


def orthogonal_stack(stack):
    widened = stack.astype(jnp.float32)
    norms = jnp.sqrt(jnp.sum(widened * widened, axis=(1, 2), keepdims=True))
    iterate = (widened / (norms + norm_epsilon)).astype(jnp.bfloat16)
    for sweep in range(ITERS):
        gram_matrix = jnp.einsum(
            "kri,krj->kij", iterate, iterate, preferred_element_type=jnp.float32
        ).astype(jnp.bfloat16)
        square = jnp.einsum(
            "kij,kjl->kil", gram_matrix, gram_matrix, preferred_element_type=jnp.float32
        )
        polynomial = (cubic_coef * gram_matrix.astype(jnp.float32) + quintic_coef * square).astype(
            jnp.bfloat16
        )
        product = jnp.einsum(
            "kri,kij->krj", iterate, polynomial, preferred_element_type=jnp.float32
        )
        iterate = (linear_coef * iterate.astype(jnp.float32) + product).astype(jnp.bfloat16)
    return iterate


def local(weight, momentum, gradient, assign):
    grad_local = gradient[0]
    mom_local = momentum[0]
    weight_local = weight[0]
    slot_table = assign[0]
    row_devices = lax.axis_size(ROWS_AXES)
    group_devices = lax.axis_size(EXPERTS)
    slot_count, shard_rows, col_count = grad_local.shape
    grad_wide = grad_local.astype(jnp.float32)
    sum_squares = one_axis_at_a_time(jnp.sum(grad_wide * grad_wide), ROWS_EXPERTS)
    clip_limit = math.sqrt(float(slot_count * shard_rows * col_count * row_devices * group_devices))
    clip_factor = jnp.minimum(1.0, clip_limit / (jnp.sqrt(sum_squares) + clip_epsilon))
    inverse = jnp.argsort(slot_table)
    grad_slot = jnp.take(grad_local, inverse, axis=0)
    state = beta_decay * mom_local.astype(jnp.float32) + clip_factor * grad_slot.astype(jnp.float32)
    owned_count = slot_count // row_devices
    update = (clip_factor * grad_slot.astype(jnp.float32) + beta_decay * state).astype(jnp.bfloat16)
    received = lax.all_to_all(
        update.reshape(row_devices, owned_count, shard_rows, col_count),
        ROWS_AXES,
        split_axis=0,
        concat_axis=2,
        tiled=True,
    )
    count = received.shape[1]
    stacked = received.reshape(count, received.shape[2], col_count)
    result = orthogonal_stack(stacked).reshape(received.shape)
    returned = cut_exchange(result, ROWS_AXES, 2, 2, 0)
    ortho_slot = returned.reshape(slot_count, shard_rows, col_count)
    ortho = jnp.take(ortho_slot, slot_table, axis=0)
    shape_scale = 0.2 * math.sqrt(max(ROWS, COLS))
    new_weight = weight_local.astype(jnp.float32) * (
        1.0 - learn_rate * weight_decay
    ) - learn_rate * shape_scale * ortho.astype(jnp.float32)
    return (new_weight.astype(jnp.bfloat16)[None], state.astype(jnp.bfloat16)[None])


def solution(mesh):
    torus = Mesh(
        mesh.devices.reshape(4, 4, 4, 2, 2),
        ("rows_0", "rows_1", "rows_2", "experts_0", "experts_1"),
    )
    placed = (
        P(EXPERTS, None, ROWS_AXES, None),
        P(EXPERTS, None, ROWS_AXES, None),
        P(EXPERTS, None, ROWS_AXES, None),
        P(EXPERTS, None),
    )
    return jax.shard_map(
        local,
        mesh=torus,
        in_specs=placed,
        out_specs=(P(EXPERTS, None, ROWS_AXES, None), P(EXPERTS, None, ROWS_AXES, None)),
        check_vma=False,
    )
```

profile of v0, /device:TPU:8, one launch (start us, length us, event | category | flops | bytes accessed | tf_op | source)
XLA Modules:
  0.0 234.9 jit_solution(9163084922135627753)
XLA Ops:
  0.6 0.0 copy-start.3
  0.6 3.3 %multiply_reduce_fusion = f32[]{:T(128)} fusion(bf16[1,64,32,512]{3,2,1,0:T(8,128)(2,1)} %param.8), kind=kLoop, calls=%fused_computation.17 | loop fusion | flops 3145727 | bytes 2097156 | tf_op jit(solution)/shard_map/reduce_sum | solution.py:91
  3.9 11.1 %psum.35 = f32[]{:T(128)} all-reduce(f32[]{:T(128)} %multiply_reduce_fusion), channel_id=1, replica_groups=mesh['rows_0'=4,'rows_1'=4,'rows_2'=4,'experts_0'=2,'experts_1'=2] {'row..., use_global_device_ids=true, to_apply=%region_1.0 | all-reduce | flops 1 | bytes 8 | tf_op jit(solution)/shard_map/psum | solution.py:29
  15.0 15.5 %psum.36 = f32[]{:T(128)} all-reduce(f32[]{:T(128)} %psum.35), channel_id=1, replica_groups=mesh['rows_0'=4,'rows_1'=4,'rows_2'=4,'experts_0'=2,'experts_1'=2] {'row..., use_global_device_ids=true, to_apply=%region_2.0 | all-reduce | flops 1 | bytes 8 | tf_op jit(solution)/shard_map/psum | solution.py:29
  30.6 0.0 copy-done.3
  30.6 2.0 sort.17
  32.6 9.3 %psum.37 = f32[]{:T(128)} all-reduce(f32[]{:T(128)} %psum.36), channel_id=1, replica_groups=mesh['rows_0'=4,'rows_1'=4,'rows_2'=4,'experts_0'=2,'experts_1'=2] {'row..., use_global_device_ids=true, to_apply=%region_3.0 | all-reduce | flops 1 | bytes 8 | tf_op jit(solution)/shard_map/psum | solution.py:29
  41.9 5.5 %psum.38 = f32[]{:T(128)} all-reduce(f32[]{:T(128)} %psum.37), channel_id=1, replica_groups=mesh['rows_0'=4,'rows_1'=4,'rows_2'=4,'experts_0'=2,'experts_1'=2] {'exp..., use_global_device_ids=true, to_apply=%region_4.0 | all-reduce | flops 1 | bytes 8 | tf_op jit(solution)/shard_map/psum | solution.py:29
  47.5 3.1 %psum.39 = f32[]{:T(128)} all-reduce(f32[]{:T(128)} %psum.38), channel_id=1, replica_groups=mesh['rows_0'=4,'rows_1'=4,'rows_2'=4,'experts_0'=2,'experts_1'=2] {'exp..., use_global_device_ids=true, to_apply=%region_5.0 | all-reduce | flops 1 | bytes 8 | tf_op jit(solution)/shard_map/psum | solution.py:29
  51.2 2.3 gather_fusion
  53.6 4.3 %fusion.4 = (bf16[1,64,32,512]{3,2,1,0:T(8,128)(2,1)}, bf16[64,1,32,512]{3,2,1,0:T(8,128)(2,1)S(1)}) fusion(bf16[1,64,32,512]{3,2,1,0:T(8,128)(2,1)} %param.7, f32[]{:T(128)S(6)} %min_shard_map.3, bf16[64,32,512]{2,1,0:T(8,128)(2,1)S(1)} %gather_fusion, pred[64]{0:T(512)(128)(4,1)S(1)} %compare_and_fusion.1), kind=kLoop, calls=%fused_computation.18 | loop fusion | flops 10485760 | bytes 8388676 | tf_op jit(solution)/shard_map/broadcast_in_dim | solution.py:116
  57.9 60.1 %all_to_all.19 = bf16[64,1,32,512]{3,2,1,0:T(8,128)(2,1)S(1)} all-to-all(bf16[64,1,32,512]{3,2,1,0:T(8,128)(2,1)S(1)} %get-tuple-element.10), channel_id=1, replica_groups=mesh['rows_0'=4,'rows_1'=4,'rows_2'=4,'experts_0'=2,'experts_1'=2] {'row..., dimensions={0} | all-to-all | bytes 4194304 | tf_op jit(solution)/shard_map/all_to_all | solution.py:99
  117.9 1.7 fusion
  120.3 1.2 fusion.1
  121.6 2.5 %copy.19 = bf16[64,1,32,512]{3,2,0,1:T(8,128)(2,1)} copy(bf16[64,1,32,512]{3,0,2,1:T(8,128)(2,1)S(1)} %fusion.1) | data formatting | bytes 4194304 | tf_op jit(solution)/shard_map/convert_element_type | solution.py:64
  124.0 1.3 fusion.22
  125.3 3.8 %add_convert_fusion.4 = bf16[2048,512]{1,0:T(8,128)(2,1)S(1)} fusion(bf16[2048,512]{1,0:T(8,128)(2,1)} %bitcast.77, bf16[512,512]{1,0:T(8,128)(2,1)S(1)} %fusion.22), kind=kOutput, calls=%fused_computation.13 | convolution fusion | flops 1347682304 | bytes 4718592 | tf_op jit(solution)/shard_map/kri,kij->krj/dot_general | solution.py:75
  129.2 1.3 convolution_convert_fusion.3
  130.5 2.9 %add_convert_fusion.3 = bf16[2048,512]{1,0:T(8,128)(2,1)} fusion(bf16[2048,512]{1,0:T(8,128)(2,1)S(1)} %add_convert_fusion.4, bf16[512,512]{1,0:T(8,128)(2,1)S(1)} %convolution_convert_fusion.3), kind=kOutput, calls=%fused_computation.12 | convolution fusion | flops 1347682304 | bytes 4718592 | tf_op jit(solution)/shard_map/kri,kij->krj/dot_general | solution.py:75
  133.4 0.0 copy-start
  133.4 3.6 %convolution_convert_fusion.2 = bf16[512,512]{1,0:T(8,128)(2,1)S(1)} fusion(bf16[2048,512]{1,0:T(8,128)(2,1)} %add_convert_fusion.3), kind=kOutput, calls=%fused_computation.44 | convolution fusion | flops 1074003968 | bytes 2621440 | tf_op jit(solution)/shard_map/kri,krj->kij/dot_general | solution.py:66
  137.0 0.0 copy-done
  137.1 2.9 %add_convert_fusion.2 = bf16[2048,512]{1,0:T(8,128)(2,1)} fusion(bf16[2048,512]{1,0:T(8,128)(2,1)S(1)} %copy-done, bf16[512,512]{1,0:T(8,128)(2,1)S(1)} %convolution_convert_fusion.2), kind=kOutput, calls=%fused_computation.11 | convolution fusion | flops 1347682304 | bytes 4718592 | tf_op jit(solution)/shard_map/kri,kij->krj/dot_general | solution.py:75
  140.0 0.0 copy-start.1
  140.0 3.6 %convolution_convert_fusion.1 = bf16[512,512]{1,0:T(8,128)(2,1)S(1)} fusion(bf16[2048,512]{1,0:T(8,128)(2,1)} %add_convert_fusion.2), kind=kOutput, calls=%fused_computation.43 | convolution fusion | flops 1074003968 | bytes 2621440 | tf_op jit(solution)/shard_map/kri,krj->kij/dot_general | solution.py:66
  143.6 0.0 copy-done.1
  143.6 3.2 %add_convert_fusion.1 = bf16[2048,512]{1,0:T(8,128)(2,1)} fusion(bf16[2048,512]{1,0:T(8,128)(2,1)S(1)} %copy-done.1, bf16[512,512]{1,0:T(8,128)(2,1)S(1)} %convolution_convert_fusion.1), kind=kOutput, calls=%fused_computation.10 | convolution fusion | flops 1347682304 | bytes 4718592 | tf_op jit(solution)/shard_map/kri,kij->krj/dot_general | solution.py:75
  146.8 0.0 copy-start.2
  146.8 3.6 %convolution_convert_fusion = bf16[512,512]{1,0:T(8,128)(2,1)S(1)} fusion(bf16[2048,512]{1,0:T(8,128)(2,1)} %add_convert_fusion.1), kind=kOutput, calls=%fused_computation.42 | convolution fusion | flops 1074003968 | bytes 2621440 | tf_op jit(solution)/shard_map/kri,krj->kij/dot_general | solution.py:66
  150.5 0.0 copy-done.2
  150.5 2.9 %add_convert_fusion = bf16[2048,512]{1,0:T(8,128)(2,1)} fusion(bf16[2048,512]{1,0:T(8,128)(2,1)S(1)} %copy-done.2, bf16[512,512]{1,0:T(8,128)(2,1)S(1)} %convolution_convert_fusion), kind=kOutput, calls=%fused_computation.9 | convolution fusion | flops 1347682304 | bytes 4718592 | tf_op jit(solution)/shard_map/kri,kij->krj/dot_general | solution.py:75
  153.4 2.7 %fusion.45 = (bf16[64,1,1,16,512]{4,3,2,1,0:T(8,128)(2,1)S(1)}, bf16[64,1,1,16,512]{4,3,2,1,0:T(8,128)(2,1)}) fusion(bf16[64,1,1,32,512]{4,3,2,1,0:T(8,128)(2,1)} %bitcast.76), kind=kLoop, calls=%fused_computation.72 | loop fusion | bytes 4194304 | tf_op jit(solution)/shard_map/split | solution.py:55
  156.1 36.4 %all_to_all.20 = bf16[64,1,1,16,512]{4,3,2,1,0:T(8,128)(2,1)S(1)} all-to-all(bf16[64,1,1,16,512]{4,3,2,1,0:T(8,128)(2,1)S(1)} %get-tuple-element.11), channel_id=1, replica_groups=mesh['rows_0'=4,'rows_1'=4,'rows_2'=4,'experts_0'=2,'experts_1'=2] {'row..., dimensions={0} | all-to-all | bytes 2097152 | tf_op jit(solution)/shard_map/all_to_all | solution.py:57
  192.5 6.3 %all-to-all-start.2 = ((bf16[64,1,1,16,512]{4,3,2,1,0:T(8,128)(2,1)}), bf16[64,1,1,16,512]{4,3,2,1,0:T(8,128)(2,1)S(1)}, u32[]{:S(2)}, u32[]{:S(2)}) async-start(bf16[64,1,1,16,512]{4,3,2,1,0:T(8,128)(2,1)} %get-tuple-element.12), calls=%async_computation.2 | async-start | bytes 2097152 | tf_op jit(solution)/shard_map/all_to_all | solution.py:57
  198.9 28.1 %all-to-all-done.2 = bf16[64,1,1,16,512]{4,3,2,1,0:T(8,128)(2,1)S(1)} async-done(((bf16[64,1,1,16,512]{4,3,2,1,0:T(8,128)(2,1)}), bf16[64,1,1,16,512]{4,3,2,1,0:T(8,128)(2,1)S(1)}, u32[]{:S(2)}, u32[]{:S(2)}) %all-to-all-start.2) | async-done | bytes 1048608 | tf_op jit(solution)/shard_map/all_to_all | solution.py:57
  227.0 1.5 maximum_bitcast_fusion
  228.5 2.3 gather_fusion.1
  230.8 4.1 %fusion.6 = bf16[1,64,32,512]{3,2,1,0:T(8,128)(2,1)} fusion(bf16[1,64,32,512]{3,2,1,0:T(8,128)(2,1)} %param.6, bf16[64,32,512]{2,1,0:T(8,128)(2,1)S(1)} %gather_fusion.1, pred[64]{0:T(512)(128)(4,1)S(1)} %compare_and_fusion), kind=kLoop, calls=%fused_computation.20 | loop fusion | flops 7340032 | bytes 6291520 | tf_op jit(solution)/shard_map/broadcast_in_dim | solution.py:116
  (7 shorter events, 0.0 us)
Async XLA Ops:
  0.6 29.9 %copy-start.3 = (s32[1,64]{1,0:T(1,128)S(1)}, s32[1,64]{1,0:T(1,128)}, u32[]{:S(2)}) copy-start(s32[1,64]{1,0:T(1,128)} %param.9) | copy-start | bytes 772
  133.4 3.6 %copy-start = (bf16[2048,512]{1,0:T(8,128)(2,1)S(1)}, bf16[2048,512]{1,0:T(8,128)(2,1)}, u32[]{:S(2)}) copy-start(bf16[2048,512]{1,0:T(8,128)(2,1)} %add_convert_fusion.3) | copy-start | bytes 6291460
  140.0 3.6 %copy-start.1 = (bf16[2048,512]{1,0:T(8,128)(2,1)S(1)}, bf16[2048,512]{1,0:T(8,128)(2,1)}, u32[]{:S(2)}) copy-start(bf16[2048,512]{1,0:T(8,128)(2,1)} %add_convert_fusion.2) | copy-start | bytes 6291460
  146.8 3.6 %copy-start.2 = (bf16[2048,512]{1,0:T(8,128)(2,1)S(1)}, bf16[2048,512]{1,0:T(8,128)(2,1)}, u32[]{:S(2)}) copy-start(bf16[2048,512]{1,0:T(8,128)(2,1)} %add_convert_fusion.1) | copy-start | bytes 6291460
  192.5 34.4 %all-to-all-start.2 = ((bf16[64,1,1,16,512]{4,3,2,1,0:T(8,128)(2,1)}), bf16[64,1,1,16,512]{4,3,2,1,0:T(8,128)(2,1)S(1)}, u32[]{:S(2)}, u32[]{:S(2)}) async-start(bf16[64,1,1,16,512]{4,3,2,1,0:T(8,128)(2,1)} %get-tuple-element.12), calls=%async_computation.2 | async-start | bytes 2097152 | tf_op jit(solution)/shard_map/all_to_all | solution.py:57
where the time goes:
time: 235 us
  blocking collectives  141 us (60%)
  matrix products  29.3 us (12%)
  waiting for transfers between devices  28.1 us (12%)
  other arithmetic  18.2 us (8%)
  local copies, waits for them, and re-layouts  9.76 us (4%)
  starting transfers between devices  6.31 us (3%)
    all_to_all x1, blocking collectives, local(): lax.all_to_all(update.reshape(row_devices, owned_count, shard_rows, col_c...  60.1 us
    psum x5, blocking collectives, one_axis_at_a_time(): return functools.reduce(lax.psum, axes, shard)  44.6 us
    all_to_all x1, blocking collectives, cut_exchange(): lax.all_to_all(piece, axis, split_axis=0, concat_axis=0, tiled=True)  36.4 us
    all_to_all x1, waiting for transfers between devices, cut_exchange(): lax.all_to_all(piece, axis, split_axis=0, concat_axis=0, tiled=True)  28.1 us
    dot_general x5, matrix products, orthogonal_stack(): jnp.einsum('kri,kij->krj', iterate, polynomial, preferred_element_type=jn...  15.8 us
    dot_general x5, matrix products, orthogonal_stack(): jnp.einsum('kri,krj->kij', iterate, iterate, preferred_element_type=jnp.f...  13.5 us
    all_to_all x1, starting transfers between devices, cut_exchange(): lax.all_to_all(piece, axis, split_axis=0, concat_axis=0, tiled=True)  6.31 us
  transfers between devices with their start and end apart: 1, of which 1 were waited for; matrix products, arithmetic and copies ran while one was open for 0% of the time, Pallas kernels for 0%

commit v1 on v0

v1 whole, which is shorter than its diff:
```python
import functools
import math

import jax
import jax.numpy as jnp
from jax import lax
from jax.experimental import pallas as pl
from jax.experimental.pallas import tpu as pltpu
from jax.sharding import Mesh
from jax.sharding import PartitionSpec as P

ROWS = 2048
COLS = 512
ROWS_AXES = ("rows_0", "rows_1", "rows_2")
EXPERTS = ("experts_0", "experts_1")
ALL_AXES = ROWS_AXES + EXPERTS
DEVICES = 256
STAGES = (3, 2)

linear_coef = 3.4445
cubic_coef = -4.775
quintic_coef = 2.0315
beta_decay = 0.95
learn_rate = 0.5
weight_decay = 0.1
norm_epsilon = 1e-07
clip_epsilon = 1e-06
CHUNK = 8

bf16 = jnp.bfloat16
f32 = jnp.float32


def squares_kernel(grad_ref, out_ref, acc_ref):
    step = pl.program_id(0)

    @pl.when(step == 0)
    def _():
        acc_ref[...] = jnp.zeros_like(acc_ref)

    wide = grad_ref[...].astype(f32)
    acc_ref[...] += jnp.sum(wide * wide, axis=0)

    @pl.when(step == pl.num_programs(0) - 1)
    def _():
        folded = acc_ref[:, 0:128]
        for k in range(1, COLS // 128):
            folded = folded + acc_ref[:, 128 * k : 128 * (k + 1)]
        out_ref[...] = jnp.broadcast_to(jnp.sum(folded, axis=0, keepdims=True), out_ref.shape)


def partial_squares(grad):
    slots, rows, cols = grad.shape
    return pl.pallas_call(
        squares_kernel,
        grid=(slots // CHUNK,),
        in_specs=[pl.BlockSpec((CHUNK, rows, cols), lambda i: (i, 0, 0))],
        out_specs=pl.BlockSpec((DEVICES, 128), lambda i: (0, 0)),
        out_shape=jax.ShapeDtypeStruct((DEVICES, 128), f32),
        scratch_shapes=[pltpu.VMEM((rows, cols), f32)],
        compiler_params=pltpu.CompilerParams(vmem_limit_bytes=56 << 20),
        cost_estimate=pl.CostEstimate(flops=2 * grad.size, bytes_accessed=2 * grad.size, transcendentals=0),
        name="squares",
    )(grad)


def clip_from(partials, count):
    total = jnp.sum(partials)
    limit = math.sqrt(float(count))
    return jnp.minimum(1.0, limit / (jnp.sqrt(total) + clip_epsilon))


def fetch(chunk, slots_ref, grad_hbm, mom_hbm, grad_buf, mom_buf, sems):
    base = chunk * CHUNK
    pltpu.make_async_copy(
        grad_hbm.at[pl.ds(base, CHUNK)], grad_buf.at[pl.ds(base, CHUNK)], sems.at[0, chunk]
    ).start()
    for k in range(CHUNK):
        pltpu.make_async_copy(
            mom_hbm.at[slots_ref[base + k]], mom_buf.at[base + k], sems.at[1, chunk]
        ).start()


def await_fetch(chunk, grad_hbm, mom_hbm, grad_buf, mom_buf, sems):
    rows = pl.ds(chunk * CHUNK, CHUNK)
    pltpu.make_async_copy(grad_hbm.at[rows], grad_buf.at[rows], sems.at[0, chunk]).wait()
    pltpu.make_async_copy(mom_hbm.at[rows], mom_buf.at[rows], sems.at[1, chunk]).wait()


def update_kernel(count, slots_ref, part_ref, grad_hbm, mom_hbm, out_hbm, grad_buf, mom_buf, sems, out_sem):
    chunks = grad_buf.shape[0] // CHUNK
    for chunk in range(chunks):
        fetch(chunk, slots_ref, grad_hbm, mom_hbm, grad_buf, mom_buf, sems)
    clip = clip_from(part_ref[...], count)

    @pl.loop(0, chunks)
    def _(chunk):
        await_fetch(chunk, grad_hbm, mom_hbm, grad_buf, mom_buf, sems)
        rows = pl.ds(chunk * CHUNK, CHUNK)
        scaled = clip * grad_buf[rows].astype(f32)
        state = beta_decay * mom_buf[rows].astype(f32) + scaled
        mom_buf[rows] = (scaled + beta_decay * state).astype(bf16)
        pltpu.make_async_copy(mom_buf.at[rows], out_hbm.at[rows], out_sem.at[chunk]).start()

    for chunk in range(chunks):
        rows = pl.ds(chunk * CHUNK, CHUNK)
        pltpu.make_async_copy(mom_buf.at[rows], out_hbm.at[rows], out_sem.at[chunk]).wait()


def state_kernel(count, slots_ref, part_ref, grad_hbm, mom_hbm, out_hbm, grad_buf, mom_buf, sems, out_sem):
    chunks = grad_buf.shape[0] // CHUNK
    for chunk in range(chunks):
        fetch(chunk, slots_ref, grad_hbm, mom_hbm, grad_buf, mom_buf, sems)
    clip = clip_from(part_ref[...], count)

    @pl.loop(0, chunks)
    def _(chunk):
        await_fetch(chunk, grad_hbm, mom_hbm, grad_buf, mom_buf, sems)
        base = chunk * CHUNK
        rows = pl.ds(base, CHUNK)
        state = beta_decay * mom_buf[rows].astype(f32) + clip * grad_buf[rows].astype(f32)
        mom_buf[rows] = state.astype(bf16)
        for k in range(CHUNK):
            pltpu.make_async_copy(
                mom_buf.at[base + k], out_hbm.at[slots_ref[base + k]], out_sem.at[chunk]
            ).start()

    for chunk in range(chunks):
        rows = pl.ds(chunk * CHUNK, CHUNK)
        pltpu.make_async_copy(mom_buf.at[rows], out_hbm.at[rows], out_sem.at[chunk]).wait()


def momentum_call(kernel, name, count, slots, partials, grad, mom):
    chunks = grad.shape[0] // CHUNK
    return pl.pallas_call(
        functools.partial(kernel, count),
        grid_spec=pltpu.PrefetchScalarGridSpec(
            num_scalar_prefetch=1,
            grid=(1,),
            in_specs=[
                pl.BlockSpec(partials.shape, lambda i, s: (0, 0)),
                pl.BlockSpec(memory_space=pl.ANY),
                pl.BlockSpec(memory_space=pl.ANY),
            ],
            out_specs=pl.BlockSpec(memory_space=pl.ANY),
            scratch_shapes=[
                pltpu.VMEM(grad.shape, bf16),
                pltpu.VMEM(grad.shape, bf16),
                pltpu.SemaphoreType.DMA((2, chunks)),
                pltpu.SemaphoreType.DMA((chunks,)),
            ],
        ),
        out_shape=jax.ShapeDtypeStruct(grad.shape, bf16),
        compiler_params=pltpu.CompilerParams(vmem_limit_bytes=56 << 20),
        cost_estimate=pl.CostEstimate(flops=6 * grad.size, bytes_accessed=6 * grad.size, transcendentals=0),
        name=name,
    )(slots, partials, grad, mom)


def gram_of(tall_ref):
    tall = tall_ref[...]
    return lax.dot_general(tall, tall, (((0,), (0,)), ((), ())), preferred_element_type=f32)


def times(left, right):
    return jnp.dot(left, right, preferred_element_type=f32)


def composed(gram, steps):
    row = lax.broadcasted_iota(jnp.int32, gram.shape, 0)
    col = lax.broadcasted_iota(jnp.int32, gram.shape, 1)
    whole = None
    for step in range(steps):
        rounded = gram.astype(bf16)
        kept = rounded.astype(f32)
        poly = (cubic_coef * kept + quintic_coef * times(rounded, rounded)).astype(bf16)
        if whole is None:
            whole = poly.astype(f32) + jnp.where(row == col, linear_coef, 0.0)
        else:
            whole = linear_coef * whole + times(whole.astype(bf16), poly)
        if step + 1 < steps:
            half = linear_coef * kept + times(rounded, poly)
            gram = linear_coef * half + times(half.astype(bf16), poly)
    return whole.astype(bf16)


def orthogonal_kernel(in_ref, out_ref):
    gram = gram_of(in_ref)
    row = lax.broadcasted_iota(jnp.int32, gram.shape, 0)
    col = lax.broadcasted_iota(jnp.int32, gram.shape, 1)
    inverse = 1.0 / (jnp.sqrt(jnp.sum(jnp.where(row == col, gram, 0.0))) + norm_epsilon)
    factor = composed(gram * inverse * inverse, STAGES[0])
    tile = 256
    for k in range(ROWS // tile):
        rows = pl.ds(k * tile, tile)
        out_ref[rows] = (times(in_ref[rows], factor) * inverse).astype(bf16)
    for steps in STAGES[1:]:
        factor = composed(gram_of(out_ref), steps)
        for k in range(ROWS // tile):
            rows = pl.ds(k * tile, tile)
            out_ref[rows] = times(out_ref[rows], factor).astype(bf16)


def orthogonal(tall):
    return pl.pallas_call(
        orthogonal_kernel,
        out_shape=jax.ShapeDtypeStruct(tall.shape, bf16),
        compiler_params=pltpu.CompilerParams(
            vmem_limit_bytes=32 << 20
        ),
        cost_estimate=pl.CostEstimate(flops=8 * 10**9, bytes_accessed=4 * tall.size, transcendentals=0),
        name="orthogonal",
    )(tall)

def local(weight, momentum, gradient, assign):
    grad = gradient[0]
    mom = momentum[0]
    slots = assign[0]
    count = grad.size * lax.axis_size(ALL_AXES)
    shared = lax.all_to_all(
        partial_squares(grad).reshape(DEVICES, 1, 128), ALL_AXES, split_axis=0, concat_axis=0, tiled=True
    ).reshape(DEVICES, 128)
    update = momentum_call(update_kernel, "update", count, slots, shared, grad, mom)
    received = lax.all_to_all(update, ROWS_AXES, split_axis=0, concat_axis=0, tiled=True)
    state = momentum_call(state_kernel, "state", count, slots, shared, grad, mom)
    received, state = lax.optimization_barrier((received, state))
    result = orthogonal(received.reshape(ROWS, COLS)).reshape(received.shape)
    ortho = lax.all_to_all(result, ROWS_AXES, split_axis=0, concat_axis=0, tiled=True)
    shape_scale = 0.2 * math.sqrt(max(ROWS, COLS))
    new_weight = weight[0].astype(f32) * (1.0 - learn_rate * weight_decay) - (
        learn_rate * shape_scale
    ) * ortho.astype(f32)
    return (new_weight.astype(bf16)[None], state[None])


def solution(mesh):
    torus = Mesh(
        mesh.devices.reshape(4, 4, 4, 2, 2),
        ("rows_0", "rows_1", "rows_2", "experts_0", "experts_1"),
    )
    sharded = P(EXPERTS, None, ROWS_AXES, None)
    return jax.shard_map(
        local,
        mesh=torus,
        in_specs=(sharded, sharded, sharded, P(EXPERTS, None)),
        out_specs=(sharded, sharded),
        check_vma=False,
    )
```

time: 235 us -> 163 us (0.69)
  blocking collectives: 141 us -> 81.7 us
  matrix products: 29.3 us -> 0 us
  Pallas kernels: 0 us -> 24.2 us
  waiting for transfers between devices: 28.1 us -> 48.5 us
  other arithmetic: 18.2 us -> 2.34 us
  local copies, waits for them, and re-layouts: 9.76 us -> 0.01 us
    psum x5 -> x0, blocking collectives: 44.6 us -> none  [one_axis_at_a_time(): return functools.reduce(lax.psum, axes, shard)]
    dot_general x10 -> x0, matrix products: 29.3 us -> none  [the longest x5 15.8 us: orthogonal_stack(): jnp.einsum('kri,kij->krj', iterate, polynomial, preferred_element_type=jn...]
    pallas_call x0 -> x4, Pallas kernels: none -> 24.2 us  [the longest x2 9.76 us: momentum_call(): pl.pallas_call(functools.partial(kernel, count), grid_spec=pltpu.Prefetch...]
    all_to_all x1, waiting for transfers between devices: 28.1 us -> 48.5 us  [local(): lax.all_to_all(update, ROWS_AXES, split_axis=0, concat_axis=0, tiled=True)]
    all_to_all x2, blocking collectives: 96.5 us -> 81.7 us  [the longest x1 54.2 us: local(): lax.all_to_all(result, ROWS_AXES, split_axis=0, concat_axis=0, tiled=True)]
    broadcast_in_dim x2 -> x1, other arithmetic: 8.46 us -> 2.34 us  [local(): return (new_weight.astype(bf16)[None], state[None])]
    reduce_sum x2 -> x0, other arithmetic: 4.96 us -> none  [the longest x1 3.28 us: local(): jnp.sum(grad_wide * grad_wide)]
    gather x2 -> x0, local copies, waits for them, and re-layouts: 4.54 us -> none  [the longest x1 2.27 us: local(): grad_slot = jnp.take(grad_local, inverse, axis=0)]
  transfers between devices with their start and end apart: 1 -> 1, of which waited for: 1 -> 1; matrix products, arithmetic and copies ran while one was open for 0% -> 0% of each run, Pallas kernels for 0% -> 3%
where the time goes in v1:
time: 163 us
  blocking collectives  81.7 us (50%)
  waiting for transfers between devices  48.5 us (30%)
  Pallas kernels  24.2 us (15%)
  starting transfers between devices  5.54 us (3%)
  other arithmetic  2.34 us (1%)
    all_to_all x1, blocking collectives, local(): lax.all_to_all(result, ROWS_AXES, split_axis=0, concat_axis=0, tiled=True)  54.2 us
    all_to_all x1, waiting for transfers between devices, local(): lax.all_to_all(update, ROWS_AXES, split_axis=0, concat_axis=0, tiled=True)  48.5 us
    all_to_all x1, blocking collectives, local(): lax.all_to_all(partial_squares(grad).reshape(DEVICES, 1, 128), ALL_AXES,...  27.4 us
    pallas_call x2, Pallas kernels, momentum_call(): pl.pallas_call(functools.partial(kernel, count), grid_spec=pltpu.Prefetch...  9.76 us
    pallas_call x1, Pallas kernels, orthogonal(): pl.pallas_call(orthogonal_kernel, out_shape=jax.ShapeDtypeStruct(tall.sha...  9.69 us
    all_to_all x1, starting transfers between devices, local(): lax.all_to_all(update, ROWS_AXES, split_axis=0, concat_axis=0, tiled=True)  5.54 us
    pallas_call x1, Pallas kernels, partial_squares(): pl.pallas_call(squares_kernel, grid=(slots // CHUNK,), in_specs=[pl.Block...  4.75 us
  transfers between devices with their start and end apart: 1, of which 1 were waited for; matrix products, arithmetic and copies ran while one was open for 0% of the time, Pallas kernels for 3%

profile of v1, /device:TPU:8, one launch (start us, length us, event | category | flops | bytes accessed | tf_op | source)
XLA Modules:
  0.0 162.9 jit_solution(517111610804777458)
XLA Ops:
  0.6 4.7 %squares.1 = f32[256,128]{1,0:T(8,128)} custom-call(bf16[64,32,512]{2,1,0:T(8,128)(2,1)} %bitcast.20), custom_call_target="tpu_custom_call" | custom-call | flops 2097152 | bytes 2097152 | tf_op jit(solution)/shard_map/squares/pallas_call | solution.py:54
  5.4 27.4 %all_to_all.15 = f32[256,1,128]{2,1,0:T(1,128)} all-to-all(f32[256,1,128]{2,1,0:T(1,128)} %bitcast.28), channel_id=1, replica_groups=mesh['rows_0'=4,'rows_1'=4,'rows_2'=4,'experts_0'=2,'experts_1'=2] {'row..., dimensions={0} | all-to-all | bytes 262144 | tf_op jit(solution)/shard_map/all_to_all | solution.py:220
  32.8 4.9 %update.1 = bf16[64,32,512]{2,1,0:T(8,128)(2,1)} custom-call(s32[64]{0:T(128)} %bitcast.29, f32[256,128]{1,0:T(8,128)} %bitcast.26, bf16[64,32,512]{2,1,0:T(8,128)(2,1)} %bitcast.21, bf16[64,32,512]{2,1,0:T(8,128)(2,1)} %bitcast.23), custom_call_target="tpu_custom_call" | custom-call | flops 6291456 | bytes 6291456 | tf_op jit(solution)/shard_map/update/pallas_call | solution.py:135
  37.7 5.5 %all-to-all-start.1 = ((bf16[64,32,512]{2,1,0:T(8,128)(2,1)}), bf16[64,32,512]{2,1,0:T(8,128)(2,1)S(1)}, u32[]{:S(2)}, u32[]{:S(2)}) async-start(bf16[64,32,512]{2,1,0:T(8,128)(2,1)} %update.1), calls=%async_computation.1 | async-start | bytes 4194304 | tf_op jit(solution)/shard_map/all_to_all | solution.py:224
  43.3 4.9 %state.1 = bf16[64,32,512]{2,1,0:T(8,128)(2,1)} custom-call(s32[64]{0:T(128)} %bitcast.30, f32[256,128]{1,0:T(8,128)} %bitcast.27, bf16[64,32,512]{2,1,0:T(8,128)(2,1)} %bitcast.22, bf16[64,32,512]{2,1,0:T(8,128)(2,1)} %bitcast.24), custom_call_target="tpu_custom_call" | custom-call | flops 6291456 | bytes 6291456 | tf_op jit(solution)/shard_map/state/pallas_call | solution.py:135
  48.1 48.5 %all-to-all-done.1 = bf16[64,32,512]{2,1,0:T(8,128)(2,1)S(1)} async-done(((bf16[64,32,512]{2,1,0:T(8,128)(2,1)}), bf16[64,32,512]{2,1,0:T(8,128)(2,1)S(1)}, u32[]{:S(2)}, u32[]{:S(2)}) %all-to-all-start.1) | async-done | bytes 2097184 | tf_op jit(solution)/shard_map/all_to_all | solution.py:224
  96.6 9.7 %orthogonal.1 = bf16[2048,512]{1,0:T(8,128)(2,1)S(1)} custom-call(bf16[2048,512]{1,0:T(8,128)(2,1)S(1)} %bitcast.18), custom_call_target="tpu_custom_call" | custom-call | flops 8000000000 | bytes 4194304 | tf_op jit(solution)/shard_map/orthogonal/pallas_call | solution.py:205
  106.3 0.0 copy-start
  106.3 54.2 %all_to_all.16 = bf16[64,32,512]{2,1,0:T(8,128)(2,1)S(1)} all-to-all(bf16[64,32,512]{2,1,0:T(8,128)(2,1)S(1)} %bitcast.19), channel_id=1, replica_groups=mesh['rows_0'=4,'rows_1'=4,'rows_2'=4,'experts_0'=2,'experts_1'=2] {'row..., dimensions={0} | all-to-all | bytes 4194304 | tf_op jit(solution)/shard_map/all_to_all | solution.py:228
  160.6 0.0 copy-done
  160.6 2.3 %fusion.1 = bf16[1,64,32,512]{3,2,1,0:T(8,128)(2,1)} fusion(bf16[64,32,512]{2,1,0:T(8,128)(2,1)S(1)} %all_to_all.16, bf16[1,64,32,512]{3,2,1,0:T(8,128)(2,1)S(1)} %copy-done), kind=kLoop, calls=%fused_computation.2 | loop fusion | flops 6291456 | bytes 6291456 | tf_op jit(solution)/shard_map/broadcast_in_dim | solution.py:233
Async XLA Ops:
  37.7 58.9 %all-to-all-start.1 = ((bf16[64,32,512]{2,1,0:T(8,128)(2,1)}), bf16[64,32,512]{2,1,0:T(8,128)(2,1)S(1)}, u32[]{:S(2)}, u32[]{:S(2)}) async-start(bf16[64,32,512]{2,1,0:T(8,128)(2,1)} %update.1), calls=%async_computation.1 | async-start | bytes 4194304 | tf_op jit(solution)/shard_map/all_to_all | solution.py:224
  106.3 54.3 %copy-start = (bf16[1,64,32,512]{3,2,1,0:T(8,128)(2,1)S(1)}, bf16[1,64,32,512]{3,2,1,0:T(8,128)(2,1)}, u32[]{:S(2)}) copy-start(bf16[1,64,32,512]{3,2,1,0:T(8,128)(2,1)} %param.4) | copy-start | bytes 6291460

commit v2 on v1

v2 whole, which is shorter than its diff:
```python
import functools
import math

import jax
import jax.numpy as jnp
from jax import lax
from jax.experimental import pallas as pl
from jax.experimental.pallas import tpu as pltpu
from jax.sharding import Mesh
from jax.sharding import PartitionSpec as P


ROWS = 2048
COLS = 512
ROWS_AXES = ("rows_0", "rows_1", "rows_2")
EXPERTS = ("experts_0", "experts_1")
ALL_AXES = ROWS_AXES + EXPERTS
DEVICES = 256
ITERS = 5
PLANE = ("rows_0", "rows_2")
DEPTH = "rows_1"
SENDING = ((2,), (1, 3), (0,))
RETURNING = ((0,), (1, 3), (2,))
SIDE = 128
BLOCKS = tuple((i, j) for i in range(4) for j in range(i, 4))

linear_coef = 3.4445
cubic_coef = -4.775
quintic_coef = 2.0315
beta_decay = 0.95
learn_rate = 0.5
weight_decay = 0.1
norm_epsilon = 1e-07
clip_epsilon = 1e-06
CHUNK = 8
LARGE_GRANT = 56 << 20
SMALL_GRANT = 16 << 20

bf16 = jnp.bfloat16
f32 = jnp.float32


def squares_kernel(grad_hbm, out_ref, grad_buf, acc_ref, sems):
    chunks = grad_buf.shape[0] // CHUNK
    for chunk in range(chunks):
        rows = pl.ds(chunk * CHUNK, CHUNK)
        pltpu.make_async_copy(grad_hbm.at[rows], grad_buf.at[rows], sems.at[chunk]).start()
    acc_ref[...] = jnp.zeros_like(acc_ref)

    @pl.loop(0, chunks)
    def _(chunk):
        rows = pl.ds(chunk * CHUNK, CHUNK)
        pltpu.make_async_copy(grad_hbm.at[rows], grad_buf.at[rows], sems.at[chunk]).wait()
        wide = grad_buf[rows].astype(f32)
        acc_ref[...] += jnp.sum(wide * wide, axis=0)

    folded = acc_ref[:, 0:128]
    for k in range(1, COLS // 128):
        folded = folded + acc_ref[:, 128 * k : 128 * (k + 1)]
    out_ref[...] = jnp.broadcast_to(jnp.sum(folded, axis=0, keepdims=True), out_ref.shape)


def partial_squares(grad):
    slots, rows, cols = grad.shape
    return pl.pallas_call(
        squares_kernel,
        in_specs=[pl.BlockSpec(memory_space=pltpu.HBM)],
        out_shape=jax.ShapeDtypeStruct((DEVICES, 128), f32),
        scratch_shapes=[
            pltpu.VMEM(grad.shape, bf16),
            pltpu.VMEM((rows, cols), f32),
            pltpu.SemaphoreType.DMA((slots // CHUNK,)),
        ],
        compiler_params=pltpu.CompilerParams(vmem_limit_bytes=LARGE_GRANT),
        cost_estimate=pl.CostEstimate(flops=2 * grad.size, bytes_accessed=2 * grad.size, transcendentals=0),
        name="squares",
    )(grad)


def clip_from(partials, count):
    total = jnp.sum(partials)
    limit = math.sqrt(float(count))
    return jnp.minimum(1.0, limit / (jnp.sqrt(total) + clip_epsilon))


def rows_of(peer, away, plane):
    return peer * 4 + lax.rem(plane + away, 4)


def pack_kernel(
    count, group, place_ref, slots_ref, part_ref, grad_hbm, mom_hbm, out_hbm, out_buf, grad_buf, mom_buf, sems, out_sem
):
    plane = place_ref[0]
    peers = out_buf.shape[0]
    rows = grad_buf.shape[2]
    for peer in range(peers):
        for k, away in enumerate(group):
            matrix = rows_of(peer, away, plane)
            pltpu.make_async_copy(grad_hbm.at[matrix], grad_buf.at[peer, k], sems.at[0, peer]).start()
            pltpu.make_async_copy(mom_hbm.at[slots_ref[matrix]], mom_buf.at[peer, k], sems.at[1, peer]).start()
    clip = clip_from(part_ref[...], count)

    @pl.loop(0, peers)
    def _(peer):
        pltpu.make_async_copy(grad_hbm.at[pl.ds(0, len(group))], grad_buf.at[peer], sems.at[0, peer]).wait()
        pltpu.make_async_copy(mom_hbm.at[pl.ds(0, len(group))], mom_buf.at[peer], sems.at[1, peer]).wait()
        for k in range(len(group)):
            scaled = clip * grad_buf[peer, k].astype(f32)
            state = beta_decay * mom_buf[peer, k].astype(f32) + scaled
            out_buf[peer, k * rows : (k + 1) * rows] = (scaled + beta_decay * state).astype(bf16)
        pltpu.make_async_copy(out_buf.at[peer], out_hbm.at[peer], out_sem).start()

    pltpu.make_async_copy(out_buf, out_hbm, out_sem).wait()


def packed(group, count, place, slots, partials, grad, mom):
    slot_count, rows, cols = grad.shape
    peers = slot_count // 4
    shape = (peers, len(group) * rows, cols)
    buffer = pltpu.VMEM((peers, len(group), rows, cols), bf16)
    size = peers * len(group) * rows * cols
    return pl.pallas_call(
        functools.partial(pack_kernel, count, group),
        grid_spec=pltpu.PrefetchScalarGridSpec(
            num_scalar_prefetch=2,
            grid=(1,),
            in_specs=[
                pl.BlockSpec(partials.shape, lambda i, p, s: (0, 0)),
                pl.BlockSpec(memory_space=pltpu.HBM),
                pl.BlockSpec(memory_space=pltpu.HBM),
            ],
            out_specs=pl.BlockSpec(memory_space=pltpu.HBM),
            scratch_shapes=[
                pltpu.VMEM(shape, bf16),
                buffer,
                buffer,
                pltpu.SemaphoreType.DMA((2, peers)),
                pltpu.SemaphoreType.DMA(()),
            ],
        ),
        out_shape=jax.ShapeDtypeStruct(shape, bf16),
        compiler_params=pltpu.CompilerParams(vmem_limit_bytes=LARGE_GRANT),
        cost_estimate=pl.CostEstimate(flops=6 * size, bytes_accessed=6 * size, transcendentals=0),
        name="pack",
    )(place, slots, partials, grad, mom)


def state_kernel(count, slots_ref, part_ref, grad_hbm, mom_hbm, out_hbm, grad_buf, mom_buf, sems, out_sem):
    chunks = grad_buf.shape[0] // CHUNK
    for chunk in range(chunks):
        base = chunk * CHUNK
        pltpu.make_async_copy(
            grad_hbm.at[pl.ds(base, CHUNK)], grad_buf.at[pl.ds(base, CHUNK)], sems.at[0, chunk]
        ).start()
        for k in range(CHUNK):
            pltpu.make_async_copy(
                mom_hbm.at[slots_ref[base + k]], mom_buf.at[base + k], sems.at[1, chunk]
            ).start()
    clip = clip_from(part_ref[...], count)

    @pl.loop(0, chunks)
    def _(chunk):
        base = chunk * CHUNK
        rows = pl.ds(base, CHUNK)
        pltpu.make_async_copy(grad_hbm.at[rows], grad_buf.at[rows], sems.at[0, chunk]).wait()
        pltpu.make_async_copy(mom_hbm.at[rows], mom_buf.at[rows], sems.at[1, chunk]).wait()
        state = beta_decay * mom_buf[rows].astype(f32) + clip * grad_buf[rows].astype(f32)
        mom_buf[rows] = state.astype(bf16)
        for k in range(CHUNK):
            pltpu.make_async_copy(
                mom_buf.at[base + k], out_hbm.at[slots_ref[base + k]], out_sem.at[chunk]
            ).start()

    for chunk in range(chunks):
        rows = pl.ds(chunk * CHUNK, CHUNK)
        pltpu.make_async_copy(mom_buf.at[rows], out_hbm.at[rows], out_sem.at[chunk]).wait()


def new_state(count, slots, partials, grad, mom):
    chunks = grad.shape[0] // CHUNK
    return pl.pallas_call(
        functools.partial(state_kernel, count),
        grid_spec=pltpu.PrefetchScalarGridSpec(
            num_scalar_prefetch=1,
            grid=(1,),
            in_specs=[
                pl.BlockSpec(partials.shape, lambda i, s: (0, 0)),
                pl.BlockSpec(memory_space=pltpu.HBM),
                pl.BlockSpec(memory_space=pltpu.HBM),
            ],
            out_specs=pl.BlockSpec(memory_space=pltpu.HBM),
            scratch_shapes=[
                pltpu.VMEM(grad.shape, bf16),
                pltpu.VMEM(grad.shape, bf16),
                pltpu.SemaphoreType.DMA((2, chunks)),
                pltpu.SemaphoreType.DMA((chunks,)),
            ],
        ),
        out_shape=jax.ShapeDtypeStruct(grad.shape, bf16),
        compiler_params=pltpu.CompilerParams(vmem_limit_bytes=LARGE_GRANT),
        cost_estimate=pl.CostEstimate(flops=6 * grad.size, bytes_accessed=6 * grad.size, transcendentals=0),
        name="state",
    )(slots, partials, grad, mom)


def times(left, right):
    return jnp.dot(left, right, preferred_element_type=f32)


def gram_of(tall):
    return lax.dot_general(tall, tall, (((0,), (0,)), ((), ())), preferred_element_type=f32)


def rows_at(in_ref, k):
    part = in_ref[:, k * (in_ref.shape[1] // 2) : (k + 1) * (in_ref.shape[1] // 2)] if k is not None else in_ref[...]
    return part.reshape(part.shape[0] * part.shape[1], part.shape[2])


def store_upper(out_ref, full):
    for n, (i, j) in enumerate(BLOCKS):
        out_ref[n * SIDE : (n + 1) * SIDE, :] = full[
            i * SIDE : (i + 1) * SIDE, j * SIDE : (j + 1) * SIDE
        ].astype(out_ref.dtype)


def load_full(full_ref, blocks):
    for n, (i, j) in enumerate(BLOCKS):
        block = blocks[n * SIDE : (n + 1) * SIDE, :]
        full_ref[i * SIDE : (i + 1) * SIDE, j * SIDE : (j + 1) * SIDE] = block.astype(full_ref.dtype)
        if i != j:
            full_ref[j * SIDE : (j + 1) * SIDE, i * SIDE : (i + 1) * SIDE] = block.T.astype(full_ref.dtype)


def gram_kernel(in_ref, *out_refs):
    for k, out_ref in enumerate(out_refs):
        store_upper(out_ref, gram_of(rows_at(in_ref, k if len(out_refs) > 1 else None)))


def partial_grams(received, group):
    shape = jax.ShapeDtypeStruct((len(BLOCKS) * SIDE, SIDE), bf16)
    return pl.pallas_call(
        gram_kernel,
        out_shape=[shape] * len(group),
        compiler_params=pltpu.CompilerParams(vmem_limit_bytes=SMALL_GRANT),
        cost_estimate=pl.CostEstimate(
            flops=2 * received.size * COLS, bytes_accessed=2 * received.size, transcendentals=0
        ),
        name="gram",
    )(received)


def composed(gram, steps):
    row = lax.broadcasted_iota(jnp.int32, gram.shape, 0)
    col = lax.broadcasted_iota(jnp.int32, gram.shape, 1)
    whole = None
    for step in range(steps):
        rounded = gram.astype(bf16)
        kept = rounded.astype(f32)
        poly = (cubic_coef * kept + quintic_coef * times(rounded, rounded)).astype(bf16)
        if whole is None:
            whole = poly.astype(f32) + jnp.where(row == col, linear_coef, 0.0)
        else:
            whole = linear_coef * whole + times(whole.astype(bf16), poly)
        if step + 1 < steps:
            half = linear_coef * kept + times(rounded, poly)
            gram = linear_coef * half + times(half.astype(bf16), poly)
    return whole


def factor_kernel(own_ref, a_ref, b_ref, c_ref, out_ref, full_ref):
    others = a_ref[...].astype(f32) + b_ref[...].astype(f32) + c_ref[...].astype(f32)
    load_full(full_ref, others)
    gram = gram_of(rows_at(own_ref, None)) + full_ref[...]
    row = lax.broadcasted_iota(jnp.int32, gram.shape, 0)
    col = lax.broadcasted_iota(jnp.int32, gram.shape, 1)
    inverse = 1.0 / (jnp.sqrt(jnp.sum(jnp.where(row == col, gram, 0.0))) + norm_epsilon)
    store_upper(out_ref, composed(gram * inverse * inverse, ITERS) * inverse)


def shared_factor(own, parts):
    return pl.pallas_call(
        factor_kernel,
        out_shape=jax.ShapeDtypeStruct((len(BLOCKS) * SIDE, SIDE), bf16),
        scratch_shapes=[pltpu.VMEM((COLS, COLS), f32)],
        compiler_params=pltpu.CompilerParams(vmem_limit_bytes=SMALL_GRANT),
        cost_estimate=pl.CostEstimate(flops=5 * 10**9, bytes_accessed=4 * own.size, transcendentals=0),
        name="factor",
    )(own, *parts)


def apply_kernel(in_ref, *refs):
    factors, (out_hbm, out_buf, full_ref, out_sem) = refs[:-4], refs[-4:]
    rows = in_ref.shape[1] // len(factors)
    for k, factor in enumerate(factors):
        load_full(full_ref, factor[...].astype(f32))
        product = times(rows_at(in_ref, k if len(factors) > 1 else None), full_ref[...])
        out_buf[:, k * rows : (k + 1) * rows] = product.reshape(in_ref.shape[0], rows, COLS).astype(bf16)
    copy = pltpu.make_async_copy(out_buf, out_hbm, out_sem)
    copy.start()
    copy.wait()


def applied(received, factors):
    return pl.pallas_call(
        apply_kernel,
        out_shape=jax.ShapeDtypeStruct(received.shape, bf16),
        out_specs=pl.BlockSpec(memory_space=pltpu.HBM),
        scratch_shapes=[
            pltpu.VMEM(received.shape, bf16),
            pltpu.VMEM((COLS, COLS), bf16),
            pltpu.SemaphoreType.DMA(()),
        ],
        compiler_params=pltpu.CompilerParams(vmem_limit_bytes=SMALL_GRANT),
        cost_estimate=pl.CostEstimate(
            flops=2 * received.size * COLS, bytes_accessed=4 * received.size, transcendentals=0
        ),
        name="apply",
    )(received, *factors)


def finish_kernel(group, place_ref, ortho_ref, weight_hbm, *refs):
    out_hbm, weight_buf, sems, out_sem = refs[-4:]
    plane = place_ref[0]
    peers = ortho_ref.shape[0]
    rows = weight_buf.shape[2]
    scale = learn_rate * 0.2 * math.sqrt(max(ROWS, COLS))
    for peer in range(peers):
        for k, away in enumerate(group):
            pltpu.make_async_copy(
                weight_hbm.at[rows_of(peer, away, plane)], weight_buf.at[peer, k], sems.at[peer]
            ).start()

    @pl.loop(0, peers)
    def _(peer):
        pltpu.make_async_copy(weight_hbm.at[pl.ds(0, len(group))], weight_buf.at[peer], sems.at[peer]).wait()
        for k, away in enumerate(group):
            ortho = ortho_ref[peer, k * rows : (k + 1) * rows].astype(f32)
            weight = weight_buf[peer, k].astype(f32)
            weight_buf[peer, k] = (weight * (1.0 - learn_rate * weight_decay) - scale * ortho).astype(bf16)
            pltpu.make_async_copy(
                weight_buf.at[peer, k], out_hbm.at[rows_of(peer, away, plane)], out_sem.at[peer]
            ).start()

    for peer in range(peers):
        pltpu.make_async_copy(weight_buf.at[peer], out_hbm.at[pl.ds(0, len(group))], out_sem.at[peer]).wait()


def finished(group, place, ortho, weight, before):
    peers = ortho.shape[0]
    rows = weight.shape[1]
    inplace = pl.BlockSpec(memory_space=pltpu.HBM)
    earlier = () if before is None else (before,)
    return pl.pallas_call(
        functools.partial(finish_kernel, group),
        grid_spec=pltpu.PrefetchScalarGridSpec(
            num_scalar_prefetch=1,
            grid=(1,),
            in_specs=[pl.BlockSpec(ortho.shape, lambda i, p: (0, 0, 0)), inplace] + [inplace] * len(earlier),
            out_specs=inplace,
            scratch_shapes=[
                pltpu.VMEM((peers, len(group), rows, COLS), bf16),
                pltpu.SemaphoreType.DMA((peers,)),
                pltpu.SemaphoreType.DMA((peers,)),
            ],
        ),
        out_shape=jax.ShapeDtypeStruct(weight.shape, bf16),
        input_output_aliases={3: 0} if earlier else {},
        compiler_params=pltpu.CompilerParams(vmem_limit_bytes=SMALL_GRANT),
        cost_estimate=pl.CostEstimate(flops=3 * ortho.size, bytes_accessed=6 * ortho.size, transcendentals=0),
        name="finish",
    )(place, ortho, weight, *earlier)


def shifted(value, planes):
    count = lax.axis_size(DEPTH)
    return lax.ppermute(value, DEPTH, [(k, (k + planes) % count) for k in range(count)])


def across(value):
    return lax.all_to_all(value, PLANE, split_axis=0, concat_axis=0, tiled=True)


def local(weight, momentum, gradient, assign):
    grad = gradient[0]
    mom = momentum[0]
    slots = assign[0]
    place = lax.axis_index(DEPTH).reshape(1)
    count = grad.size * lax.axis_size(ALL_AXES)
    shared = lax.all_to_all(
        partial_squares(grad).reshape(DEVICES, 1, 128), ALL_AXES, split_axis=0, concat_axis=0, tiled=True
    ).reshape(DEVICES, 128)
    held = {}
    parts = []
    for group in SENDING:
        ready = packed(group, count, place, slots, shared, grad, mom)
        held[group] = across(ready)
        if group == (0,):
            continue
        grams = partial_grams(held[group], group)
        for away, part in zip(group, grams):
            parts.append(shifted(part, away))
    state = new_state(count, slots, shared, grad, mom)
    factor = shared_factor(held[(0,)], parts)
    result = None
    for group in RETURNING:
        factors = []
        for away in group:
            factors.append(shifted(factor, -away) if away else factor)
        ready = applied(held[group], factors)
        ortho = across(ready)
        result = finished(group, place, ortho, weight[0], result)
    return (result[None], state[None])


def solution(mesh):
    torus = Mesh(
        mesh.devices.reshape(4, 4, 4, 2, 2),
        ("rows_0", "rows_1", "rows_2", "experts_0", "experts_1"),
    )
    sharded = P(EXPERTS, None, ROWS_AXES, None)
    return jax.shard_map(
        local,
        mesh=torus,
        in_specs=(sharded, sharded, sharded, P(EXPERTS, None)),
        out_specs=(sharded, sharded),
        check_vma=False,
    )
```

time: 163 us -> 188 us (1.15)
  blocking collectives: 81.7 us -> 0 us
  starting transfers between devices: 5.54 us -> 63 us
  waiting for transfers between devices: 48.5 us -> 82.3 us
  Pallas kernels: 24.2 us -> 39.7 us
  other arithmetic: 2.34 us -> 0 us
    all_to_all x2 -> x0, blocking collectives: 81.7 us -> none  [the longest x1 54.2 us: local(): lax.all_to_all(result, ROWS_AXES, split_axis=0, concat_axis=0, tiled=True)]
    ppermute x0 -> x6, waiting for transfers between devices: none -> 51.8 us  [shifted(): lax.ppermute(value, DEPTH, [(k, (k + planes) % count) for k in range(coun...]
    all_to_all x1 -> x7, starting transfers between devices: 5.54 us -> 51 us  [the longest x6 36.4 us: across(): return lax.all_to_all(value, PLANE, split_axis=0, concat_axis=0, tiled=True)]
    all_to_all x1 -> x7, waiting for transfers between devices: 48.5 us -> 30.4 us  [the longest x6 18.1 us: across(): return lax.all_to_all(value, PLANE, split_axis=0, concat_axis=0, tiled=True)]
    pallas_call x4 -> x14, Pallas kernels: 24.2 us -> 39.7 us  [the longest x3 11.5 us: packed(): pl.pallas_call(functools.partial(pack_kernel, count, group), grid_spec=pl...]
    ppermute x0 -> x6, starting transfers between devices: none -> 12 us  [shifted(): lax.ppermute(value, DEPTH, [(k, (k + planes) % count) for k in range(coun...]
    broadcast_in_dim x1 -> x0, other arithmetic: 2.34 us -> none  [local(): return (new_weight.astype(bf16)[None], state[None])]
  transfers between devices with their start and end apart: 1 -> 13, of which waited for: 1 -> 10; matrix products, arithmetic and copies ran while one was open for 0% -> 0% of each run, Pallas kernels for 3% -> 12%
where the time goes in v2:
time: 188 us; the launch traced here: 187 us
  waiting for transfers between devices  82.3 us (44%)
  starting transfers between devices  63 us (34%)
  Pallas kernels  39.7 us (21%)
    ppermute x6, waiting for transfers between devices, shifted(): lax.ppermute(value, DEPTH, [(k, (k + planes) % count) for k in range(coun...  51.8 us
    all_to_all x6, starting transfers between devices, across(): return lax.all_to_all(value, PLANE, split_axis=0, concat_axis=0, tiled=True)  36.4 us
    all_to_all x6, waiting for transfers between devices, across(): return lax.all_to_all(value, PLANE, split_axis=0, concat_axis=0, tiled=True)  18.1 us
    all_to_all x1, starting transfers between devices, local(): lax.all_to_all(partial_squares(grad).reshape(DEVICES, 1, 128), ALL_AXES,...  14.6 us
    all_to_all x1, waiting for transfers between devices, local(): lax.all_to_all(partial_squares(grad).reshape(DEVICES, 1, 128), ALL_AXES,...  12.3 us
    ppermute x6, starting transfers between devices, shifted(): lax.ppermute(value, DEPTH, [(k, (k + planes) % count) for k in range(coun...  12 us
    pallas_call x3, Pallas kernels, packed(): pl.pallas_call(functools.partial(pack_kernel, count, group), grid_spec=pl...  11.5 us
    pallas_call x3, Pallas kernels, finished(): pl.pallas_call(functools.partial(finish_kernel, group), grid_spec=pltpu.P...  7.48 us
  transfers between devices with their start and end apart: 13, of which 10 were waited for; matrix products, arithmetic and copies ran while one was open for 0% of the time, Pallas kernels for 12%

profile of v2, /device:TPU:8, one launch (start us, length us, event | category | flops | bytes accessed | tf_op | source)
XLA Modules:
  0.0 186.6 jit_solution(7065594846379230629)
XLA Ops:
  0.6 2.3 %squares.1 = f32[256,128]{1,0:T(8,128)} custom-call(bf16[64,32,512]{2,1,0:T(8,128)(2,1)} %bitcast.14), custom_call_target="tpu_custom_call" | custom-call | flops 2097152 | bytes 2097152 | tf_op jit(solution)/shard_map/squares/pallas_call | solution.py:65
  2.9 14.6 %all-to-all-start = ((f32[256,1,128]{2,1,0:T(1,128)}), f32[256,1,128]{2,1,0:T(1,128)S(1)}, u32[]{:S(2)}, u32[]{:S(2)}) async-start(f32[256,1,128]{2,1,0:T(1,128)} %bitcast.29), calls=%async_computation | async-start | bytes 262144 | tf_op jit(solution)/shard_map/all_to_all | solution.py:389
  17.5 12.3 %all-to-all-done = f32[256,1,128]{2,1,0:T(1,128)S(1)} async-done(((f32[256,1,128]{2,1,0:T(1,128)}), f32[256,1,128]{2,1,0:T(1,128)S(1)}, u32[]{:S(2)}, u32[]{:S(2)}) %all-to-all-start) | async-done | bytes 131104 | tf_op jit(solution)/shard_map/all_to_all | solution.py:389
  29.8 0.0 copy-start.3
  29.8 0.7 copy-done.3
  30.5 3.7 %pack.3 = bf16[16,32,512]{2,1,0:T(8,128)(2,1)} custom-call(s32[1]{0:T(128)} %bitcast.place_ref, s32[64]{0:T(128)} %bitcast.30, f32[256,128]{1,0:T(8,128)} %bitcast.24, bf16[64,32,512]{2,1,0:T(8,128)(2,1)} %bitcast.15, bf16[64,32,512]{2,1,0:T(8,128)(2,1)} %bitcast.19), custom_call_target="tpu_custom_call" | custom-call | flops 1572864 | bytes 1572864 | tf_op jit(solution)/shard_map/pack/pallas_call | solution.py:122
  34.2 4.8 %all-to-all-start.1 = ((bf16[16,32,512]{2,1,0:T(8,128)(2,1)}), bf16[16,32,512]{2,1,0:T(8,128)(2,1)S(1)}, u32[]{:S(2)}, u32[]{:S(2)}) async-start(bf16[16,32,512]{2,1,0:T(8,128)(2,1)} %pack.3), calls=%async_computation.1 | async-start | bytes 1048576 | tf_op jit(solution)/shard_map/all_to_all | solution.py:380
  39.0 4.0 %pack.5 = bf16[16,64,512]{2,1,0:T(8,128)(2,1)} custom-call(s32[1]{0:T(128)} %bitcast.place_ref, s32[64]{0:T(128)} %bitcast.31, f32[256,128]{1,0:T(8,128)} %bitcast.25, bf16[64,32,512]{2,1,0:T(8,128)(2,1)} %bitcast.16, bf16[64,32,512]{2,1,0:T(8,128)(2,1)} %bitcast.20), custom_call_target="tpu_custom_call" | custom-call | flops 3145728 | bytes 3145728 | tf_op jit(solution)/shard_map/pack/pallas_call | solution.py:122
  43.1 6.2 %all-to-all-done.1.in_ref = bf16[16,32,512]{2,1,0:T(8,128)(2,1)S(1)} async-done(((bf16[16,32,512]{2,1,0:T(8,128)(2,1)}), bf16[16,32,512]{2,1,0:T(8,128)(2,1)S(1)}, u32[]{:S(2)}, u32[]{:S(2)}) %all-to-all-start.1) | async-done | bytes 524320 | tf_op jit(solution)/shard_map/all_to_all | solution.py:380
  49.3 4.9 %all-to-all-start.3 = ((bf16[16,64,512]{2,1,0:T(8,128)(2,1)}), bf16[16,64,512]{2,1,0:T(8,128)(2,1)S(1)}, u32[]{:S(2)}, u32[]{:S(2)}) async-start(bf16[16,64,512]{2,1,0:T(8,128)(2,1)} %pack.5), calls=%async_computation.3 | async-start | bytes 2097152 | tf_op jit(solution)/shard_map/all_to_all | solution.py:380
  54.2 3.7 %pack.4 = bf16[16,32,512]{2,1,0:T(8,128)(2,1)} custom-call(s32[1]{0:T(128)} %bitcast.place_ref, s32[64]{0:T(128)} %bitcast.32, f32[256,128]{1,0:T(8,128)} %bitcast.26, bf16[64,32,512]{2,1,0:T(8,128)(2,1)} %bitcast.17, bf16[64,32,512]{2,1,0:T(8,128)(2,1)} %bitcast.21), custom_call_target="tpu_custom_call" | custom-call | flops 1572864 | bytes 1572864 | tf_op jit(solution)/shard_map/pack/pallas_call | solution.py:122
  57.9 11.1 %all-to-all-done.3.in_ref = bf16[16,64,512]{2,1,0:T(8,128)(2,1)S(1)} async-done(((bf16[16,64,512]{2,1,0:T(8,128)(2,1)}), bf16[16,64,512]{2,1,0:T(8,128)(2,1)S(1)}, u32[]{:S(2)}, u32[]{:S(2)}) %all-to-all-start.3) | async-done | bytes 1048608 | tf_op jit(solution)/shard_map/all_to_all | solution.py:380
  68.9 5.0 %all-to-all-start.2 = ((bf16[16,32,512]{2,1,0:T(8,128)(2,1)}), bf16[16,32,512]{2,1,0:T(8,128)(2,1)S(1)}, u32[]{:S(2)}, u32[]{:S(2)}) async-start(bf16[16,32,512]{2,1,0:T(8,128)(2,1)} %pack.4), calls=%async_computation.2 | async-start | bytes 1048576 | tf_op jit(solution)/shard_map/all_to_all | solution.py:380
  73.9 0.5 gram.2
  74.4 2.1 %collective-permute-start = (bf16[1280,128]{1,0:T(8,128)(2,1)S(1)}, bf16[1280,128]{1,0:T(8,128)(2,1)S(1)}, u32[]{:S(2)}, u32[]{:S(2)}) collective-permute-start(bf16[1280,128]{1,0:T(8,128)(2,1)S(1)} %gram.2), channel_id=1, source_target_pairs={{0,32},{16,48},{32,0},{48,16},{1,33},{17,49},{33,1},{49,17},{2,34}... | collective-permute-start | bytes 983048 | tf_op jit(solution)/shard_map/ppermute | solution.py:376
  76.4 1.2 gram.3
  77.6 1.8 collective-permute-start.1
  79.4 2.4 %collective-permute-start.2 = (bf16[1280,128]{1,0:T(8,128)(2,1)S(1)}, bf16[1280,128]{1,0:T(8,128)(2,1)}, u32[]{:S(2)}, u32[]{:S(2)}) collective-permute-start(bf16[1280,128]{1,0:T(8,128)(2,1)S(1)} %get-tuple-element.5), channel_id=1, source_target_pairs={{0,48},{16,0},{32,16},{48,32},{1,49},{17,1},{33,17},{49,33},{2,50}... | collective-permute-start | bytes 983048 | tf_op jit(solution)/shard_map/ppermute | solution.py:376
  81.8 0.9 all-to-all-done.2.own_ref.in_ref
  82.6 12.8 %collective-permute-done.a_ref = bf16[1280,128]{1,0:T(8,128)(2,1)S(1)} collective-permute-done((bf16[1280,128]{1,0:T(8,128)(2,1)S(1)}, bf16[1280,128]{1,0:T(8,128)(2,1)S(1)}, u32[]{:S(2)}, u32[]{:S(2)}) %collective-permute-start) | collective-permute-done | bytes 327712 | tf_op jit(solution)/shard_map/ppermute | solution.py:376
  95.4 3.6 %collective-permute-done.1.b_ref = bf16[1280,128]{1,0:T(8,128)(2,1)S(1)} collective-permute-done((bf16[1280,128]{1,0:T(8,128)(2,1)}, bf16[1280,128]{1,0:T(8,128)(2,1)S(1)}, u32[]{:S(2)}, u32[]{:S(2)}) %collective-permute-start.1) | collective-permute-done | bytes 327712 | tf_op jit(solution)/shard_map/ppermute | solution.py:376
  99.0 5.6 %collective-permute-done.2.c_ref = bf16[1280,128]{1,0:T(8,128)(2,1)} collective-permute-done((bf16[1280,128]{1,0:T(8,128)(2,1)S(1)}, bf16[1280,128]{1,0:T(8,128)(2,1)}, u32[]{:S(2)}, u32[]{:S(2)}) %collective-permute-start.2) | collective-permute-done | bytes 327712 | tf_op jit(solution)/shard_map/ppermute | solution.py:376
  104.7 7.3 %factor.1.refs_0_ = bf16[1280,128]{1,0:T(8,128)(2,1)S(1)} custom-call(bf16[16,32,512]{2,1,0:T(8,128)(2,1)S(1)} %all-to-all-done.2.own_ref.in_ref, bf16[1280,128]{1,0:T(8,128)(2,1)S(1)} %collective-permute-done.a_ref, bf16[1280,128]{1,0:T(8,128)(2,1)S(1)} %collective-permute-done.1.b_ref, bf16[1280,128]{1,0:T(8,128)(2,1)} %collective-permute-done.2.c_ref), custom_call_target="tpu_custom_call" | custom-call | flops 5000000000 | bytes 1048576 | tf_op jit(solution)/shard_map/factor/pallas_call | solution.py:281
  112.0 1.3 apply.5
  113.3 7.2 %all-to-all-start.6 = ((bf16[16,32,512]{2,1,0:T(8,128)(2,1)}), bf16[16,32,512]{2,1,0:T(8,128)(2,1)S(1)}, u32[]{:S(2)}, u32[]{:S(2)}) async-start(bf16[16,32,512]{2,1,0:T(8,128)(2,1)} %apply.5), calls=%async_computation.6 | async-start | bytes 1048576 | tf_op jit(solution)/shard_map/all_to_all | solution.py:380
  120.6 3.5 %collective-permute-start.5 = (bf16[1280,128]{1,0:T(8,128)(2,1)S(1)}, bf16[1280,128]{1,0:T(8,128)(2,1)S(1)}, u32[]{:S(2)}, u32[]{:S(2)}) collective-permute-start(bf16[1280,128]{1,0:T(8,128)(2,1)S(1)} %factor.1.refs_0_), channel_id=1, source_target_pairs={{0,16},{16,32},{32,48},{48,0},{1,17},{17,33},{33,49},{49,1},{2,18}... | collective-permute-start | bytes 983048 | tf_op jit(solution)/shard_map/ppermute | solution.py:376
  124.1 0.6 collective-permute-start.4
  124.7 11.1 %collective-permute-done.5.refs_1_ = bf16[1280,128]{1,0:T(8,128)(2,1)S(1)} collective-permute-done((bf16[1280,128]{1,0:T(8,128)(2,1)S(1)}, bf16[1280,128]{1,0:T(8,128)(2,1)S(1)}, u32[]{:S(2)}, u32[]{:S(2)}) %collective-permute-start.5) | collective-permute-done | bytes 327712 | tf_op jit(solution)/shard_map/ppermute | solution.py:376
  135.8 4.1 %collective-permute-done.4.refs_0_ = bf16[1280,128]{1,0:T(8,128)(2,1)S(1)} collective-permute-done((bf16[1280,128]{1,0:T(8,128)(2,1)S(1)}, bf16[1280,128]{1,0:T(8,128)(2,1)S(1)}, u32[]{:S(2)}, u32[]{:S(2)}) %collective-permute-start.4) | collective-permute-done | bytes 327712 | tf_op jit(solution)/shard_map/ppermute | solution.py:376
  139.9 1.8 apply.4
  141.8 0.0 all-to-all-done.6.ortho_ref
  141.8 0.0 copy-start.1
  141.8 7.2 %all-to-all-start.5 = ((bf16[16,64,512]{2,1,0:T(8,128)(2,1)}), bf16[16,64,512]{2,1,0:T(8,128)(2,1)S(1)}, u32[]{:S(2)}, u32[]{:S(2)}) async-start(bf16[16,64,512]{2,1,0:T(8,128)(2,1)} %apply.4), calls=%async_computation.5 | async-start | bytes 2097152 | tf_op jit(solution)/shard_map/all_to_all | solution.py:380
  149.0 1.7 collective-permute-start.3
  150.7 14.6 %collective-permute-done.3.refs_0_ = bf16[1280,128]{1,0:T(8,128)(2,1)S(1)} collective-permute-done((bf16[1280,128]{1,0:T(8,128)(2,1)S(1)}, bf16[1280,128]{1,0:T(8,128)(2,1)S(1)}, u32[]{:S(2)}, u32[]{:S(2)}) %collective-permute-start.3) | collective-permute-done | bytes 327712 | tf_op jit(solution)/shard_map/ppermute | solution.py:376
  165.3 1.4 apply.3
  166.6 0.0 all-to-all-done.5.ortho_ref
  166.7 0.0 copy-done.1
  166.7 7.2 %all-to-all-start.4 = ((bf16[16,32,512]{2,1,0:T(8,128)(2,1)}), bf16[16,32,512]{2,1,0:T(8,128)(2,1)}, u32[]{:S(2)}, u32[]{:S(2)}) async-start(bf16[16,32,512]{2,1,0:T(8,128)(2,1)} %apply.3), calls=%async_computation.4 | async-start | bytes 1048576 | tf_op jit(solution)/shard_map/all_to_all | solution.py:380
  173.9 0.0 copy-start
  173.9 0.0 copy-start.2
  173.9 5.0 %state.1 = bf16[64,32,512]{2,1,0:T(8,128)(2,1)} custom-call(s32[64]{0:T(128)} %bitcast.33, f32[256,128]{1,0:T(8,128)} %bitcast.27, bf16[64,32,512]{2,1,0:T(8,128)(2,1)} %bitcast.18, bf16[64,32,512]{2,1,0:T(8,128)(2,1)} %bitcast.22), custom_call_target="tpu_custom_call" | custom-call | flops 6291456 | bytes 6291456 | tf_op jit(solution)/shard_map/state/pallas_call | solution.py:181
  178.9 0.0 copy-done
  179.0 0.0 copy-done.2
  179.0 1.9 finish.3.refs_0_
  180.8 2.7 %finish.4.refs_0_ = bf16[64,32,512]{2,1,0:T(8,128)(2,1)} custom-call(s32[1]{0:T(128)} %bitcast.place_ref, bf16[16,64,512]{2,1,0:T(8,128)(2,1)S(1)} %all-to-all-done.5.ortho_ref, bf16[64,32,512]{2,1,0:T(8,128)(2,1)S(1)} %bitcast.12, bf16[64,32,512]{2,1,0:T(8,128)(2,1)} %finish.3.refs_0_), custom_call_target="tpu_custom_call", output_to_operand_aliasing={{}: (3, {})} | custom-call | flops 1572864 | bytes 3145728 | tf_op jit(solution)/shard_map/finish/pallas_call | solution.py:353
  183.6 0.0 all-to-all-done.4.ortho_ref
  183.6 2.9 %finish.5 = bf16[64,32,512]{2,1,0:T(8,128)(2,1)} custom-call(s32[1]{0:T(128)} %bitcast.place_ref, bf16[16,32,512]{2,1,0:T(8,128)(2,1)} %all-to-all-done.4.ortho_ref, bf16[64,32,512]{2,1,0:T(8,128)(2,1)S(1)} %bitcast.13, bf16[64,32,512]{2,1,0:T(8,128)(2,1)} %finish.4.refs_0_), custom_call_target="tpu_custom_call", output_to_operand_aliasing={{}: (3, {})} | custom-call | flops 786432 | bytes 1572864 | tf_op jit(solution)/shard_map/finish/pallas_call | solution.py:353
Async XLA Ops:
  2.9 26.9 %all-to-all-start = ((f32[256,1,128]{2,1,0:T(1,128)}), f32[256,1,128]{2,1,0:T(1,128)S(1)}, u32[]{:S(2)}, u32[]{:S(2)}) async-start(f32[256,1,128]{2,1,0:T(1,128)} %bitcast.29), calls=%async_computation | async-start | bytes 262144 | tf_op jit(solution)/shard_map/all_to_all | solution.py:389
  29.8 0.7 copy-start.3
  34.2 15.0 %all-to-all-start.1 = ((bf16[16,32,512]{2,1,0:T(8,128)(2,1)}), bf16[16,32,512]{2,1,0:T(8,128)(2,1)S(1)}, u32[]{:S(2)}, u32[]{:S(2)}) async-start(bf16[16,32,512]{2,1,0:T(8,128)(2,1)} %pack.3), calls=%async_computation.1 | async-start | bytes 1048576 | tf_op jit(solution)/shard_map/all_to_all | solution.py:380
  49.3 19.7 %all-to-all-start.3 = ((bf16[16,64,512]{2,1,0:T(8,128)(2,1)}), bf16[16,64,512]{2,1,0:T(8,128)(2,1)S(1)}, u32[]{:S(2)}, u32[]{:S(2)}) async-start(bf16[16,64,512]{2,1,0:T(8,128)(2,1)} %pack.5), calls=%async_computation.3 | async-start | bytes 2097152 | tf_op jit(solution)/shard_map/all_to_all | solution.py:380
  68.9 13.7 %all-to-all-start.2 = ((bf16[16,32,512]{2,1,0:T(8,128)(2,1)}), bf16[16,32,512]{2,1,0:T(8,128)(2,1)S(1)}, u32[]{:S(2)}, u32[]{:S(2)}) async-start(bf16[16,32,512]{2,1,0:T(8,128)(2,1)} %pack.4), calls=%async_computation.2 | async-start | bytes 1048576 | tf_op jit(solution)/shard_map/all_to_all | solution.py:380
  74.4 21.1 %collective-permute-start = (bf16[1280,128]{1,0:T(8,128)(2,1)S(1)}, bf16[1280,128]{1,0:T(8,128)(2,1)S(1)}, u32[]{:S(2)}, u32[]{:S(2)}) collective-permute-start(bf16[1280,128]{1,0:T(8,128)(2,1)S(1)} %gram.2), channel_id=1, source_target_pairs={{0,32},{16,48},{32,0},{48,16},{1,33},{17,49},{33,1},{49,17},{2,34}... | collective-permute-start | bytes 983048 | tf_op jit(solution)/shard_map/ppermute | solution.py:376
  77.6 21.4 %collective-permute-start.1 = (bf16[1280,128]{1,0:T(8,128)(2,1)}, bf16[1280,128]{1,0:T(8,128)(2,1)S(1)}, u32[]{:S(2)}, u32[]{:S(2)}) collective-permute-start(bf16[1280,128]{1,0:T(8,128)(2,1)} %get-tuple-element.4), channel_id=1, source_target_pairs={{0,16},{16,32},{32,48},{48,0},{1,17},{17,33},{33,49},{49,1},{2,18}... | collective-permute-start | bytes 983048 | tf_op jit(solution)/shard_map/ppermute | solution.py:376
  79.4 25.3 %collective-permute-start.2 = (bf16[1280,128]{1,0:T(8,128)(2,1)S(1)}, bf16[1280,128]{1,0:T(8,128)(2,1)}, u32[]{:S(2)}, u32[]{:S(2)}) collective-permute-start(bf16[1280,128]{1,0:T(8,128)(2,1)S(1)} %get-tuple-element.5), channel_id=1, source_target_pairs={{0,48},{16,0},{32,16},{48,32},{1,49},{17,1},{33,17},{49,33},{2,50}... | collective-permute-start | bytes 983048 | tf_op jit(solution)/shard_map/ppermute | solution.py:376
  113.3 28.5 %all-to-all-start.6 = ((bf16[16,32,512]{2,1,0:T(8,128)(2,1)}), bf16[16,32,512]{2,1,0:T(8,128)(2,1)S(1)}, u32[]{:S(2)}, u32[]{:S(2)}) async-start(bf16[16,32,512]{2,1,0:T(8,128)(2,1)} %apply.5), calls=%async_computation.6 | async-start | bytes 1048576 | tf_op jit(solution)/shard_map/all_to_all | solution.py:380
  120.6 15.3 %collective-permute-start.5 = (bf16[1280,128]{1,0:T(8,128)(2,1)S(1)}, bf16[1280,128]{1,0:T(8,128)(2,1)S(1)}, u32[]{:S(2)}, u32[]{:S(2)}) collective-permute-start(bf16[1280,128]{1,0:T(8,128)(2,1)S(1)} %factor.1.refs_0_), channel_id=1, source_target_pairs={{0,16},{16,32},{32,48},{48,0},{1,17},{17,33},{33,49},{49,1},{2,18}... | collective-permute-start | bytes 983048 | tf_op jit(solution)/shard_map/ppermute | solution.py:376
  124.1 15.9 %collective-permute-start.4 = (bf16[1280,128]{1,0:T(8,128)(2,1)S(1)}, bf16[1280,128]{1,0:T(8,128)(2,1)S(1)}, u32[]{:S(2)}, u32[]{:S(2)}) collective-permute-start(bf16[1280,128]{1,0:T(8,128)(2,1)S(1)} %factor.1.refs_0_), channel_id=1, source_target_pairs={{0,48},{16,0},{32,16},{48,32},{1,49},{17,1},{33,17},{49,33},{2,50}... | collective-permute-start | bytes 983048 | tf_op jit(solution)/shard_map/ppermute | solution.py:376
  141.8 24.9 %copy-start.1 = (bf16[16,32,512]{2,1,0:T(8,128)(2,1)}, bf16[16,32,512]{2,1,0:T(8,128)(2,1)S(1)}, u32[]{:S(2)}) copy-start(bf16[16,32,512]{2,1,0:T(8,128)(2,1)S(1)} %all-to-all-done.6.ortho_ref) | copy-start | bytes 1572868
  141.8 24.8 %all-to-all-start.5 = ((bf16[16,64,512]{2,1,0:T(8,128)(2,1)}), bf16[16,64,512]{2,1,0:T(8,128)(2,1)S(1)}, u32[]{:S(2)}, u32[]{:S(2)}) async-start(bf16[16,64,512]{2,1,0:T(8,128)(2,1)} %apply.4), calls=%async_computation.5 | async-start | bytes 2097152 | tf_op jit(solution)/shard_map/all_to_all | solution.py:380
  149.0 16.2 %collective-permute-start.3 = (bf16[1280,128]{1,0:T(8,128)(2,1)S(1)}, bf16[1280,128]{1,0:T(8,128)(2,1)S(1)}, u32[]{:S(2)}, u32[]{:S(2)}) collective-permute-start(bf16[1280,128]{1,0:T(8,128)(2,1)S(1)} %factor.1.refs_0_), channel_id=1, source_target_pairs={{0,32},{16,48},{32,0},{48,16},{1,33},{17,49},{33,1},{49,17},{2,34}... | collective-permute-start | bytes 983048 | tf_op jit(solution)/shard_map/ppermute | solution.py:376
  166.7 16.9 %all-to-all-start.4 = ((bf16[16,32,512]{2,1,0:T(8,128)(2,1)}), bf16[16,32,512]{2,1,0:T(8,128)(2,1)}, u32[]{:S(2)}, u32[]{:S(2)}) async-start(bf16[16,32,512]{2,1,0:T(8,128)(2,1)} %apply.3), calls=%async_computation.4 | async-start | bytes 1048576 | tf_op jit(solution)/shard_map/all_to_all | solution.py:380
  173.9 5.0 %copy-start = (bf16[1,64,32,512]{3,2,1,0:T(8,128)(2,1)S(1)}, bf16[1,64,32,512]{3,2,1,0:T(8,128)(2,1)}, u32[]{:S(2)}) copy-start(bf16[1,64,32,512]{3,2,1,0:T(8,128)(2,1)} %param.4) | copy-start | bytes 6291460
  173.9 5.0 %copy-start.2 = (bf16[16,32,512]{2,1,0:T(8,128)(2,1)S(1)}, bf16[16,32,512]{2,1,0:T(8,128)(2,1)}, u32[]{:S(2)}) copy-start(bf16[16,32,512]{2,1,0:T(8,128)(2,1)} %copy-done.1) | copy-start | bytes 1572868

commit v3 on v2

--- a/solution.py
+++ b/solution.py
@@ -15,11 +15,12 @@
 ROWS_AXES = ("rows_0", "rows_1", "rows_2")
 EXPERTS = ("experts_0", "experts_1")
 ALL_AXES = ROWS_AXES + EXPERTS
-DEVICES = 256
 ITERS = 5
 PLANE = ("rows_0", "rows_2")
 DEPTH = "rows_1"
-SENDING = ((2,), (1, 3), (0,))
+OTHERS = ("rows_1", "experts_0", "experts_1")
+EARLY = 2
+SENDING = ((1, 3), (0,))
 RETURNING = ((0,), (1, 3), (2,))
 SIDE = 128
 BLOCKS = tuple((i, j) for i in range(4) for j in range(i, 4))
@@ -40,45 +41,95 @@
 f32 = jnp.float32
 
 
-def squares_kernel(grad_hbm, out_ref, grad_buf, acc_ref, sems):
+def first_kernel(place_ref, slots_ref, grad_hbm, mom_hbm, out_hbm, grad_buf, acc_ref, out_buf, grad_sems, sems, out_sem):
+    plane = place_ref[0]
     chunks = grad_buf.shape[0] // CHUNK
+    peers, rows = out_buf.shape[0], grad_buf.shape[1]
     for chunk in range(chunks):
-        rows = pl.ds(chunk * CHUNK, CHUNK)
-        pltpu.make_async_copy(grad_hbm.at[rows], grad_buf.at[rows], sems.at[chunk]).start()
+        part = pl.ds(chunk * CHUNK, CHUNK)
+        pltpu.make_async_copy(grad_hbm.at[part], grad_buf.at[part], grad_sems.at[chunk]).start()
+    for peer in range(peers):
+        matrix = rows_of(peer, EARLY, plane)
+        pltpu.make_async_copy(grad_hbm.at[matrix], out_buf.at[peer, pl.ds(0, rows)], sems.at[0]).start()
+        pltpu.make_async_copy(
+            mom_hbm.at[slots_ref[matrix]], out_buf.at[peer, pl.ds(rows, rows)], sems.at[1]
+        ).start()
     acc_ref[...] = jnp.zeros_like(acc_ref)
 
     @pl.loop(0, chunks)
     def _(chunk):
-        rows = pl.ds(chunk * CHUNK, CHUNK)
-        pltpu.make_async_copy(grad_hbm.at[rows], grad_buf.at[rows], sems.at[chunk]).wait()
-        wide = grad_buf[rows].astype(f32)
+        part = pl.ds(chunk * CHUNK, CHUNK)
+        pltpu.make_async_copy(grad_hbm.at[part], grad_buf.at[part], grad_sems.at[chunk]).wait()
+        wide = grad_buf[part].astype(f32)
         acc_ref[...] += jnp.sum(wide * wide, axis=0)
 
     folded = acc_ref[:, 0:128]
     for k in range(1, COLS // 128):
         folded = folded + acc_ref[:, 128 * k : 128 * (k + 1)]
-    out_ref[...] = jnp.broadcast_to(jnp.sum(folded, axis=0, keepdims=True), out_ref.shape)
-
-
-def partial_squares(grad):
-    slots, rows, cols = grad.shape
-    return pl.pallas_call(
-        squares_kernel,
-        in_specs=[pl.BlockSpec(memory_space=pltpu.HBM)],
-        out_shape=jax.ShapeDtypeStruct((DEVICES, 128), f32),
-        scratch_shapes=[
-            pltpu.VMEM(grad.shape, bf16),
-            pltpu.VMEM((rows, cols), f32),
-            pltpu.SemaphoreType.DMA((slots // CHUNK,)),
-        ],
+    lanes = jnp.sum(folded, axis=0, keepdims=True)
+    high = lanes.astype(bf16)
+    rest = lanes - high.astype(f32)
+    middle = rest.astype(bf16)
+    low = (rest - middle.astype(f32)).astype(bf16)
+    block = jnp.concatenate(
+        [jnp.broadcast_to(term, (8, 128)) for term in (high, middle, low, jnp.zeros_like(low))], axis=1
+    )
+    for peer in range(peers):
+        out_buf[peer, 2 * rows : 2 * rows + 8] = block
+    blocks = grad_hbm.at[pl.ds(0, peers)]
+    pltpu.make_async_copy(blocks, out_buf.at[:, pl.ds(0, rows)], sems.at[0]).wait()
+    pltpu.make_async_copy(blocks, out_buf.at[:, pl.ds(rows, rows)], sems.at[1]).wait()
+    copy = pltpu.make_async_copy(out_buf, out_hbm, out_sem)
+    copy.start()
+    copy.wait()
+
+
+def first_chunk(place, slots, grad, mom):
+    slot_count, rows, cols = grad.shape
+    shape = (slot_count // 4, 2 * rows + 8, cols)
+    return pl.pallas_call(
+        first_kernel,
+        grid_spec=pltpu.PrefetchScalarGridSpec(
+            num_scalar_prefetch=2,
+            grid=(1,),
+            in_specs=[pl.BlockSpec(memory_space=pltpu.HBM)] * 2,
+            out_specs=pl.BlockSpec(memory_space=pltpu.HBM),
+            scratch_shapes=[
+                pltpu.VMEM(grad.shape, bf16),
+                pltpu.VMEM((rows, cols), f32),
+                pltpu.VMEM(shape, bf16),
+                pltpu.SemaphoreType.DMA((slot_count // CHUNK,)),
+                pltpu.SemaphoreType.DMA((2,)),
+                pltpu.SemaphoreType.DMA(()),
+            ],
+        ),
+        out_shape=jax.ShapeDtypeStruct(shape, bf16),
         compiler_params=pltpu.CompilerParams(vmem_limit_bytes=LARGE_GRANT),
-        cost_estimate=pl.CostEstimate(flops=2 * grad.size, bytes_accessed=2 * grad.size, transcendentals=0),
-        name="squares",
-    )(grad)
+        cost_estimate=pl.CostEstimate(flops=2 * grad.size, bytes_accessed=5 * grad.size, transcendentals=0),
+        name="first",
+    )(place, slots, grad, mom)
+
+
+def plane_kernel(in_ref, out_ref):
+    total = jnp.zeros((8, 128), f32)
+    start = in_ref.shape[1] - 8
+    for peer in range(in_ref.shape[0]):
+        for k in range(3):
+            total = total + in_ref[peer, start:, 128 * k : 128 * (k + 1)].astype(f32)
+    out_ref[...] = jnp.broadcast_to(total[None], out_ref.shape)
+
+
+def plane_squares(received, others):
+    return pl.pallas_call(
+        plane_kernel,
+        out_shape=jax.ShapeDtypeStruct((others, 8, 128), f32),
+        compiler_params=pltpu.CompilerParams(vmem_limit_bytes=SMALL_GRANT),
+        name="plane",
+    )(received)
 
 
 def clip_from(partials, count):
-    total = jnp.sum(partials)
+    total = jnp.sum(partials[:, 0, :])
     limit = math.sqrt(float(count))
     return jnp.minimum(1.0, limit / (jnp.sqrt(total) + clip_epsilon))
 
@@ -125,7 +176,7 @@
             num_scalar_prefetch=2,
             grid=(1,),
             in_specs=[
-                pl.BlockSpec(partials.shape, lambda i, p, s: (0, 0)),
+                pl.BlockSpec(partials.shape, lambda i, p, s: (0, 0, 0)),
                 pl.BlockSpec(memory_space=pltpu.HBM),
                 pl.BlockSpec(memory_space=pltpu.HBM),
             ],
@@ -184,7 +235,7 @@
             num_scalar_prefetch=1,
             grid=(1,),
             in_specs=[
-                pl.BlockSpec(partials.shape, lambda i, s: (0, 0)),
+                pl.BlockSpec(partials.shape, lambda i, s: (0, 0, 0)),
                 pl.BlockSpec(memory_space=pltpu.HBM),
                 pl.BlockSpec(memory_space=pltpu.HBM),
             ],
@@ -247,6 +298,31 @@
         ),
         name="gram",
     )(received)
+
+
+def early_kernel(count, part_ref, in_ref, rows_ref, gram_ref):
+    clip = clip_from(part_ref[...], count)
+    rows = rows_ref.shape[1]
+    scaled = clip * in_ref[:, 0:rows].astype(f32)
+    state = beta_decay * in_ref[:, rows : 2 * rows].astype(f32) + scaled
+    rows_ref[...] = (scaled + beta_decay * state).astype(bf16)
+    store_upper(gram_ref, gram_of(rows_at(rows_ref, None)))
+
+
+def early_gram(count, partials, received):
+    peers, height, cols = received.shape
+    return pl.pallas_call(
+        functools.partial(early_kernel, count),
+        out_shape=[
+            jax.ShapeDtypeStruct((peers, (height - 8) // 2, cols), bf16),
+            jax.ShapeDtypeStruct((len(BLOCKS) * SIDE, SIDE), bf16),
+        ],
+        compiler_params=pltpu.CompilerParams(vmem_limit_bytes=SMALL_GRANT),
+        cost_estimate=pl.CostEstimate(
+            flops=received.size * COLS, bytes_accessed=4 * received.size, transcendentals=0
+        ),
+        name="early",
+    )(partials, received)
 
 
 def composed(gram, steps):
@@ -386,11 +462,13 @@
     slots = assign[0]
     place = lax.axis_index(DEPTH).reshape(1)
     count = grad.size * lax.axis_size(ALL_AXES)
-    shared = lax.all_to_all(
-        partial_squares(grad).reshape(DEVICES, 1, 128), ALL_AXES, split_axis=0, concat_axis=0, tiled=True
-    ).reshape(DEVICES, 128)
     held = {}
     parts = []
+    early = across(first_chunk(place, slots, grad, mom))
+    partial = plane_squares(early, lax.axis_size(OTHERS))
+    shared = lax.all_to_all(partial, OTHERS, split_axis=0, concat_axis=0, tiled=True)
+    held[(EARLY,)], part = early_gram(count, shared, early)
+    parts.append(shifted(part, EARLY))
     for group in SENDING:
         ready = packed(group, count, place, slots, shared, grad, mom)
         held[group] = across(ready)

time: 188 us -> 192 us (1.021)
  blocking collectives: 0 us -> 40.7 us
  starting transfers between devices: 63 us -> 42.7 us
  waiting for transfers between devices: 82.3 us -> 70.1 us
  Pallas kernels: 39.7 us -> 36.4 us
    all_to_all x0 -> x2, blocking collectives: none -> 40.7 us  [the longest x1 24.4 us: across(): return lax.all_to_all(value, PLANE, split_axis=0, concat_axis=0, tiled=True)]
    all_to_all x1 -> x0, starting transfers between devices: 14.6 us -> none  [local(): lax.all_to_all(partial_squares(grad).reshape(DEVICES, 1, 128), ALL_AXES,...]
    all_to_all x1 -> x0, waiting for transfers between devices: 12.3 us -> none  [local(): lax.all_to_all(partial_squares(grad).reshape(DEVICES, 1, 128), ALL_AXES,...]
    all_to_all x6 -> x5, starting transfers between devices: 36.4 us -> 31.7 us  [across(): return lax.all_to_all(value, PLANE, split_axis=0, concat_axis=0, tiled=True)]
    ppermute x6, waiting for transfers between devices: 51.8 us -> 56.3 us  [shifted(): lax.ppermute(value, DEPTH, [(k, (k + planes) % count) for k in range(coun...]
    all_to_all x6 -> x5, waiting for transfers between devices: 18.1 us -> 13.8 us  [across(): return lax.all_to_all(value, PLANE, split_axis=0, concat_axis=0, tiled=True)]
    pallas_call x3 -> x2, Pallas kernels: 11.5 us -> 7.73 us  [packed(): pl.pallas_call(functools.partial(pack_kernel, count, group), grid_spec=pl...]
    pallas_call x1 -> x3, Pallas kernels: 2.28 us -> 4.59 us  [the longest x1 3.77 us: first_chunk(): pl.pallas_call(first_kernel, grid_spec=pltpu.PrefetchScalarGridSpec(num_s...]
  transfers between devices with their start and end apart: 13 -> 11, of which waited for: 10 -> 8; matrix products, arithmetic and copies ran while one was open for 0% -> 0% of each run, Pallas kernels for 12% -> 9%
where the time goes in v3:
time: 192 us; the launch traced here: 191 us
  waiting for transfers between devices  70.1 us (37%)
  starting transfers between devices  42.7 us (22%)
  blocking collectives  40.7 us (21%)
  Pallas kernels  36.4 us (19%)
    ppermute x6, waiting for transfers between devices, shifted(): lax.ppermute(value, DEPTH, [(k, (k + planes) % count) for k in range(coun...  56.3 us
    all_to_all x5, starting transfers between devices, across(): return lax.all_to_all(value, PLANE, split_axis=0, concat_axis=0, tiled=True)  31.7 us
    all_to_all x1, blocking collectives, across(): return lax.all_to_all(value, PLANE, split_axis=0, concat_axis=0, tiled=True)  24.4 us
    all_to_all x1, blocking collectives, local(): lax.all_to_all(partial, OTHERS, split_axis=0, concat_axis=0, tiled=True)  16.3 us
    all_to_all x5, waiting for transfers between devices, across(): return lax.all_to_all(value, PLANE, split_axis=0, concat_axis=0, tiled=True)  13.8 us
    ppermute x6, starting transfers between devices, shifted(): lax.ppermute(value, DEPTH, [(k, (k + planes) % count) for k in range(coun...  11 us
    pallas_call x2, Pallas kernels, packed(): pl.pallas_call(functools.partial(pack_kernel, count, group), grid_spec=pl...  7.73 us
    pallas_call x3, Pallas kernels, finished(): pl.pallas_call(functools.partial(finish_kernel, group), grid_spec=pltpu.P...  7.47 us
  transfers between devices with their start and end apart: 11, of which 8 were waited for; matrix products, arithmetic and copies ran while one was open for 0% of the time, Pallas kernels for 9%

profile of v3, /device:TPU:8, one launch (start us, length us, event | category | flops | bytes accessed | tf_op | source)
XLA Modules:
  0.0 190.8 jit_solution(16382324215044014393)
XLA Ops:
  0.6 3.8 %first.1 = bf16[16,72,512]{2,1,0:T(8,128)(2,1)} custom-call(s32[1]{0:T(128)} %bitcast.place_ref, s32[64]{0:T(128)} %bitcast.20, bf16[64,32,512]{2,1,0:T(8,128)(2,1)} %bitcast.10, bf16[64,32,512]{2,1,0:T(8,128)(2,1)} %bitcast.14), custom_call_target="tpu_custom_call" | custom-call | flops 2097152 | bytes 5242880 | tf_op jit(solution)/shard_map/first/pallas_call | solution.py:90
  4.4 24.4 %all_to_all.35.in_ref = bf16[16,72,512]{2,1,0:T(8,128)(2,1)S(1)} all-to-all(bf16[16,72,512]{2,1,0:T(8,128)(2,1)} %first.1), channel_id=1, replica_groups=mesh['rows_0'=4,'rows_1'=4,'rows_2'=4,'experts_0'=2,'experts_1'=2] {'row..., dimensions={0} | all-to-all | bytes 2359296 | tf_op jit(solution)/shard_map/all_to_all | solution.py:456
  28.8 0.1 plane.1
  28.9 16.3 %all_to_all.36.part_ref = f32[16,8,128]{2,1,0:T(8,128)} all-to-all(f32[16,8,128]{2,1,0:T(8,128)S(1)} %plane.1), channel_id=1, replica_groups=mesh['rows_0'=4,'rows_1'=4,'rows_2'=4,'experts_0'=2,'experts_1'=2] {'row..., dimensions={0} | all-to-all | bytes 131072 | tf_op jit(solution)/shard_map/all_to_all | solution.py:469
  45.1 4.0 %pack.3 = bf16[16,64,512]{2,1,0:T(8,128)(2,1)} custom-call(s32[1]{0:T(128)} %bitcast.place_ref, s32[64]{0:T(128)} %bitcast.21, f32[16,8,128]{2,1,0:T(8,128)} %all_to_all.36.part_ref, bf16[64,32,512]{2,1,0:T(8,128)(2,1)} %bitcast.11, bf16[64,32,512]{2,1,0:T(8,128)(2,1)} %bitcast.15), custom_call_target="tpu_custom_call" | custom-call | flops 3145728 | bytes 3145728 | tf_op jit(solution)/shard_map/pack/pallas_call | solution.py:173
  49.1 5.1 %all-to-all-start.3 = ((bf16[16,64,512]{2,1,0:T(8,128)(2,1)}), bf16[16,64,512]{2,1,0:T(8,128)(2,1)S(1)}, u32[]{:S(2)}, u32[]{:S(2)}) async-start(bf16[16,64,512]{2,1,0:T(8,128)(2,1)} %pack.3), calls=%async_computation.3 | async-start | bytes 2097152 | tf_op jit(solution)/shard_map/all_to_all | solution.py:456
  54.2 0.0 copy-start.3
  54.2 3.8 %pack.2 = bf16[16,32,512]{2,1,0:T(8,128)(2,1)} custom-call(s32[1]{0:T(128)} %bitcast.place_ref, s32[64]{0:T(128)} %bitcast.22, f32[16,8,128]{2,1,0:T(8,128)} %all_to_all.36.part_ref, bf16[64,32,512]{2,1,0:T(8,128)(2,1)} %bitcast.12, bf16[64,32,512]{2,1,0:T(8,128)(2,1)} %bitcast.16), custom_call_target="tpu_custom_call" | custom-call | flops 1572864 | bytes 1572864 | tf_op jit(solution)/shard_map/pack/pallas_call | solution.py:173
  58.0 13.5 %all-to-all-done.3.in_ref = bf16[16,64,512]{2,1,0:T(8,128)(2,1)S(1)} async-done(((bf16[16,64,512]{2,1,0:T(8,128)(2,1)}), bf16[16,64,512]{2,1,0:T(8,128)(2,1)S(1)}, u32[]{:S(2)}, u32[]{:S(2)}) %all-to-all-start.3) | async-done | bytes 1048608 | tf_op jit(solution)/shard_map/all_to_all | solution.py:456
  71.5 4.9 %all-to-all-start.2 = ((bf16[16,32,512]{2,1,0:T(8,128)(2,1)}), bf16[16,32,512]{2,1,0:T(8,128)(2,1)S(1)}, u32[]{:S(2)}, u32[]{:S(2)}) async-start(bf16[16,32,512]{2,1,0:T(8,128)(2,1)} %pack.2), calls=%async_computation.2 | async-start | bytes 1048576 | tf_op jit(solution)/shard_map/all_to_all | solution.py:456
  76.4 0.0 copy-done.3
  76.4 0.8 early.1
  77.1 0.0 copy-start.4
  77.1 0.9 collective-permute-start
  78.1 0.7 gram.1
  78.8 2.1 %collective-permute-start.1 = (bf16[1280,128]{1,0:T(8,128)(2,1)S(1)}, bf16[1280,128]{1,0:T(8,128)(2,1)S(1)}, u32[]{:S(2)}, u32[]{:S(2)}) collective-permute-start(bf16[1280,128]{1,0:T(8,128)(2,1)S(1)} %get-tuple-element.8), channel_id=1, source_target_pairs={{0,16},{16,32},{32,48},{48,0},{1,17},{17,33},{33,49},{49,1},{2,18}... | collective-permute-start | bytes 983048 | tf_op jit(solution)/shard_map/ppermute | solution.py:452
  81.0 2.1 %collective-permute-start.2 = (bf16[1280,128]{1,0:T(8,128)(2,1)S(1)}, bf16[1280,128]{1,0:T(8,128)(2,1)S(1)}, u32[]{:S(2)}, u32[]{:S(2)}) collective-permute-start(bf16[1280,128]{1,0:T(8,128)(2,1)S(1)} %get-tuple-element.9), channel_id=1, source_target_pairs={{0,48},{16,0},{32,16},{48,32},{1,49},{17,1},{33,17},{49,33},{2,50}... | collective-permute-start | bytes 983048 | tf_op jit(solution)/shard_map/ppermute | solution.py:452
  83.0 0.0 copy-done.4
  83.0 15.4 %collective-permute-done.a_ref = bf16[1280,128]{1,0:T(8,128)(2,1)S(1)} collective-permute-done((bf16[1280,128]{1,0:T(8,128)(2,1)S(1)}, bf16[1280,128]{1,0:T(8,128)(2,1)S(1)}, u32[]{:S(2)}, u32[]{:S(2)}) %collective-permute-start) | collective-permute-done | bytes 327712 | tf_op jit(solution)/shard_map/ppermute | solution.py:452
  98.5 0.0 all-to-all-done.2.own_ref.in_ref
  98.5 3.1 %collective-permute-done.1.b_ref = bf16[1280,128]{1,0:T(8,128)(2,1)S(1)} collective-permute-done((bf16[1280,128]{1,0:T(8,128)(2,1)S(1)}, bf16[1280,128]{1,0:T(8,128)(2,1)S(1)}, u32[]{:S(2)}, u32[]{:S(2)}) %collective-permute-start.1) | collective-permute-done | bytes 327712 | tf_op jit(solution)/shard_map/ppermute | solution.py:452
  101.6 6.6 %collective-permute-done.2.c_ref = bf16[1280,128]{1,0:T(8,128)(2,1)S(1)} collective-permute-done((bf16[1280,128]{1,0:T(8,128)(2,1)S(1)}, bf16[1280,128]{1,0:T(8,128)(2,1)S(1)}, u32[]{:S(2)}, u32[]{:S(2)}) %collective-permute-start.2) | collective-permute-done | bytes 327712 | tf_op jit(solution)/shard_map/ppermute | solution.py:452
  108.2 6.4 %factor.1.refs_0_ = bf16[1280,128]{1,0:T(8,128)(2,1)S(1)} custom-call(bf16[16,32,512]{2,1,0:T(8,128)(2,1)S(1)} %all-to-all-done.2.own_ref.in_ref, bf16[1280,128]{1,0:T(8,128)(2,1)S(1)} %collective-permute-done.a_ref, bf16[1280,128]{1,0:T(8,128)(2,1)S(1)} %collective-permute-done.1.b_ref, bf16[1280,128]{1,0:T(8,128)(2,1)S(1)} %collective-permute-done.2.c_ref), custom_call_target="tpu_custom_call" | custom-call | flops 5000000000 | bytes 1048576 | tf_op jit(solution)/shard_map/factor/pallas_call | solution.py:357
  114.6 1.3 apply.5
  115.9 7.2 %all-to-all-start.6 = ((bf16[16,32,512]{2,1,0:T(8,128)(2,1)}), bf16[16,32,512]{2,1,0:T(8,128)(2,1)S(1)}, u32[]{:S(2)}, u32[]{:S(2)}) async-start(bf16[16,32,512]{2,1,0:T(8,128)(2,1)} %apply.5), calls=%async_computation.6 | async-start | bytes 1048576 | tf_op jit(solution)/shard_map/all_to_all | solution.py:456
  123.1 0.0 copy-start.5
  123.2 2.9 %collective-permute-start.5 = (bf16[1280,128]{1,0:T(8,128)(2,1)S(1)}, bf16[1280,128]{1,0:T(8,128)(2,1)S(1)}, u32[]{:S(2)}, u32[]{:S(2)}) collective-permute-start(bf16[1280,128]{1,0:T(8,128)(2,1)S(1)} %factor.1.refs_0_), channel_id=1, source_target_pairs={{0,16},{16,32},{32,48},{48,0},{1,17},{17,33},{33,49},{49,1},{2,18}... | collective-permute-start | bytes 983048 | tf_op jit(solution)/shard_map/ppermute | solution.py:452
  126.0 1.4 collective-permute-start.4
  127.4 14.1 %collective-permute-done.5.refs_1_ = bf16[1280,128]{1,0:T(8,128)(2,1)S(1)} collective-permute-done((bf16[1280,128]{1,0:T(8,128)(2,1)S(1)}, bf16[1280,128]{1,0:T(8,128)(2,1)S(1)}, u32[]{:S(2)}, u32[]{:S(2)}) %collective-permute-start.5) | collective-permute-done | bytes 327712 | tf_op jit(solution)/shard_map/ppermute | solution.py:452
  141.5 0.4 collective-permute-done.4.refs_0_
  141.9 1.8 apply.4
  143.7 0.0 all-to-all-done.6.ortho_ref
  143.7 0.0 copy-start.1
  143.8 7.2 %all-to-all-start.5 = ((bf16[16,64,512]{2,1,0:T(8,128)(2,1)}), bf16[16,64,512]{2,1,0:T(8,128)(2,1)S(1)}, u32[]{:S(2)}, u32[]{:S(2)}) async-start(bf16[16,64,512]{2,1,0:T(8,128)(2,1)} %apply.4), calls=%async_computation.5 | async-start | bytes 2097152 | tf_op jit(solution)/shard_map/all_to_all | solution.py:456
  151.0 1.6 collective-permute-start.3
  152.6 16.6 %collective-permute-done.3.refs_0_ = bf16[1280,128]{1,0:T(8,128)(2,1)S(1)} collective-permute-done((bf16[1280,128]{1,0:T(8,128)(2,1)S(1)}, bf16[1280,128]{1,0:T(8,128)(2,1)S(1)}, u32[]{:S(2)}, u32[]{:S(2)}) %collective-permute-start.3) | collective-permute-done | bytes 327712 | tf_op jit(solution)/shard_map/ppermute | solution.py:452
  169.2 0.0 copy-done.5
  169.2 1.3 apply.3
  170.6 0.0 all-to-all-done.5.ortho_ref
  170.6 0.0 copy-done.1
  170.6 7.2 %all-to-all-start.4 = ((bf16[16,32,512]{2,1,0:T(8,128)(2,1)}), bf16[16,32,512]{2,1,0:T(8,128)(2,1)}, u32[]{:S(2)}, u32[]{:S(2)}) async-start(bf16[16,32,512]{2,1,0:T(8,128)(2,1)} %apply.3), calls=%async_computation.4 | async-start | bytes 1048576 | tf_op jit(solution)/shard_map/all_to_all | solution.py:456
  177.8 0.0 copy-start
  177.8 0.0 copy-start.2
  177.8 5.0 %state.1 = bf16[64,32,512]{2,1,0:T(8,128)(2,1)} custom-call(s32[64]{0:T(128)} %bitcast.23, f32[16,8,128]{2,1,0:T(8,128)} %all_to_all.36.part_ref, bf16[64,32,512]{2,1,0:T(8,128)(2,1)} %bitcast.13, bf16[64,32,512]{2,1,0:T(8,128)(2,1)} %bitcast.17), custom_call_target="tpu_custom_call" | custom-call | flops 6291456 | bytes 6291456 | tf_op jit(solution)/shard_map/state/pallas_call | solution.py:232
  182.8 0.0 copy-done
  182.8 0.0 copy-done.2
  182.8 1.9 finish.3.refs_0_
  184.7 2.7 %finish.4.refs_0_ = bf16[64,32,512]{2,1,0:T(8,128)(2,1)} custom-call(s32[1]{0:T(128)} %bitcast.place_ref, bf16[16,64,512]{2,1,0:T(8,128)(2,1)S(1)} %all-to-all-done.5.ortho_ref, bf16[64,32,512]{2,1,0:T(8,128)(2,1)S(1)} %bitcast.8, bf16[64,32,512]{2,1,0:T(8,128)(2,1)} %finish.3.refs_0_), custom_call_target="tpu_custom_call", output_to_operand_aliasing={{}: (3, {})} | custom-call | flops 1572864 | bytes 3145728 | tf_op jit(solution)/shard_map/finish/pallas_call | solution.py:429
  187.5 0.3 all-to-all-done.4.ortho_ref
  187.8 2.9 %finish.5 = bf16[64,32,512]{2,1,0:T(8,128)(2,1)} custom-call(s32[1]{0:T(128)} %bitcast.place_ref, bf16[16,32,512]{2,1,0:T(8,128)(2,1)} %all-to-all-done.4.ortho_ref, bf16[64,32,512]{2,1,0:T(8,128)(2,1)S(1)} %bitcast.9, bf16[64,32,512]{2,1,0:T(8,128)(2,1)} %finish.4.refs_0_), custom_call_target="tpu_custom_call", output_to_operand_aliasing={{}: (3, {})} | custom-call | flops 786432 | bytes 1572864 | tf_op jit(solution)/shard_map/finish/pallas_call | solution.py:429
Async XLA Ops:
  49.1 22.4 %all-to-all-start.3 = ((bf16[16,64,512]{2,1,0:T(8,128)(2,1)}), bf16[16,64,512]{2,1,0:T(8,128)(2,1)S(1)}, u32[]{:S(2)}, u32[]{:S(2)}) async-start(bf16[16,64,512]{2,1,0:T(8,128)(2,1)} %pack.3), calls=%async_computation.3 | async-start | bytes 2097152 | tf_op jit(solution)/shard_map/all_to_all | solution.py:456
  54.2 22.1 %copy-start.3 = (f32[16,8,128]{2,1,0:T(8,128)S(1)}, f32[16,8,128]{2,1,0:T(8,128)}, u32[]{:S(2)}) copy-start(f32[16,8,128]{2,1,0:T(8,128)} %all_to_all.36.part_ref) | copy-start | bytes 196612
  71.5 27.0 %all-to-all-start.2 = ((bf16[16,32,512]{2,1,0:T(8,128)(2,1)}), bf16[16,32,512]{2,1,0:T(8,128)(2,1)S(1)}, u32[]{:S(2)}, u32[]{:S(2)}) async-start(bf16[16,32,512]{2,1,0:T(8,128)(2,1)} %pack.2), calls=%async_computation.2 | async-start | bytes 1048576 | tf_op jit(solution)/shard_map/all_to_all | solution.py:456
  77.1 5.9 %copy-start.4 = (bf16[16,32,512]{2,1,0:T(8,128)(2,1)}, bf16[16,32,512]{2,1,0:T(8,128)(2,1)S(1)}, u32[]{:S(2)}) copy-start(bf16[16,32,512]{2,1,0:T(8,128)(2,1)S(1)} %get-tuple-element.6.in_ref) | copy-start | bytes 1572868
  77.1 21.3 %collective-permute-start = (bf16[1280,128]{1,0:T(8,128)(2,1)S(1)}, bf16[1280,128]{1,0:T(8,128)(2,1)S(1)}, u32[]{:S(2)}, u32[]{:S(2)}) collective-permute-start(bf16[1280,128]{1,0:T(8,128)(2,1)S(1)} %get-tuple-element.7), channel_id=1, source_target_pairs={{0,32},{16,48},{32,0},{48,16},{1,33},{17,49},{33,1},{49,17},{2,34}... | collective-permute-start | bytes 983048 | tf_op jit(solution)/shard_map/ppermute | solution.py:452
  78.8 22.8 %collective-permute-start.1 = (bf16[1280,128]{1,0:T(8,128)(2,1)S(1)}, bf16[1280,128]{1,0:T(8,128)(2,1)S(1)}, u32[]{:S(2)}, u32[]{:S(2)}) collective-permute-start(bf16[1280,128]{1,0:T(8,128)(2,1)S(1)} %get-tuple-element.8), channel_id=1, source_target_pairs={{0,16},{16,32},{32,48},{48,0},{1,17},{17,33},{33,49},{49,1},{2,18}... | collective-permute-start | bytes 983048 | tf_op jit(solution)/shard_map/ppermute | solution.py:452
  81.0 27.2 %collective-permute-start.2 = (bf16[1280,128]{1,0:T(8,128)(2,1)S(1)}, bf16[1280,128]{1,0:T(8,128)(2,1)S(1)}, u32[]{:S(2)}, u32[]{:S(2)}) collective-permute-start(bf16[1280,128]{1,0:T(8,128)(2,1)S(1)} %get-tuple-element.9), channel_id=1, source_target_pairs={{0,48},{16,0},{32,16},{48,32},{1,49},{17,1},{33,17},{49,33},{2,50}... | collective-permute-start | bytes 983048 | tf_op jit(solution)/shard_map/ppermute | solution.py:452
  115.9 27.8 %all-to-all-start.6 = ((bf16[16,32,512]{2,1,0:T(8,128)(2,1)}), bf16[16,32,512]{2,1,0:T(8,128)(2,1)S(1)}, u32[]{:S(2)}, u32[]{:S(2)}) async-start(bf16[16,32,512]{2,1,0:T(8,128)(2,1)} %apply.5), calls=%async_computation.6 | async-start | bytes 1048576 | tf_op jit(solution)/shard_map/all_to_all | solution.py:456
  123.1 46.1 %copy-start.5 = (bf16[16,32,512]{2,1,0:T(8,128)(2,1)S(1)}, bf16[16,32,512]{2,1,0:T(8,128)(2,1)}, u32[]{:S(2)}) copy-start(bf16[16,32,512]{2,1,0:T(8,128)(2,1)} %copy-done.4) | copy-start | bytes 1572868
  123.2 18.3 %collective-permute-start.5 = (bf16[1280,128]{1,0:T(8,128)(2,1)S(1)}, bf16[1280,128]{1,0:T(8,128)(2,1)S(1)}, u32[]{:S(2)}, u32[]{:S(2)}) collective-permute-start(bf16[1280,128]{1,0:T(8,128)(2,1)S(1)} %factor.1.refs_0_), channel_id=1, source_target_pairs={{0,16},{16,32},{32,48},{48,0},{1,17},{17,33},{33,49},{49,1},{2,18}... | collective-permute-start | bytes 983048 | tf_op jit(solution)/shard_map/ppermute | solution.py:452
  126.0 15.9 %collective-permute-start.4 = (bf16[1280,128]{1,0:T(8,128)(2,1)S(1)}, bf16[1280,128]{1,0:T(8,128)(2,1)S(1)}, u32[]{:S(2)}, u32[]{:S(2)}) collective-permute-start(bf16[1280,128]{1,0:T(8,128)(2,1)S(1)} %factor.1.refs_0_), channel_id=1, source_target_pairs={{0,48},{16,0},{32,16},{48,32},{1,49},{17,1},{33,17},{49,33},{2,50}... | collective-permute-start | bytes 983048 | tf_op jit(solution)/shard_map/ppermute | solution.py:452
  143.7 26.8 %copy-start.1 = (bf16[16,32,512]{2,1,0:T(8,128)(2,1)}, bf16[16,32,512]{2,1,0:T(8,128)(2,1)S(1)}, u32[]{:S(2)}) copy-start(bf16[16,32,512]{2,1,0:T(8,128)(2,1)S(1)} %all-to-all-done.6.ortho_ref) | copy-start | bytes 1572868
  143.8 26.8 %all-to-all-start.5 = ((bf16[16,64,512]{2,1,0:T(8,128)(2,1)}), bf16[16,64,512]{2,1,0:T(8,128)(2,1)S(1)}, u32[]{:S(2)}, u32[]{:S(2)}) async-start(bf16[16,64,512]{2,1,0:T(8,128)(2,1)} %apply.4), calls=%async_computation.5 | async-start | bytes 2097152 | tf_op jit(solution)/shard_map/all_to_all | solution.py:456
  151.0 18.2 %collective-permute-start.3 = (bf16[1280,128]{1,0:T(8,128)(2,1)S(1)}, bf16[1280,128]{1,0:T(8,128)(2,1)S(1)}, u32[]{:S(2)}, u32[]{:S(2)}) collective-permute-start(bf16[1280,128]{1,0:T(8,128)(2,1)S(1)} %factor.1.refs_0_), channel_id=1, source_target_pairs={{0,32},{16,48},{32,0},{48,16},{1,33},{17,49},{33,1},{49,17},{2,34}... | collective-permute-start | bytes 983048 | tf_op jit(solution)/shard_map/ppermute | solution.py:452
  170.6 17.2 %all-to-all-start.4 = ((bf16[16,32,512]{2,1,0:T(8,128)(2,1)}), bf16[16,32,512]{2,1,0:T(8,128)(2,1)}, u32[]{:S(2)}, u32[]{:S(2)}) async-start(bf16[16,32,512]{2,1,0:T(8,128)(2,1)} %apply.3), calls=%async_computation.4 | async-start | bytes 1048576 | tf_op jit(solution)/shard_map/all_to_all | solution.py:456
  177.8 5.0 %copy-start = (bf16[1,64,32,512]{3,2,1,0:T(8,128)(2,1)S(1)}, bf16[1,64,32,512]{3,2,1,0:T(8,128)(2,1)}, u32[]{:S(2)}) copy-start(bf16[1,64,32,512]{3,2,1,0:T(8,128)(2,1)} %param.4) | copy-start | bytes 6291460
  177.8 5.0 %copy-start.2 = (bf16[16,32,512]{2,1,0:T(8,128)(2,1)S(1)}, bf16[16,32,512]{2,1,0:T(8,128)(2,1)}, u32[]{:S(2)}) copy-start(bf16[16,32,512]{2,1,0:T(8,128)(2,1)} %copy-done.1) | copy-start | bytes 1572868

commit v4 on v1

--- a/solution.py
+++ b/solution.py
@@ -26,42 +26,62 @@
 norm_epsilon = 1e-07
 clip_epsilon = 1e-06
 CHUNK = 8
+LARGE_GRANT = 56 << 20
+SMALL_GRANT = 16 << 20
+STAGE_GRANT = 48 << 20
+UPDATE_GRANT = 16 << 20
 
 bf16 = jnp.bfloat16
 f32 = jnp.float32
 
 
-def squares_kernel(grad_ref, out_ref, acc_ref):
-    step = pl.program_id(0)
-
-    @pl.when(step == 0)
-    def _():
-        acc_ref[...] = jnp.zeros_like(acc_ref)
-
-    wide = grad_ref[...].astype(f32)
-    acc_ref[...] += jnp.sum(wide * wide, axis=0)
-
-    @pl.when(step == pl.num_programs(0) - 1)
-    def _():
-        folded = acc_ref[:, 0:128]
-        for k in range(1, COLS // 128):
-            folded = folded + acc_ref[:, 128 * k : 128 * (k + 1)]
-        out_ref[...] = jnp.broadcast_to(jnp.sum(folded, axis=0, keepdims=True), out_ref.shape)
-
-
-def partial_squares(grad):
-    slots, rows, cols = grad.shape
-    return pl.pallas_call(
-        squares_kernel,
-        grid=(slots // CHUNK,),
-        in_specs=[pl.BlockSpec((CHUNK, rows, cols), lambda i: (i, 0, 0))],
-        out_specs=pl.BlockSpec((DEVICES, 128), lambda i: (0, 0)),
-        out_shape=jax.ShapeDtypeStruct((DEVICES, 128), f32),
-        scratch_shapes=[pltpu.VMEM((rows, cols), f32)],
-        compiler_params=pltpu.CompilerParams(vmem_limit_bytes=56 << 20),
-        cost_estimate=pl.CostEstimate(flops=2 * grad.size, bytes_accessed=2 * grad.size, transcendentals=0),
-        name="squares",
-    )(grad)
+def prepare_kernel(slots_ref, grad_hbm, mom_hbm, part_ref, grad_ref, mom_ref, acc_ref, grad_sems, sem):
+    chunks = grad_ref.shape[0] // CHUNK
+    for chunk in range(chunks):
+        rows = pl.ds(chunk * CHUNK, CHUNK)
+        pltpu.make_async_copy(grad_hbm.at[rows], grad_ref.at[rows], grad_sems.at[chunk]).start()
+    for k in range(mom_ref.shape[0]):
+        pltpu.make_async_copy(mom_hbm.at[slots_ref[k]], mom_ref.at[k], sem).start()
+    acc_ref[...] = jnp.zeros_like(acc_ref)
+
+    @pl.loop(0, chunks)
+    def _(chunk):
+        rows = pl.ds(chunk * CHUNK, CHUNK)
+        pltpu.make_async_copy(grad_hbm.at[rows], grad_ref.at[rows], grad_sems.at[chunk]).wait()
+        wide = grad_ref[rows].astype(f32)
+        acc_ref[...] += jnp.sum(wide * wide, axis=0)
+
+    folded = acc_ref[:, 0:128]
+    for k in range(1, COLS // 128):
+        folded = folded + acc_ref[:, 128 * k : 128 * (k + 1)]
+    part_ref[...] = jnp.broadcast_to(jnp.sum(folded, axis=0, keepdims=True), part_ref.shape)
+    pltpu.make_async_copy(mom_hbm, mom_ref, sem).wait()
+
+
+def prepared(slots, grad, mom):
+    whole = pl.BlockSpec(grad.shape, lambda i, s: (0, 0, 0))
+    return pl.pallas_call(
+        prepare_kernel,
+        grid_spec=pltpu.PrefetchScalarGridSpec(
+            num_scalar_prefetch=1,
+            grid=(1,),
+            in_specs=[pl.BlockSpec(memory_space=pl.ANY)] * 2,
+            out_specs=[pl.BlockSpec((DEVICES, 128), lambda i, s: (0, 0)), whole, whole],
+            scratch_shapes=[
+                pltpu.VMEM(grad.shape[1:], f32),
+                pltpu.SemaphoreType.DMA((grad.shape[0] // CHUNK,)),
+                pltpu.SemaphoreType.DMA(()),
+            ],
+        ),
+        out_shape=[
+            jax.ShapeDtypeStruct((DEVICES, 128), f32),
+            jax.ShapeDtypeStruct(grad.shape, bf16),
+            jax.ShapeDtypeStruct(grad.shape, bf16),
+        ],
+        compiler_params=pltpu.CompilerParams(vmem_limit_bytes=STAGE_GRANT),
+        cost_estimate=pl.CostEstimate(flops=2 * grad.size, bytes_accessed=8 * grad.size, transcendentals=0),
+        name="prepare",
+    )(slots, grad, mom)
 
 
 def clip_from(partials, count):
@@ -87,24 +107,30 @@
     pltpu.make_async_copy(mom_hbm.at[rows], mom_buf.at[rows], sems.at[1, chunk]).wait()
 
 
-def update_kernel(count, slots_ref, part_ref, grad_hbm, mom_hbm, out_hbm, grad_buf, mom_buf, sems, out_sem):
-    chunks = grad_buf.shape[0] // CHUNK
-    for chunk in range(chunks):
-        fetch(chunk, slots_ref, grad_hbm, mom_hbm, grad_buf, mom_buf, sems)
+def update_kernel(count, part_ref, grad_ref, mom_ref, out_hbm, out_buf, sem):
     clip = clip_from(part_ref[...], count)
 
-    @pl.loop(0, chunks)
-    def _(chunk):
-        await_fetch(chunk, grad_hbm, mom_hbm, grad_buf, mom_buf, sems)
-        rows = pl.ds(chunk * CHUNK, CHUNK)
-        scaled = clip * grad_buf[rows].astype(f32)
-        state = beta_decay * mom_buf[rows].astype(f32) + scaled
-        mom_buf[rows] = (scaled + beta_decay * state).astype(bf16)
-        pltpu.make_async_copy(mom_buf.at[rows], out_hbm.at[rows], out_sem.at[chunk]).start()
-
-    for chunk in range(chunks):
-        rows = pl.ds(chunk * CHUNK, CHUNK)
-        pltpu.make_async_copy(mom_buf.at[rows], out_hbm.at[rows], out_sem.at[chunk]).wait()
+    @pl.loop(0, grad_ref.shape[0] // CHUNK)
+    def _(chunk):
+        rows = pl.ds(chunk * CHUNK, CHUNK)
+        scaled = clip * grad_ref[rows].astype(f32)
+        state = beta_decay * mom_ref[rows].astype(f32) + scaled
+        out_buf[rows] = (scaled + beta_decay * state).astype(bf16)
+        pltpu.make_async_copy(out_buf.at[rows], out_hbm.at[rows], sem).start()
+
+    pltpu.make_async_copy(out_buf, out_hbm, sem).wait()
+
+
+def updated(count, partials, grad, mom):
+    return pl.pallas_call(
+        functools.partial(update_kernel, count),
+        out_specs=pl.BlockSpec(memory_space=pl.ANY),
+        out_shape=jax.ShapeDtypeStruct(grad.shape, bf16),
+        scratch_shapes=[pltpu.VMEM(grad.shape, bf16), pltpu.SemaphoreType.DMA(())],
+        compiler_params=pltpu.CompilerParams(vmem_limit_bytes=UPDATE_GRANT),
+        cost_estimate=pl.CostEstimate(flops=6 * grad.size, bytes_accessed=6 * grad.size, transcendentals=0),
+        name="update",
+    )(partials, grad, mom)
 
 
 def state_kernel(count, slots_ref, part_ref, grad_hbm, mom_hbm, out_hbm, grad_buf, mom_buf, sems, out_sem):
@@ -151,7 +177,7 @@
             ],
         ),
         out_shape=jax.ShapeDtypeStruct(grad.shape, bf16),
-        compiler_params=pltpu.CompilerParams(vmem_limit_bytes=56 << 20),
+        compiler_params=pltpu.CompilerParams(vmem_limit_bytes=LARGE_GRANT),
         cost_estimate=pl.CostEstimate(flops=6 * grad.size, bytes_accessed=6 * grad.size, transcendentals=0),
         name=name,
     )(slots, partials, grad, mom)
@@ -212,25 +238,47 @@
         name="orthogonal",
     )(tall)
 
+def finish_kernel(ortho_ref, weight_ref, out_hbm, out_buf, sem):
+    scale = learn_rate * 0.2 * math.sqrt(max(ROWS, COLS))
+
+    @pl.loop(0, ortho_ref.shape[0] // CHUNK)
+    def _(chunk):
+        rows = pl.ds(chunk * CHUNK, CHUNK)
+        kept = weight_ref[rows].astype(f32) * (1.0 - learn_rate * weight_decay)
+        out_buf[rows] = (kept - scale * ortho_ref[rows].astype(f32)).astype(bf16)
+        pltpu.make_async_copy(out_buf.at[rows], out_hbm.at[rows], sem).start()
+
+    pltpu.make_async_copy(out_buf, out_hbm, sem).wait()
+
+
+def finished(ortho, weight):
+    return pl.pallas_call(
+        finish_kernel,
+        out_specs=pl.BlockSpec(memory_space=pl.ANY),
+        out_shape=jax.ShapeDtypeStruct(weight.shape, bf16),
+        scratch_shapes=[pltpu.VMEM(weight.shape, bf16), pltpu.SemaphoreType.DMA(())],
+        compiler_params=pltpu.CompilerParams(vmem_limit_bytes=SMALL_GRANT),
+        cost_estimate=pl.CostEstimate(flops=3 * ortho.size, bytes_accessed=6 * ortho.size, transcendentals=0),
+        name="finish",
+    )(ortho, weight)
+
+
 def local(weight, momentum, gradient, assign):
     grad = gradient[0]
     mom = momentum[0]
     slots = assign[0]
     count = grad.size * lax.axis_size(ALL_AXES)
+    partials, near_grad, near_mom = prepared(slots, grad, mom)
     shared = lax.all_to_all(
-        partial_squares(grad).reshape(DEVICES, 1, 128), ALL_AXES, split_axis=0, concat_axis=0, tiled=True
+        partials.reshape(DEVICES, 1, 128), ALL_AXES, split_axis=0, concat_axis=0, tiled=True
     ).reshape(DEVICES, 128)
-    update = momentum_call(update_kernel, "update", count, slots, shared, grad, mom)
+    update = updated(count, shared, near_grad, near_mom)
     received = lax.all_to_all(update, ROWS_AXES, split_axis=0, concat_axis=0, tiled=True)
     state = momentum_call(state_kernel, "state", count, slots, shared, grad, mom)
     received, state = lax.optimization_barrier((received, state))
     result = orthogonal(received.reshape(ROWS, COLS)).reshape(received.shape)
     ortho = lax.all_to_all(result, ROWS_AXES, split_axis=0, concat_axis=0, tiled=True)
-    shape_scale = 0.2 * math.sqrt(max(ROWS, COLS))
-    new_weight = weight[0].astype(f32) * (1.0 - learn_rate * weight_decay) - (
-        learn_rate * shape_scale
-    ) * ortho.astype(f32)
-    return (new_weight.astype(bf16)[None], state[None])
+    return (finished(ortho, weight[0])[None], state[None])
 
 
 def solution(mesh):

time: 163 us -> 159 us (0.975)
  the two profiles are of different devices: /device:TPU:8 before, /device:TPU:32 now
where the time goes in v4:
time: 159 us; the launch traced here: 158 us
  blocking collectives  82.2 us (52%)
  waiting for transfers between devices  49.1 us (31%)
  Pallas kernels  21 us (13%)
  starting transfers between devices  4.71 us (3%)
    all_to_all x1, blocking collectives, local(): lax.all_to_all(result, ROWS_AXES, split_axis=0, concat_axis=0, tiled=True)  55.2 us
    all_to_all x1, waiting for transfers between devices, local(): lax.all_to_all(update, ROWS_AXES, split_axis=0, concat_axis=0, tiled=True)  49.1 us
    all_to_all x1, blocking collectives, local(): lax.all_to_all(partials.reshape(DEVICES, 1, 128), ALL_AXES, split_axis=0,...  27 us
    pallas_call x1, Pallas kernels, orthogonal(): pl.pallas_call(orthogonal_kernel, out_shape=jax.ShapeDtypeStruct(tall.sha...  9.69 us
    pallas_call x1, Pallas kernels, momentum_call(): pl.pallas_call(functools.partial(kernel, count), grid_spec=pltpu.Prefetch...  4.88 us
    all_to_all x1, starting transfers between devices, local(): lax.all_to_all(update, ROWS_AXES, split_axis=0, concat_axis=0, tiled=True)  4.71 us
  transfers between devices with their start and end apart: 1, of which 1 were waited for; matrix products, arithmetic and copies ran while one was open for 0% of the time, Pallas kernels for 3%

profile of v4, /device:TPU:32, one launch (start us, length us, event | category | flops | bytes accessed | tf_op | source)
XLA Modules:
  0.0 158.3 jit_solution(1434505706622621135)
XLA Ops:
  0.6 0.0 copy-start.2
  0.6 0.6 copy-done.2
  1.3 2.9 %prepare.1 = (f32[256,128]{1,0:T(8,128)S(1)}, bf16[64,32,512]{2,1,0:T(8,128)(2,1)S(1)}, bf16[64,32,512]{2,1,0:T(8,128)(2,1)S(1)}) custom-call(s32[64]{0:T(128)S(1)} %bitcast.19, bf16[64,32,512]{2,1,0:T(8,128)(2,1)} %bitcast.20, bf16[64,32,512]{2,1,0:T(8,128)(2,1)} %bitcast.22), custom_call_target="tpu_custom_call" | custom-call | flops 2097152 | bytes 8388608 | tf_op jit(solution)/shard_map/prepare/pallas_call | solution.py:63
  4.2 27.0 %all_to_all.15 = f32[256,1,128]{2,1,0:T(1,128)S(1)} all-to-all(f32[256,1,128]{2,1,0:T(1,128)S(1)} %bitcast.17), channel_id=1, replica_groups=mesh['rows_0'=4,'rows_1'=4,'rows_2'=4,'experts_0'=2,'experts_1'=2] {'row..., dimensions={0} | all-to-all | bytes 262144 | tf_op jit(solution)/shard_map/all_to_all | solution.py:272
  31.2 0.0 copy-start.1
  31.2 2.0 %update.1 = bf16[64,32,512]{2,1,0:T(8,128)(2,1)} custom-call(f32[256,128]{1,0:T(8,128)S(1)} %bitcast.15, bf16[64,32,512]{2,1,0:T(8,128)(2,1)S(1)} %get-tuple-element.8.grad_ref, bf16[64,32,512]{2,1,0:T(8,128)(2,1)S(1)} %get-tuple-element.9.mom_ref), custom_call_target="tpu_custom_call" | custom-call | flops 6291456 | bytes 6291456 | tf_op jit(solution)/shard_map/update/pallas_call | solution.py:125
  33.2 0.0 copy-done.1
  33.2 4.7 %all-to-all-start.1 = ((bf16[64,32,512]{2,1,0:T(8,128)(2,1)}), bf16[64,32,512]{2,1,0:T(8,128)(2,1)S(1)}, u32[]{:S(2)}, u32[]{:S(2)}) async-start(bf16[64,32,512]{2,1,0:T(8,128)(2,1)} %update.1), calls=%async_computation.1 | async-start | bytes 4194304 | tf_op jit(solution)/shard_map/all_to_all | solution.py:276
  37.9 4.9 %state.1 = bf16[64,32,512]{2,1,0:T(8,128)(2,1)} custom-call(s32[64]{0:T(128)} %bitcast.18, f32[256,128]{1,0:T(8,128)} %bitcast.16, bf16[64,32,512]{2,1,0:T(8,128)(2,1)} %bitcast.21, bf16[64,32,512]{2,1,0:T(8,128)(2,1)} %bitcast.23), custom_call_target="tpu_custom_call" | custom-call | flops 6291456 | bytes 6291456 | tf_op jit(solution)/shard_map/state/pallas_call | solution.py:161
  42.8 49.1 %all-to-all-done.1 = bf16[64,32,512]{2,1,0:T(8,128)(2,1)S(1)} async-done(((bf16[64,32,512]{2,1,0:T(8,128)(2,1)}), bf16[64,32,512]{2,1,0:T(8,128)(2,1)S(1)}, u32[]{:S(2)}, u32[]{:S(2)}) %all-to-all-start.1) | async-done | bytes 2097184 | tf_op jit(solution)/shard_map/all_to_all | solution.py:276
  91.9 9.7 %orthogonal.1 = bf16[2048,512]{1,0:T(8,128)(2,1)S(1)} custom-call(bf16[2048,512]{1,0:T(8,128)(2,1)S(1)} %bitcast.13), custom_call_target="tpu_custom_call" | custom-call | flops 8000000000 | bytes 4194304 | tf_op jit(solution)/shard_map/orthogonal/pallas_call | solution.py:231
  101.6 0.0 copy-start
  101.6 55.2 %all_to_all.16.ortho_ref = bf16[64,32,512]{2,1,0:T(8,128)(2,1)S(1)} all-to-all(bf16[64,32,512]{2,1,0:T(8,128)(2,1)S(1)} %bitcast.14), channel_id=1, replica_groups=mesh['rows_0'=4,'rows_1'=4,'rows_2'=4,'experts_0'=2,'experts_1'=2] {'row..., dimensions={0} | all-to-all | bytes 4194304 | tf_op jit(solution)/shard_map/all_to_all | solution.py:280
  156.8 0.0 copy-done
  156.8 1.5 finish.1
Async XLA Ops:
  0.6 0.7 copy-start.2
  31.2 2.0 %copy-start.1 = (f32[256,1,128]{2,1,0:T(1,128)}, f32[256,1,128]{2,1,0:T(1,128)S(1)}, u32[]{:S(2)}) copy-start(f32[256,1,128]{2,1,0:T(1,128)S(1)} %all_to_all.15) | copy-start | bytes 393220
  33.2 58.7 %all-to-all-start.1 = ((bf16[64,32,512]{2,1,0:T(8,128)(2,1)}), bf16[64,32,512]{2,1,0:T(8,128)(2,1)S(1)}, u32[]{:S(2)}, u32[]{:S(2)}) async-start(bf16[64,32,512]{2,1,0:T(8,128)(2,1)} %update.1), calls=%async_computation.1 | async-start | bytes 4194304 | tf_op jit(solution)/shard_map/all_to_all | solution.py:276
  101.6 55.3 %copy-start = (bf16[1,64,32,512]{3,2,1,0:T(8,128)(2,1)S(1)}, bf16[1,64,32,512]{3,2,1,0:T(8,128)(2,1)}, u32[]{:S(2)}) copy-start(bf16[1,64,32,512]{3,2,1,0:T(8,128)(2,1)} %param.4) | copy-start | bytes 6291460

commit v5 on v4

v5 whole, which is shorter than its diff:
```python
import functools
import math

import jax
import jax.numpy as jnp
from jax import lax
from jax.experimental import pallas as pl
from jax.experimental.pallas import tpu as pltpu
from jax.sharding import Mesh
from jax.sharding import PartitionSpec as P


ROWS = 2048
COLS = 512
ROWS_AXES = ("rows_0", "rows_1", "rows_2")
EXPERTS = ("experts_0", "experts_1")
ALL_AXES = ROWS_AXES + EXPERTS
DEVICES = 256
ITERS = 5
DEPTH = "rows_1"
CORE = "experts_1"
SPREAD = ("rows_0", "rows_1", "rows_2", "experts_1")
SIDE = 128
BLOCKS = tuple((i, j) for i in range(4) for j in range(i, 4))

linear_coef = 3.4445
cubic_coef = -4.775
quintic_coef = 2.0315
beta_decay = 0.95
learn_rate = 0.5
weight_decay = 0.1
norm_epsilon = 1e-07
clip_epsilon = 1e-06
CHUNK = 8
LARGE_GRANT = 56 << 20
SMALL_GRANT = 16 << 20
STAGE_GRANT = 48 << 20
UPDATE_GRANT = 16 << 20

bf16 = jnp.bfloat16
f32 = jnp.float32


def exchange_groups():
    return [
        [
            ((x * 4 + (2 * pair + member + core) % 4) * 4 + y) * 2 + core
            for x in range(4)
            for member in range(2)
            for y in range(4)
        ]
        for core in range(2)
        for pair in range(2)
    ]


def rows_of(peer, away, pair):
    return peer * 2 + lax.rem(pair + away, 2)


def prepare_kernel(pair_ref, slots_ref, grad_hbm, mom_hbm, part_ref, grad_ref, mom_ref, acc_ref, grad_sems, sem):
    chunks = grad_ref.shape[0] // CHUNK
    half = grad_ref.shape[0] // 2
    pair = pair_ref[0]
    for k in range(2 * half):
        matrix = rows_of(k % half, 1 - k // half, pair)
        pltpu.make_async_copy(grad_hbm.at[matrix], grad_ref.at[k], grad_sems.at[k // CHUNK]).start()
    for k in range(2 * half):
        matrix = rows_of(k % half, 1 - k // half, pair)
        pltpu.make_async_copy(mom_hbm.at[slots_ref[matrix]], mom_ref.at[k], sem).start()
    acc_ref[...] = jnp.zeros_like(acc_ref)

    @pl.loop(0, chunks)
    def _(chunk):
        rows = pl.ds(chunk * CHUNK, CHUNK)
        pltpu.make_async_copy(grad_hbm.at[rows], grad_ref.at[rows], grad_sems.at[chunk]).wait()
        wide = grad_ref[rows].astype(f32)
        acc_ref[...] += jnp.sum(wide * wide, axis=0)

    folded = acc_ref[:, 0:128]
    for k in range(1, COLS // 128):
        folded = folded + acc_ref[:, 128 * k : 128 * (k + 1)]
    part_ref[...] = jnp.broadcast_to(jnp.sum(folded, axis=0, keepdims=True), part_ref.shape)
    pltpu.make_async_copy(mom_hbm, mom_ref, sem).wait()


def prepared(pair, slots, grad, mom):
    whole = pl.BlockSpec(grad.shape, lambda i, p, s: (0, 0, 0))
    return pl.pallas_call(
        prepare_kernel,
        grid_spec=pltpu.PrefetchScalarGridSpec(
            num_scalar_prefetch=2,
            grid=(1,),
            in_specs=[pl.BlockSpec(memory_space=pl.ANY)] * 2,
            out_specs=[pl.BlockSpec((DEVICES, 128), lambda i, p, s: (0, 0)), whole, whole],
            scratch_shapes=[
                pltpu.VMEM(grad.shape[1:], f32),
                pltpu.SemaphoreType.DMA((grad.shape[0] // CHUNK,)),
                pltpu.SemaphoreType.DMA(()),
            ],
        ),
        out_shape=[
            jax.ShapeDtypeStruct((DEVICES, 128), f32),
            jax.ShapeDtypeStruct(grad.shape, bf16),
            jax.ShapeDtypeStruct(grad.shape, bf16),
        ],
        compiler_params=pltpu.CompilerParams(vmem_limit_bytes=STAGE_GRANT),
        cost_estimate=pl.CostEstimate(flops=2 * grad.size, bytes_accessed=8 * grad.size, transcendentals=0),
        name="prepare",
    )(pair, slots, grad, mom)


def clip_from(partials, count):
    total = jnp.sum(partials)
    limit = math.sqrt(float(count))
    return jnp.minimum(1.0, limit / (jnp.sqrt(total) + clip_epsilon))


def fetch(chunk, slots_ref, grad_hbm, mom_hbm, grad_buf, mom_buf, sems):
    base = chunk * CHUNK
    pltpu.make_async_copy(
        grad_hbm.at[pl.ds(base, CHUNK)], grad_buf.at[pl.ds(base, CHUNK)], sems.at[0, chunk]
    ).start()
    for k in range(CHUNK):
        pltpu.make_async_copy(
            mom_hbm.at[slots_ref[base + k]], mom_buf.at[base + k], sems.at[1, chunk]
        ).start()


def await_fetch(chunk, grad_hbm, mom_hbm, grad_buf, mom_buf, sems):
    rows = pl.ds(chunk * CHUNK, CHUNK)
    pltpu.make_async_copy(grad_hbm.at[rows], grad_buf.at[rows], sems.at[0, chunk]).wait()
    pltpu.make_async_copy(mom_hbm.at[rows], mom_buf.at[rows], sems.at[1, chunk]).wait()


def update_kernel(count, first, part_ref, grad_ref, mom_ref, out_hbm, out_buf, sem):
    clip = clip_from(part_ref[...], count)

    @pl.loop(0, out_buf.shape[0] // CHUNK)
    def _(chunk):
        rows = pl.ds(chunk * CHUNK, CHUNK)
        source = pl.ds(first + chunk * CHUNK, CHUNK)
        scaled = clip * grad_ref[source].astype(f32)
        state = beta_decay * mom_ref[source].astype(f32) + scaled
        out_buf[rows] = (scaled + beta_decay * state).astype(bf16)
        pltpu.make_async_copy(out_buf.at[rows], out_hbm.at[rows], sem).start()

    pltpu.make_async_copy(out_buf, out_hbm, sem).wait()


def updated(count, away, partials, grad, mom):
    half = grad.shape[0] // 2
    shape = (half,) + grad.shape[1:]
    return pl.pallas_call(
        functools.partial(update_kernel, count, half * (1 - away)),
        out_specs=pl.BlockSpec(memory_space=pl.ANY),
        out_shape=jax.ShapeDtypeStruct(shape, bf16),
        scratch_shapes=[pltpu.VMEM(shape, bf16), pltpu.SemaphoreType.DMA(())],
        compiler_params=pltpu.CompilerParams(vmem_limit_bytes=UPDATE_GRANT),
        cost_estimate=pl.CostEstimate(flops=3 * grad.size, bytes_accessed=3 * grad.size, transcendentals=0),
        name="update",
    )(partials, grad, mom)


def state_kernel(count, slots_ref, part_ref, grad_hbm, mom_hbm, out_hbm, grad_buf, mom_buf, sems, out_sem):
    chunks = grad_buf.shape[0] // CHUNK
    for chunk in range(chunks):
        fetch(chunk, slots_ref, grad_hbm, mom_hbm, grad_buf, mom_buf, sems)
    clip = clip_from(part_ref[...], count)

    @pl.loop(0, chunks)
    def _(chunk):
        await_fetch(chunk, grad_hbm, mom_hbm, grad_buf, mom_buf, sems)
        base = chunk * CHUNK
        rows = pl.ds(base, CHUNK)
        state = beta_decay * mom_buf[rows].astype(f32) + clip * grad_buf[rows].astype(f32)
        mom_buf[rows] = state.astype(bf16)
        for k in range(CHUNK):
            pltpu.make_async_copy(
                mom_buf.at[base + k], out_hbm.at[slots_ref[base + k]], out_sem.at[chunk]
            ).start()

    for chunk in range(chunks):
        rows = pl.ds(chunk * CHUNK, CHUNK)
        pltpu.make_async_copy(mom_buf.at[rows], out_hbm.at[rows], out_sem.at[chunk]).wait()


def momentum_call(kernel, count, slots, partials, grad, mom):
    chunks = grad.shape[0] // CHUNK
    return pl.pallas_call(
        functools.partial(kernel, count),
        grid_spec=pltpu.PrefetchScalarGridSpec(
            num_scalar_prefetch=1,
            grid=(1,),
            in_specs=[
                pl.BlockSpec(partials.shape, lambda i, s: (0, 0)),
                pl.BlockSpec(memory_space=pl.ANY),
                pl.BlockSpec(memory_space=pl.ANY),
            ],
            out_specs=pl.BlockSpec(memory_space=pl.ANY),
            scratch_shapes=[
                pltpu.VMEM(grad.shape, bf16),
                pltpu.VMEM(grad.shape, bf16),
                pltpu.SemaphoreType.DMA((2, chunks)),
                pltpu.SemaphoreType.DMA((chunks,)),
            ],
        ),
        out_shape=jax.ShapeDtypeStruct(grad.shape, bf16),
        compiler_params=pltpu.CompilerParams(vmem_limit_bytes=LARGE_GRANT),
        cost_estimate=pl.CostEstimate(flops=6 * grad.size, bytes_accessed=6 * grad.size, transcendentals=0),
    )(slots, partials, grad, mom)


def times(left, right):
    return jnp.dot(left, right, preferred_element_type=f32)


def gram_of(tall):
    return lax.dot_general(tall, tall, (((0,), (0,)), ((), ())), preferred_element_type=f32)


def rows_at(in_ref):
    part = in_ref[...]
    return part.reshape(part.shape[0] * part.shape[1], part.shape[2])


def store_upper(out_ref, full):
    for n, (i, j) in enumerate(BLOCKS):
        out_ref[n * SIDE : (n + 1) * SIDE, :] = full[
            i * SIDE : (i + 1) * SIDE, j * SIDE : (j + 1) * SIDE
        ].astype(out_ref.dtype)


def load_full(full_ref, blocks):
    for n, (i, j) in enumerate(BLOCKS):
        block = blocks[n * SIDE : (n + 1) * SIDE, :]
        full_ref[i * SIDE : (i + 1) * SIDE, j * SIDE : (j + 1) * SIDE] = block.astype(full_ref.dtype)
        if i != j:
            full_ref[j * SIDE : (j + 1) * SIDE, i * SIDE : (i + 1) * SIDE] = block.T.astype(full_ref.dtype)


def gram_kernel(in_ref, out_ref):
    store_upper(out_ref, gram_of(rows_at(in_ref)))


def partial_gram(received):
    return pl.pallas_call(
        gram_kernel,
        out_shape=jax.ShapeDtypeStruct((len(BLOCKS) * SIDE, SIDE), bf16),
        compiler_params=pltpu.CompilerParams(vmem_limit_bytes=SMALL_GRANT),
        cost_estimate=pl.CostEstimate(
            flops=2 * received.size * COLS, bytes_accessed=2 * received.size, transcendentals=0
        ),
        name="gram",
    )(received)


def composed(gram, steps):
    row = lax.broadcasted_iota(jnp.int32, gram.shape, 0)
    col = lax.broadcasted_iota(jnp.int32, gram.shape, 1)
    whole = None
    for step in range(steps):
        rounded = gram.astype(bf16)
        kept = rounded.astype(f32)
        poly = (cubic_coef * kept + quintic_coef * times(rounded, rounded)).astype(bf16)
        if whole is None:
            whole = poly.astype(f32) + jnp.where(row == col, linear_coef, 0.0)
        else:
            whole = linear_coef * whole + times(whole.astype(bf16), poly)
        if step + 1 < steps:
            half = linear_coef * kept + times(rounded, poly)
            gram = linear_coef * half + times(half.astype(bf16), poly)
    return whole


def factor_kernel(own_ref, part_ref, out_ref, full_ref):
    load_full(full_ref, part_ref[...].astype(f32))
    gram = gram_of(rows_at(own_ref)) + full_ref[...]
    row = lax.broadcasted_iota(jnp.int32, gram.shape, 0)
    col = lax.broadcasted_iota(jnp.int32, gram.shape, 1)
    inverse = 1.0 / (jnp.sqrt(jnp.sum(jnp.where(row == col, gram, 0.0))) + norm_epsilon)
    store_upper(out_ref, composed(gram * inverse * inverse, ITERS) * inverse)


def shared_factor(own, part):
    return pl.pallas_call(
        factor_kernel,
        out_shape=jax.ShapeDtypeStruct((len(BLOCKS) * SIDE, SIDE), bf16),
        scratch_shapes=[pltpu.VMEM((COLS, COLS), f32)],
        compiler_params=pltpu.CompilerParams(vmem_limit_bytes=SMALL_GRANT),
        cost_estimate=pl.CostEstimate(flops=5 * 10**9, bytes_accessed=4 * own.size, transcendentals=0),
        name="factor",
    )(own, part)


def apply_kernel(in_ref, factor_ref, out_hbm, out_buf, full_ref, out_sem):
    load_full(full_ref, factor_ref[...].astype(f32))
    peers, rows, cols = in_ref.shape
    step = peers // 4

    for k in range(4):
        part = pl.ds(k * step, step)
        product = times(in_ref[part].reshape(step * rows, cols), full_ref[...])
        out_buf[part] = product.reshape(step, rows, cols).astype(bf16)
        pltpu.make_async_copy(out_buf.at[part], out_hbm.at[part], out_sem).start()
    pltpu.make_async_copy(out_buf, out_hbm, out_sem).wait()


def applied(received, factor):
    return pl.pallas_call(
        apply_kernel,
        out_specs=pl.BlockSpec(memory_space=pl.ANY),
        out_shape=jax.ShapeDtypeStruct(received.shape, bf16),
        scratch_shapes=[
            pltpu.VMEM(received.shape, bf16),
            pltpu.VMEM((COLS, COLS), bf16),
            pltpu.SemaphoreType.DMA(()),
        ],
        compiler_params=pltpu.CompilerParams(vmem_limit_bytes=SMALL_GRANT),
        cost_estimate=pl.CostEstimate(
            flops=2 * received.size * COLS, bytes_accessed=4 * received.size, transcendentals=0
        ),
        name="apply",
    )(received, factor)


def finish_kernel(group, place_ref, ortho_ref, weight_hbm, *refs):
    out_hbm, weight_buf, sems, out_sem = refs[-4:]
    plane = place_ref[0]
    peers = ortho_ref.shape[0]
    rows = weight_buf.shape[2]
    scale = learn_rate * 0.2 * math.sqrt(max(ROWS, COLS))
    for peer in range(peers):
        for k, away in enumerate(group):
            pltpu.make_async_copy(
                weight_hbm.at[rows_of(peer, away, plane)], weight_buf.at[peer, k], sems.at[peer]
            ).start()

    @pl.loop(0, peers)
    def _(peer):
        pltpu.make_async_copy(weight_hbm.at[pl.ds(0, len(group))], weight_buf.at[peer], sems.at[peer]).wait()
        for k, away in enumerate(group):
            ortho = ortho_ref[peer, k * rows : (k + 1) * rows].astype(f32)
            weight = weight_buf[peer, k].astype(f32)
            weight_buf[peer, k] = (weight * (1.0 - learn_rate * weight_decay) - scale * ortho).astype(bf16)
            pltpu.make_async_copy(
                weight_buf.at[peer, k], out_hbm.at[rows_of(peer, away, plane)], out_sem.at[peer]
            ).start()

    for peer in range(peers):
        pltpu.make_async_copy(weight_buf.at[peer], out_hbm.at[pl.ds(0, len(group))], out_sem.at[peer]).wait()


def finished(group, place, ortho, weight, before):
    peers = ortho.shape[0]
    rows = weight.shape[1]
    anywhere = pl.BlockSpec(memory_space=pl.ANY)
    earlier = () if before is None else (before,)
    return pl.pallas_call(
        functools.partial(finish_kernel, group),
        grid_spec=pltpu.PrefetchScalarGridSpec(
            num_scalar_prefetch=1,
            grid=(1,),
            in_specs=[pl.BlockSpec(ortho.shape, lambda i, p: (0, 0, 0)), anywhere] + [anywhere] * len(earlier),
            out_specs=anywhere,
            scratch_shapes=[
                pltpu.VMEM((peers, len(group), rows, COLS), bf16),
                pltpu.SemaphoreType.DMA((peers,)),
                pltpu.SemaphoreType.DMA((peers,)),
            ],
        ),
        out_shape=jax.ShapeDtypeStruct(weight.shape, bf16),
        input_output_aliases={3: 0} if earlier else {},
        compiler_params=pltpu.CompilerParams(vmem_limit_bytes=SMALL_GRANT),
        cost_estimate=pl.CostEstimate(flops=3 * ortho.size, bytes_accessed=6 * ortho.size, transcendentals=0),
        name="finish",
    )(place, ortho, weight, *earlier)


def across(value):
    return lax.all_to_all(
        value, SPREAD, split_axis=0, concat_axis=0, axis_index_groups=exchange_groups(), tiled=True
    )


def opposite(value):
    count = lax.axis_size(DEPTH)
    return lax.ppermute(value, DEPTH, [(k, (k + count // 2) % count) for k in range(count)])


def local(weight, momentum, gradient, assign):
    grad = gradient[0]
    mom = momentum[0]
    slots = assign[0]
    plane = lax.axis_index(DEPTH) + lax.axis_size(DEPTH) - lax.axis_index(CORE)
    pair = (lax.rem(plane, 4) // 2).reshape(1)
    count = grad.size * lax.axis_size(ALL_AXES)
    partials, near_grad, near_mom = prepared(pair, slots, grad, mom)
    shared = lax.all_to_all(
        partials.reshape(DEVICES, 1, 128), ALL_AXES, split_axis=0, concat_axis=0, tiled=True
    ).reshape(DEVICES, 128)
    ready = updated(count, 1, shared, near_grad, near_mom)
    far = across(ready)
    ready = updated(count, 0, shared, near_grad, near_mom)
    own = across(ready)
    part = partial_gram(far)
    part = opposite(part)
    state = momentum_call(state_kernel, count, slots, shared, grad, mom)
    factor = shared_factor(own, part)
    given = opposite(factor)
    ready = applied(own, factor)
    ortho = across(ready)
    result = finished((0,), pair, ortho, weight[0], None)
    ready = applied(far, given)
    ortho = across(ready)
    result = finished((1,), pair, ortho, weight[0], result)
    return (result[None], state[None])


def solution(mesh):
    torus = Mesh(
        mesh.devices.reshape(4, 4, 4, 2, 2),
        ("rows_0", "rows_1", "rows_2", "experts_0", "experts_1"),
    )
    sharded = P(EXPERTS, None, ROWS_AXES, None)
    return jax.shard_map(
        local,
        mesh=torus,
        in_specs=(sharded, sharded, sharded, P(EXPERTS, None)),
        out_specs=(sharded, sharded),
        check_vma=False,
    )
```

time: 159 us -> 169 us (1.063)
  the two profiles are of different devices: /device:TPU:32 before, /device:TPU:8 now
where the time goes in v5:
time: 169 us; the launch traced here: 168 us
  waiting for transfers between devices  77.7 us (46%)
  starting transfers between devices  30.3 us (18%)
  blocking collectives  26.8 us (16%)
  Pallas kernels  26.2 us (16%)
  local copies, waits for them, and re-layouts  6.47 us (4%)
    all_to_all x4, waiting for transfers between devices, across(): lax.all_to_all(value, SPREAD, split_axis=0, concat_axis=0, axis_index_gro...  46.6 us
    ppermute x2, waiting for transfers between devices, opposite(): lax.ppermute(value, DEPTH, [(k, (k + count // 2) % count) for k in range(...  31.1 us
    all_to_all x1, blocking collectives, local(): lax.all_to_all(partials.reshape(DEVICES, 1, 128), ALL_AXES, split_axis=0,...  26.8 us
    all_to_all x4, starting transfers between devices, across(): lax.all_to_all(value, SPREAD, split_axis=0, concat_axis=0, axis_index_gro...  24 us
    pallas_call x1, Pallas kernels, shared_factor(): pl.pallas_call(factor_kernel, out_shape=jax.ShapeDtypeStruct((len(BLOCKS)...  6.6 us
    unnamed x18, local copies, waits for them, and re-layouts  6.47 us
    ppermute x2, starting transfers between devices, opposite(): lax.ppermute(value, DEPTH, [(k, (k + count // 2) % count) for k in range(...  6.29 us
    pallas_call x2, Pallas kernels, finished(): pl.pallas_call(functools.partial(finish_kernel, group), grid_spec=pltpu.P...  6.19 us
  transfers between devices with their start and end apart: 6, of which 6 were waited for; matrix products, arithmetic and copies ran while one was open for 0% of the time, Pallas kernels for 7%

profile of v5, /device:TPU:8, one launch (start us, length us, event | category | flops | bytes accessed | tf_op | source)
XLA Modules:
  0.0 168.2 jit_solution(5766108133866098620)
XLA Ops:
  0.7 0.0 copy-start.8
  0.7 0.6 copy-done.8
  1.3 2.8 %prepare.1 = (f32[256,128]{1,0:T(8,128)S(1)}, bf16[64,32,512]{2,1,0:T(8,128)(2,1)S(1)}, bf16[64,32,512]{2,1,0:T(8,128)(2,1)S(1)}) custom-call(s32[1]{0:T(128)} %bitcast.pair_ref.place_ref, s32[64]{0:T(128)S(1)} %bitcast.18, bf16[64,32,512]{2,1,0:T(8,128)(2,1)} %bitcast.19, bf16[64,32,512]{2,1,0:T(8,128)(2,1)} %bitcast.21), custom_call_target="tpu_custom_call" | custom-call | flops 2097152 | bytes 8388608 | tf_op jit(solution)/shard_map/prepare/pallas_call | solution.py:89
  4.1 26.8 %all_to_all.25 = f32[256,1,128]{2,1,0:T(1,128)S(1)} all-to-all(f32[256,1,128]{2,1,0:T(1,128)S(1)} %bitcast.16), channel_id=1, replica_groups=mesh['rows_0'=4,'rows_1'=4,'rows_2'=4,'experts_0'=2,'experts_1'=2] {'row..., dimensions={0} | all-to-all | bytes 262144 | tf_op jit(solution)/shard_map/all_to_all | solution.py:399
  30.9 0.0 copy-start.7
  30.9 0.9 update.2
  31.8 0.0 copy-start.1
  31.8 1.3 copy-done.1
  33.1 0.0 copy-start.6
  33.1 1.0 copy-done.6
  34.0 5.1 %all-to-all-start.1 = ((bf16[32,32,512]{2,1,0:T(8,128)(2,1)}), bf16[32,32,512]{2,1,0:T(8,128)(2,1)S(1)}, u32[]{:S(2)}, u32[]{:S(2)}) async-start(bf16[32,32,512]{2,1,0:T(8,128)(2,1)} %copy-done.6), calls=%async_computation.1 | async-start | bytes 2097152 | tf_op jit(solution)/shard_map/all_to_all | solution.py:381
  39.2 0.0 copy-done.7
  39.2 0.0 copy-start.2
  39.2 1.6 copy-done.2
  40.8 0.9 update.3
  41.6 0.0 copy-start.5
  41.6 1.0 copy-done.5
  42.6 14.9 %all-to-all-done.1.in_ref = bf16[32,32,512]{2,1,0:T(8,128)(2,1)S(1)} async-done(((bf16[32,32,512]{2,1,0:T(8,128)(2,1)}), bf16[32,32,512]{2,1,0:T(8,128)(2,1)S(1)}, u32[]{:S(2)}, u32[]{:S(2)}) %all-to-all-start.1) | async-done | bytes 1048608 | tf_op jit(solution)/shard_map/all_to_all | solution.py:381
  57.5 5.1 %all-to-all-start.2 = ((bf16[32,32,512]{2,1,0:T(8,128)(2,1)}), bf16[32,32,512]{2,1,0:T(8,128)(2,1)S(1)}, u32[]{:S(2)}, u32[]{:S(2)}) async-start(bf16[32,32,512]{2,1,0:T(8,128)(2,1)} %copy-done.5), calls=%async_computation.2 | async-start | bytes 2097152 | tf_op jit(solution)/shard_map/all_to_all | solution.py:381
  62.7 0.7 gram.1
  63.4 2.0 %collective-permute-start = (bf16[1280,128]{1,0:T(8,128)(2,1)S(1)}, bf16[1280,128]{1,0:T(8,128)(2,1)S(1)}, u32[]{:S(2)}, u32[]{:S(2)}) collective-permute-start(bf16[1280,128]{1,0:T(8,128)(2,1)S(1)} %gram.1), channel_id=1, source_target_pairs={{0,32},{16,48},{32,0},{48,16},{1,33},{17,49},{33,1},{49,17},{2,34}... | collective-permute-start | bytes 983048 | tf_op jit(solution)/shard_map/ppermute | solution.py:388
  65.4 20.5 %all-to-all-done.2.own_ref.in_ref = bf16[32,32,512]{2,1,0:T(8,128)(2,1)S(1)} async-done(((bf16[32,32,512]{2,1,0:T(8,128)(2,1)}), bf16[32,32,512]{2,1,0:T(8,128)(2,1)S(1)}, u32[]{:S(2)}, u32[]{:S(2)}) %all-to-all-start.2) | async-done | bytes 1048608 | tf_op jit(solution)/shard_map/all_to_all | solution.py:381
  85.9 5.5 %collective-permute-done.part_ref = bf16[1280,128]{1,0:T(8,128)(2,1)S(1)} collective-permute-done((bf16[1280,128]{1,0:T(8,128)(2,1)S(1)}, bf16[1280,128]{1,0:T(8,128)(2,1)S(1)}, u32[]{:S(2)}, u32[]{:S(2)}) %collective-permute-start) | collective-permute-done | bytes 327712 | tf_op jit(solution)/shard_map/ppermute | solution.py:388
  91.4 6.6 %factor.1.factor_ref = bf16[1280,128]{1,0:T(8,128)(2,1)S(1)} custom-call(bf16[32,32,512]{2,1,0:T(8,128)(2,1)S(1)} %all-to-all-done.2.own_ref.in_ref, bf16[1280,128]{1,0:T(8,128)(2,1)S(1)} %collective-permute-done.part_ref), custom_call_target="tpu_custom_call" | custom-call | flops 5000000000 | bytes 2097152 | tf_op jit(solution)/shard_map/factor/pallas_call | solution.py:286
  98.0 1.5 apply.3
  99.5 7.4 %all-to-all-start.4 = ((bf16[32,32,512]{2,1,0:T(8,128)(2,1)}), bf16[32,32,512]{2,1,0:T(8,128)(2,1)S(1)}, u32[]{:S(2)}, u32[]{:S(2)}) async-start(bf16[32,32,512]{2,1,0:T(8,128)(2,1)} %apply.3), calls=%async_computation.4 | async-start | bytes 2097152 | tf_op jit(solution)/shard_map/all_to_all | solution.py:381
  106.9 4.3 %collective-permute-start.1 = (bf16[1280,128]{1,0:T(8,128)(2,1)S(1)}, bf16[1280,128]{1,0:T(8,128)(2,1)S(1)}, u32[]{:S(2)}, u32[]{:S(2)}) collective-permute-start(bf16[1280,128]{1,0:T(8,128)(2,1)S(1)} %factor.1.factor_ref), channel_id=1, source_target_pairs={{0,32},{16,48},{32,0},{48,16},{1,33},{17,49},{33,1},{49,17},{2,34}... | collective-permute-start | bytes 983048 | tf_op jit(solution)/shard_map/ppermute | solution.py:388
  111.2 25.6 %collective-permute-done.1.factor_ref = bf16[1280,128]{1,0:T(8,128)(2,1)S(1)} collective-permute-done((bf16[1280,128]{1,0:T(8,128)(2,1)S(1)}, bf16[1280,128]{1,0:T(8,128)(2,1)S(1)}, u32[]{:S(2)}, u32[]{:S(2)}) %collective-permute-start.1) | collective-permute-done | bytes 327712 | tf_op jit(solution)/shard_map/ppermute | solution.py:388
  136.8 1.5 apply.2
  138.3 1.0 all-to-all-done.4.ortho_ref
  139.4 0.0 copy-start.3
  139.4 1.0 copy-done.3
  140.3 6.4 %all-to-all-start.3 = ((bf16[32,32,512]{2,1,0:T(8,128)(2,1)}), bf16[32,32,512]{2,1,0:T(8,128)(2,1)S(1)}, u32[]{:S(2)}, u32[]{:S(2)}) async-start(bf16[32,32,512]{2,1,0:T(8,128)(2,1)} %apply.2), calls=%async_computation.3 | async-start | bytes 2097152 | tf_op jit(solution)/shard_map/all_to_all | solution.py:381
  146.7 0.0 copy-start
  146.7 0.0 copy-start.4
  146.7 5.1 %shard_map.59 = bf16[64,32,512]{2,1,0:T(8,128)(2,1)} custom-call(s32[64]{0:T(128)} %bitcast.17, f32[256,128]{1,0:T(8,128)} %bitcast.15, bf16[64,32,512]{2,1,0:T(8,128)(2,1)} %bitcast.20, bf16[64,32,512]{2,1,0:T(8,128)(2,1)} %bitcast.22), custom_call_target="tpu_custom_call" | custom-call | flops 6291456 | bytes 6291456 | tf_op jit(solution)/shard_map/pallas_call | solution.py:190
  151.9 0.0 copy-done
  151.9 0.0 copy-done.4
  151.9 3.1 %finish.2.refs_0_ = bf16[64,32,512]{2,1,0:T(8,128)(2,1)} custom-call(s32[1]{0:T(128)} %bitcast.pair_ref.place_ref, bf16[32,32,512]{2,1,0:T(8,128)(2,1)S(1)} %copy-done.4, bf16[64,32,512]{2,1,0:T(8,128)(2,1)S(1)} %bitcast.11), custom_call_target="tpu_custom_call" | custom-call | flops 1572864 | bytes 3145728 | tf_op jit(solution)/shard_map/finish/pallas_call | solution.py:359
  155.0 10.2 %all-to-all-done.3.ortho_ref = bf16[32,32,512]{2,1,0:T(8,128)(2,1)S(1)} async-done(((bf16[32,32,512]{2,1,0:T(8,128)(2,1)}), bf16[32,32,512]{2,1,0:T(8,128)(2,1)S(1)}, u32[]{:S(2)}, u32[]{:S(2)}) %all-to-all-start.3) | async-done | bytes 1048608 | tf_op jit(solution)/shard_map/all_to_all | solution.py:381
  165.2 3.1 %finish.3 = bf16[64,32,512]{2,1,0:T(8,128)(2,1)} custom-call(s32[1]{0:T(128)} %bitcast.pair_ref.place_ref, bf16[32,32,512]{2,1,0:T(8,128)(2,1)S(1)} %all-to-all-done.3.ortho_ref, bf16[64,32,512]{2,1,0:T(8,128)(2,1)S(1)} %bitcast.12, bf16[64,32,512]{2,1,0:T(8,128)(2,1)} %finish.2.refs_0_), custom_call_target="tpu_custom_call", output_to_operand_aliasing={{}: (3, {})} | custom-call | flops 1572864 | bytes 3145728 | tf_op jit(solution)/shard_map/finish/pallas_call | solution.py:359
Async XLA Ops:
  0.7 0.7 copy-start.8
  30.9 8.3 %copy-start.7 = (f32[256,1,128]{2,1,0:T(1,128)}, f32[256,1,128]{2,1,0:T(1,128)S(1)}, u32[]{:S(2)}) copy-start(f32[256,1,128]{2,1,0:T(1,128)S(1)} %all_to_all.25) | copy-start | bytes 393220
  31.8 1.3 copy-start.1
  33.1 1.0 copy-start.6
  34.0 23.5 %all-to-all-start.1 = ((bf16[32,32,512]{2,1,0:T(8,128)(2,1)}), bf16[32,32,512]{2,1,0:T(8,128)(2,1)S(1)}, u32[]{:S(2)}, u32[]{:S(2)}) async-start(bf16[32,32,512]{2,1,0:T(8,128)(2,1)} %copy-done.6), calls=%async_computation.1 | async-start | bytes 2097152 | tf_op jit(solution)/shard_map/all_to_all | solution.py:381
  39.2 1.6 copy-start.2
  41.6 1.0 copy-start.5
  57.5 28.4 %all-to-all-start.2 = ((bf16[32,32,512]{2,1,0:T(8,128)(2,1)}), bf16[32,32,512]{2,1,0:T(8,128)(2,1)S(1)}, u32[]{:S(2)}, u32[]{:S(2)}) async-start(bf16[32,32,512]{2,1,0:T(8,128)(2,1)} %copy-done.5), calls=%async_computation.2 | async-start | bytes 2097152 | tf_op jit(solution)/shard_map/all_to_all | solution.py:381
  63.4 27.9 %collective-permute-start = (bf16[1280,128]{1,0:T(8,128)(2,1)S(1)}, bf16[1280,128]{1,0:T(8,128)(2,1)S(1)}, u32[]{:S(2)}, u32[]{:S(2)}) collective-permute-start(bf16[1280,128]{1,0:T(8,128)(2,1)S(1)} %gram.1), channel_id=1, source_target_pairs={{0,32},{16,48},{32,0},{48,16},{1,33},{17,49},{33,1},{49,17},{2,34}... | collective-permute-start | bytes 983048 | tf_op jit(solution)/shard_map/ppermute | solution.py:388
  99.5 39.9 %all-to-all-start.4 = ((bf16[32,32,512]{2,1,0:T(8,128)(2,1)}), bf16[32,32,512]{2,1,0:T(8,128)(2,1)S(1)}, u32[]{:S(2)}, u32[]{:S(2)}) async-start(bf16[32,32,512]{2,1,0:T(8,128)(2,1)} %apply.3), calls=%async_computation.4 | async-start | bytes 2097152 | tf_op jit(solution)/shard_map/all_to_all | solution.py:381
  106.9 29.9 %collective-permute-start.1 = (bf16[1280,128]{1,0:T(8,128)(2,1)S(1)}, bf16[1280,128]{1,0:T(8,128)(2,1)S(1)}, u32[]{:S(2)}, u32[]{:S(2)}) collective-permute-start(bf16[1280,128]{1,0:T(8,128)(2,1)S(1)} %factor.1.factor_ref), channel_id=1, source_target_pairs={{0,32},{16,48},{32,0},{48,16},{1,33},{17,49},{33,1},{49,17},{2,34}... | collective-permute-start | bytes 983048 | tf_op jit(solution)/shard_map/ppermute | solution.py:388
  139.4 1.0 copy-start.3
  140.3 24.8 %all-to-all-start.3 = ((bf16[32,32,512]{2,1,0:T(8,128)(2,1)}), bf16[32,32,512]{2,1,0:T(8,128)(2,1)S(1)}, u32[]{:S(2)}, u32[]{:S(2)}) async-start(bf16[32,32,512]{2,1,0:T(8,128)(2,1)} %apply.2), calls=%async_computation.3 | async-start | bytes 2097152 | tf_op jit(solution)/shard_map/all_to_all | solution.py:381
  146.7 5.2 %copy-start = (bf16[1,64,32,512]{3,2,1,0:T(8,128)(2,1)S(1)}, bf16[1,64,32,512]{3,2,1,0:T(8,128)(2,1)}, u32[]{:S(2)}) copy-start(bf16[1,64,32,512]{3,2,1,0:T(8,128)(2,1)} %param.4) | copy-start | bytes 6291460
  146.7 5.2 %copy-start.4 = (bf16[32,32,512]{2,1,0:T(8,128)(2,1)S(1)}, bf16[32,32,512]{2,1,0:T(8,128)(2,1)}, u32[]{:S(2)}) copy-start(bf16[32,32,512]{2,1,0:T(8,128)(2,1)} %copy-done.3) | copy-start | bytes 3145732

commit v6 on v5

--- a/solution.py
+++ b/solution.py
@@ -8,7 +8,6 @@
 from jax.experimental.pallas import tpu as pltpu
 from jax.sharding import Mesh
 from jax.sharding import PartitionSpec as P
-
 
 ROWS = 2048
 COLS = 512
@@ -60,13 +59,12 @@
 
 def prepare_kernel(pair_ref, slots_ref, grad_hbm, mom_hbm, part_ref, grad_ref, mom_ref, acc_ref, grad_sems, sem):
     chunks = grad_ref.shape[0] // CHUNK
-    half = grad_ref.shape[0] // 2
     pair = pair_ref[0]
-    for k in range(2 * half):
-        matrix = rows_of(k % half, 1 - k // half, pair)
+    for k in range(grad_ref.shape[0]):
+        matrix = rows_of(k // 2, 1 - k % 2, pair)
         pltpu.make_async_copy(grad_hbm.at[matrix], grad_ref.at[k], grad_sems.at[k // CHUNK]).start()
-    for k in range(2 * half):
-        matrix = rows_of(k % half, 1 - k // half, pair)
+    for k in range(mom_ref.shape[0]):
+        matrix = rows_of(k // 2, 1 - k % 2, pair)
         pltpu.make_async_copy(mom_hbm.at[slots_ref[matrix]], mom_ref.at[k], sem).start()
     acc_ref[...] = jnp.zeros_like(acc_ref)
 
@@ -133,31 +131,28 @@
     pltpu.make_async_copy(mom_hbm.at[rows], mom_buf.at[rows], sems.at[1, chunk]).wait()
 
 
-def update_kernel(count, first, part_ref, grad_ref, mom_ref, out_hbm, out_buf, sem):
+def update_kernel(count, part_ref, grad_ref, mom_ref, out_hbm, out_buf, sem):
     clip = clip_from(part_ref[...], count)
 
-    @pl.loop(0, out_buf.shape[0] // CHUNK)
+    @pl.loop(0, grad_ref.shape[0] // CHUNK)
     def _(chunk):
         rows = pl.ds(chunk * CHUNK, CHUNK)
-        source = pl.ds(first + chunk * CHUNK, CHUNK)
-        scaled = clip * grad_ref[source].astype(f32)
-        state = beta_decay * mom_ref[source].astype(f32) + scaled
+        scaled = clip * grad_ref[rows].astype(f32)
+        state = beta_decay * mom_ref[rows].astype(f32) + scaled
         out_buf[rows] = (scaled + beta_decay * state).astype(bf16)
         pltpu.make_async_copy(out_buf.at[rows], out_hbm.at[rows], sem).start()
 
     pltpu.make_async_copy(out_buf, out_hbm, sem).wait()
 
 
-def updated(count, away, partials, grad, mom):
-    half = grad.shape[0] // 2
-    shape = (half,) + grad.shape[1:]
-    return pl.pallas_call(
-        functools.partial(update_kernel, count, half * (1 - away)),
+def updated(count, partials, grad, mom):
+    return pl.pallas_call(
+        functools.partial(update_kernel, count),
         out_specs=pl.BlockSpec(memory_space=pl.ANY),
-        out_shape=jax.ShapeDtypeStruct(shape, bf16),
-        scratch_shapes=[pltpu.VMEM(shape, bf16), pltpu.SemaphoreType.DMA(())],
+        out_shape=jax.ShapeDtypeStruct(grad.shape, bf16),
+        scratch_shapes=[pltpu.VMEM(grad.shape, bf16), pltpu.SemaphoreType.DMA(())],
         compiler_params=pltpu.CompilerParams(vmem_limit_bytes=UPDATE_GRANT),
-        cost_estimate=pl.CostEstimate(flops=3 * grad.size, bytes_accessed=3 * grad.size, transcendentals=0),
+        cost_estimate=pl.CostEstimate(flops=6 * grad.size, bytes_accessed=6 * grad.size, transcendentals=0),
         name="update",
     )(partials, grad, mom)
 
@@ -185,7 +180,7 @@
         pltpu.make_async_copy(mom_buf.at[rows], out_hbm.at[rows], out_sem.at[chunk]).wait()
 
 
-def momentum_call(kernel, count, slots, partials, grad, mom):
+def momentum_call(kernel, name, count, slots, partials, grad, mom):
     chunks = grad.shape[0] // CHUNK
     return pl.pallas_call(
         functools.partial(kernel, count),
@@ -208,6 +203,7 @@
         out_shape=jax.ShapeDtypeStruct(grad.shape, bf16),
         compiler_params=pltpu.CompilerParams(vmem_limit_bytes=LARGE_GRANT),
         cost_estimate=pl.CostEstimate(flops=6 * grad.size, bytes_accessed=6 * grad.size, transcendentals=0),
+        name=name,
     )(slots, partials, grad, mom)
 
 
@@ -219,8 +215,8 @@
     return lax.dot_general(tall, tall, (((0,), (0,)), ((), ())), preferred_element_type=f32)
 
 
-def rows_at(in_ref):
-    part = in_ref[...]
+def rows_at(in_ref, k):
+    part = in_ref[:, k]
     return part.reshape(part.shape[0] * part.shape[1], part.shape[2])
 
 
@@ -239,19 +235,23 @@
             full_ref[j * SIDE : (j + 1) * SIDE, i * SIDE : (i + 1) * SIDE] = block.T.astype(full_ref.dtype)
 
 
-def gram_kernel(in_ref, out_ref):
-    store_upper(out_ref, gram_of(rows_at(in_ref)))
-
-
-def partial_gram(received):
-    return pl.pallas_call(
-        gram_kernel,
-        out_shape=jax.ShapeDtypeStruct((len(BLOCKS) * SIDE, SIDE), bf16),
+def far_kernel(in_ref, out_ref):
+    store_upper(out_ref, gram_of(rows_at(in_ref, 0)))
+
+
+def own_kernel(in_ref, out_ref):
+    out_ref[...] = gram_of(rows_at(in_ref, 1))
+
+
+def gram_call(kernel, name, received, shape):
+    return pl.pallas_call(
+        kernel,
+        out_shape=shape,
         compiler_params=pltpu.CompilerParams(vmem_limit_bytes=SMALL_GRANT),
         cost_estimate=pl.CostEstimate(
-            flops=2 * received.size * COLS, bytes_accessed=2 * received.size, transcendentals=0
+            flops=received.size * COLS, bytes_accessed=2 * received.size, transcendentals=0
         ),
-        name="gram",
+        name=name,
     )(received)
 
 
@@ -275,7 +275,7 @@
 
 def factor_kernel(own_ref, part_ref, out_ref, full_ref):
     load_full(full_ref, part_ref[...].astype(f32))
-    gram = gram_of(rows_at(own_ref)) + full_ref[...]
+    gram = own_ref[...] + full_ref[...]
     row = lax.broadcasted_iota(jnp.int32, gram.shape, 0)
     col = lax.broadcasted_iota(jnp.int32, gram.shape, 1)
     inverse = 1.0 / (jnp.sqrt(jnp.sum(jnp.where(row == col, gram, 0.0))) + norm_epsilon)
@@ -293,88 +293,75 @@
     )(own, part)
 
 
-def apply_kernel(in_ref, factor_ref, out_hbm, out_buf, full_ref, out_sem):
+def apply_kernel(which, in_ref, factor_ref, *refs):
+    out_hbm, out_buf, full_ref, out_sem = refs[-4:]
     load_full(full_ref, factor_ref[...].astype(f32))
-    peers, rows, cols = in_ref.shape
+    peers, _, rows, cols = in_ref.shape
     step = peers // 4
-
     for k in range(4):
         part = pl.ds(k * step, step)
-        product = times(in_ref[part].reshape(step * rows, cols), full_ref[...])
+        product = times(in_ref[part, which].reshape(step * rows, cols), full_ref[...])
         out_buf[part] = product.reshape(step, rows, cols).astype(bf16)
-        pltpu.make_async_copy(out_buf.at[part], out_hbm.at[part], out_sem).start()
-    pltpu.make_async_copy(out_buf, out_hbm, out_sem).wait()
-
-
-def applied(received, factor):
-    return pl.pallas_call(
-        apply_kernel,
-        out_specs=pl.BlockSpec(memory_space=pl.ANY),
+        pltpu.make_async_copy(out_buf.at[part], out_hbm.at[part, which], out_sem).start()
+    pltpu.make_async_copy(out_buf, out_hbm.at[:, which], out_sem).wait()
+
+
+def applied(which, received, factor, before):
+    earlier = () if before is None else (before,)
+    vmem = pl.BlockSpec(memory_space=pltpu.VMEM)
+    anywhere = pl.BlockSpec(memory_space=pl.ANY)
+    return pl.pallas_call(
+        functools.partial(apply_kernel, which),
+        in_specs=[vmem, vmem] + [anywhere] * len(earlier),
+        out_specs=anywhere,
         out_shape=jax.ShapeDtypeStruct(received.shape, bf16),
         scratch_shapes=[
-            pltpu.VMEM(received.shape, bf16),
+            pltpu.VMEM(received.shape[:1] + received.shape[2:], bf16),
             pltpu.VMEM((COLS, COLS), bf16),
             pltpu.SemaphoreType.DMA(()),
         ],
+        input_output_aliases={2: 0} if earlier else {},
         compiler_params=pltpu.CompilerParams(vmem_limit_bytes=SMALL_GRANT),
         cost_estimate=pl.CostEstimate(
-            flops=2 * received.size * COLS, bytes_accessed=4 * received.size, transcendentals=0
+            flops=received.size * COLS, bytes_accessed=3 * received.size, transcendentals=0
         ),
         name="apply",
-    )(received, factor)
-
-
-def finish_kernel(group, place_ref, ortho_ref, weight_hbm, *refs):
-    out_hbm, weight_buf, sems, out_sem = refs[-4:]
-    plane = place_ref[0]
-    peers = ortho_ref.shape[0]
-    rows = weight_buf.shape[2]
+    )(received, factor, *earlier)
+
+
+def finish_kernel(pair_ref, ortho_ref, weight_ref, out_hbm, out_buf, sem):
     scale = learn_rate * 0.2 * math.sqrt(max(ROWS, COLS))
-    for peer in range(peers):
-        for k, away in enumerate(group):
-            pltpu.make_async_copy(
-                weight_hbm.at[rows_of(peer, away, plane)], weight_buf.at[peer, k], sems.at[peer]
-            ).start()
-
-    @pl.loop(0, peers)
-    def _(peer):
-        pltpu.make_async_copy(weight_hbm.at[pl.ds(0, len(group))], weight_buf.at[peer], sems.at[peer]).wait()
-        for k, away in enumerate(group):
-            ortho = ortho_ref[peer, k * rows : (k + 1) * rows].astype(f32)
-            weight = weight_buf[peer, k].astype(f32)
-            weight_buf[peer, k] = (weight * (1.0 - learn_rate * weight_decay) - scale * ortho).astype(bf16)
-            pltpu.make_async_copy(
-                weight_buf.at[peer, k], out_hbm.at[rows_of(peer, away, plane)], out_sem.at[peer]
-            ).start()
-
-    for peer in range(peers):
-        pltpu.make_async_copy(weight_buf.at[peer], out_hbm.at[pl.ds(0, len(group))], out_sem.at[peer]).wait()
-
-
-def finished(group, place, ortho, weight, before):
-    peers = ortho.shape[0]
-    rows = weight.shape[1]
-    anywhere = pl.BlockSpec(memory_space=pl.ANY)
-    earlier = () if before is None else (before,)
-    return pl.pallas_call(
-        functools.partial(finish_kernel, group),
+    pair = pair_ref[0]
+
+    @pl.loop(0, ortho_ref.shape[0] // CHUNK)
+    def _(chunk):
+        base = chunk * CHUNK
+        for k in range(CHUNK):
+            matrix = base + rows_of(k // 2, 1 - k % 2, pair)
+            kept = weight_ref[matrix].astype(f32) * (1.0 - learn_rate * weight_decay)
+            out_buf[matrix] = (kept - scale * ortho_ref[base + k].astype(f32)).astype(bf16)
+        rows = pl.ds(base, CHUNK)
+        pltpu.make_async_copy(out_buf.at[rows], out_hbm.at[rows], sem).start()
+
+    pltpu.make_async_copy(out_buf, out_hbm, sem).wait()
+
+
+def finished(pair, ortho, weight):
+    whole = pl.BlockSpec(weight.shape, lambda i, p: (0, 0, 0))
+    return pl.pallas_call(
+        finish_kernel,
         grid_spec=pltpu.PrefetchScalarGridSpec(
             num_scalar_prefetch=1,
             grid=(1,),
-            in_specs=[pl.BlockSpec(ortho.shape, lambda i, p: (0, 0, 0)), anywhere] + [anywhere] * len(earlier),
-            out_specs=anywhere,
-            scratch_shapes=[
-                pltpu.VMEM((peers, len(group), rows, COLS), bf16),
-                pltpu.SemaphoreType.DMA((peers,)),
-                pltpu.SemaphoreType.DMA((peers,)),
-            ],
+            in_specs=[whole, whole],
+            out_specs=pl.BlockSpec(memory_space=pl.ANY),
+            scratch_shapes=[pltpu.VMEM(weight.shape, bf16), pltpu.SemaphoreType.DMA(())],
         ),
         out_shape=jax.ShapeDtypeStruct(weight.shape, bf16),
-        input_output_aliases={3: 0} if earlier else {},
-        compiler_params=pltpu.CompilerParams(vmem_limit_bytes=SMALL_GRANT),
+        compiler_params=pltpu.CompilerParams(vmem_limit_bytes=24 << 20),
         cost_estimate=pl.CostEstimate(flops=3 * ortho.size, bytes_accessed=6 * ortho.size, transcendentals=0),
         name="finish",
-    )(place, ortho, weight, *earlier)
+    )(pair, ortho, weight)
 
 
 def across(value):
@@ -399,22 +386,19 @@
     shared = lax.all_to_all(
         partials.reshape(DEVICES, 1, 128), ALL_AXES, split_axis=0, concat_axis=0, tiled=True
     ).reshape(DEVICES, 128)
-    ready = updated(count, 1, shared, near_grad, near_mom)
-    far = across(ready)
-    ready = updated(count, 0, shared, near_grad, near_mom)
-    own = across(ready)
-    part = partial_gram(far)
-    part = opposite(part)
-    state = momentum_call(state_kernel, count, slots, shared, grad, mom)
+    update = updated(count, shared, near_grad, near_mom)
+    received = across(update)
+    state = momentum_call(state_kernel, "state", count, slots, shared, grad, mom)
+    received, state = lax.optimization_barrier((received, state))
+    halves = received.reshape(-1, 2, *received.shape[1:])
+    upper = jax.ShapeDtypeStruct((len(BLOCKS) * SIDE, SIDE), bf16)
+    part = opposite(gram_call(far_kernel, "far", halves, upper))
+    own = gram_call(own_kernel, "own", halves, jax.ShapeDtypeStruct((COLS, COLS), f32))
     factor = shared_factor(own, part)
     given = opposite(factor)
-    ready = applied(own, factor)
-    ortho = across(ready)
-    result = finished((0,), pair, ortho, weight[0], None)
-    ready = applied(far, given)
-    ortho = across(ready)
-    result = finished((1,), pair, ortho, weight[0], result)
-    return (result[None], state[None])
+    result = applied(0, halves, given, applied(1, halves, factor, None))
+    ortho = across(result.reshape(received.shape))
+    return (finished(pair, ortho, weight[0])[None], state[None])
 
 
 def solution(mesh):

time: 169 us -> 153 us (0.905)
  the two profiles are of different devices: /device:TPU:8 before, /device:TPU:1 now
where the time goes in v6:
time: 153 us
  blocking collectives  62.9 us (41%)
  waiting for transfers between devices  58.9 us (38%)
  Pallas kernels  20.6 us (13%)
  starting transfers between devices  7.8 us (5%)
  local copies, waits for them, and re-layouts  1.97 us (1%)
    ppermute x2, waiting for transfers between devices, opposite(): lax.ppermute(value, DEPTH, [(k, (k + count // 2) % count) for k in range(...  36 us
    all_to_all x1, blocking collectives, across(): lax.all_to_all(value, SPREAD, split_axis=0, concat_axis=0, axis_index_gro...  34.5 us
    all_to_all x1, blocking collectives, local(): lax.all_to_all(partials.reshape(DEVICES, 1, 128), ALL_AXES, split_axis=0,...  28.3 us
    all_to_all x1, waiting for transfers between devices, across(): lax.all_to_all(value, SPREAD, split_axis=0, concat_axis=0, axis_index_gro...  22.9 us
    all_to_all x1, starting transfers between devices, across(): lax.all_to_all(value, SPREAD, split_axis=0, concat_axis=0, axis_index_gro...  6.15 us
    pallas_call x1, Pallas kernels, shared_factor(): pl.pallas_call(factor_kernel, out_shape=jax.ShapeDtypeStruct((len(BLOCKS)...  5.77 us
    pallas_call x1, Pallas kernels, momentum_call(): pl.pallas_call(functools.partial(kernel, count), grid_spec=pltpu.Prefetch...  4.88 us
  transfers between devices with their start and end apart: 3, of which 3 were waited for; matrix products, arithmetic and copies ran while one was open for 0% of the time, Pallas kernels for 5%

profile of v6, /device:TPU:1, one launch (start us, length us, event | category | flops | bytes accessed | tf_op | source)
XLA Modules:
  0.0 152.9 jit_solution(5951710348791724563)
XLA Ops:
  0.7 0.0 copy-start.3
  0.7 0.6 copy-done.3
  1.3 2.8 %prepare.1 = (f32[256,128]{1,0:T(8,128)S(1)}, bf16[64,32,512]{2,1,0:T(8,128)(2,1)S(1)}, bf16[64,32,512]{2,1,0:T(8,128)(2,1)S(1)}) custom-call(s32[1]{0:T(128)} %bitcast.pair_ref, s32[64]{0:T(128)S(1)} %bitcast.23, bf16[64,32,512]{2,1,0:T(8,128)(2,1)} %bitcast.24, bf16[64,32,512]{2,1,0:T(8,128)(2,1)} %bitcast.26), custom_call_target="tpu_custom_call" | custom-call | flops 2097152 | bytes 8388608 | tf_op jit(solution)/shard_map/prepare/pallas_call | solution.py:87
  4.1 28.3 %all_to_all.15 = f32[256,1,128]{2,1,0:T(1,128)S(1)} all-to-all(f32[256,1,128]{2,1,0:T(1,128)S(1)} %bitcast.21), channel_id=1, replica_groups=mesh['rows_0'=4,'rows_1'=4,'rows_2'=4,'experts_0'=2,'experts_1'=2] {'row..., dimensions={0} | all-to-all | bytes 262144 | tf_op jit(solution)/shard_map/all_to_all | solution.py:386
  32.4 0.0 copy-start.2
  32.4 1.5 update.1
  33.9 0.0 copy-done.2
  33.9 0.0 copy-start
  33.9 1.3 copy-done
  35.2 6.1 %all-to-all-start.1 = ((bf16[64,32,512]{2,1,0:T(8,128)(2,1)}), bf16[64,32,512]{2,1,0:T(8,128)(2,1)S(1)}, u32[]{:S(2)}, u32[]{:S(2)}) async-start(bf16[64,32,512]{2,1,0:T(8,128)(2,1)} %copy-done), calls=%async_computation.1 | async-start | bytes 4194304 | tf_op jit(solution)/shard_map/all_to_all | solution.py:368
  41.4 4.9 %state.1 = bf16[64,32,512]{2,1,0:T(8,128)(2,1)} custom-call(s32[64]{0:T(128)} %bitcast.22, f32[256,128]{1,0:T(8,128)} %bitcast.20, bf16[64,32,512]{2,1,0:T(8,128)(2,1)} %bitcast.25, bf16[64,32,512]{2,1,0:T(8,128)(2,1)} %bitcast.27), custom_call_target="tpu_custom_call" | custom-call | flops 6291456 | bytes 6291456 | tf_op jit(solution)/shard_map/state/pallas_call | solution.py:185
  46.3 22.9 %all-to-all-done.1 = bf16[64,32,512]{2,1,0:T(8,128)(2,1)S(1)} async-done(((bf16[64,32,512]{2,1,0:T(8,128)(2,1)}), bf16[64,32,512]{2,1,0:T(8,128)(2,1)S(1)}, u32[]{:S(2)}, u32[]{:S(2)}) %all-to-all-start.1) | async-done | bytes 2097184 | tf_op jit(solution)/shard_map/all_to_all | solution.py:368
  69.2 0.7 far.1
  69.9 0.9 collective-permute-start
  70.8 0.7 own.1.own_ref
  71.5 17.9 %collective-permute-done.part_ref = bf16[1280,128]{1,0:T(8,128)(2,1)S(1)} collective-permute-done((bf16[1280,128]{1,0:T(8,128)(2,1)S(1)}, bf16[1280,128]{1,0:T(8,128)(2,1)S(1)}, u32[]{:S(2)}, u32[]{:S(2)}) %collective-permute-start) | collective-permute-done | bytes 327712 | tf_op jit(solution)/shard_map/ppermute | solution.py:375
  89.5 5.8 %factor.1.factor_ref = bf16[1280,128]{1,0:T(8,128)(2,1)S(1)} custom-call(f32[512,512]{1,0:T(8,128)S(1)} %own.1.own_ref, bf16[1280,128]{1,0:T(8,128)(2,1)S(1)} %collective-permute-done.part_ref), custom_call_target="tpu_custom_call" | custom-call | flops 5000000000 | bytes 1048576 | tf_op jit(solution)/shard_map/factor/pallas_call | solution.py:286
  95.2 0.8 collective-permute-start.1
  96.0 1.4 apply.2.refs_0_
  97.4 18.0 %collective-permute-done.1.factor_ref = bf16[1280,128]{1,0:T(8,128)(2,1)S(1)} collective-permute-done((bf16[1280,128]{1,0:T(8,128)(2,1)S(1)}, bf16[1280,128]{1,0:T(8,128)(2,1)S(1)}, u32[]{:S(2)}, u32[]{:S(2)}) %collective-permute-start.1) | collective-permute-done | bytes 327712 | tf_op jit(solution)/shard_map/ppermute | solution.py:375
  115.5 1.4 apply.3
  116.9 0.0 copy-start.1
  116.9 34.5 %all_to_all.16.ortho_ref = bf16[64,32,512]{2,1,0:T(8,128)(2,1)S(1)} all-to-all(bf16[64,32,512]{2,1,0:T(8,128)(2,1)S(1)} %bitcast.17), channel_id=1, replica_groups={{0,4,8,12,16,20,24,28,64,68,72,76,80,84,88,92,128,132,136,140,144,148,1..., dimensions={0} | all-to-all | bytes 4194304 | tf_op jit(solution)/shard_map/all_to_all | solution.py:368
  151.4 0.0 copy-done.1
  151.4 1.5 finish.1
Async XLA Ops:
  0.7 0.7 copy-start.3
  32.4 1.5 copy-start.2
  33.9 1.3 copy-start
  35.2 33.9 %all-to-all-start.1 = ((bf16[64,32,512]{2,1,0:T(8,128)(2,1)}), bf16[64,32,512]{2,1,0:T(8,128)(2,1)S(1)}, u32[]{:S(2)}, u32[]{:S(2)}) async-start(bf16[64,32,512]{2,1,0:T(8,128)(2,1)} %copy-done), calls=%async_computation.1 | async-start | bytes 4194304 | tf_op jit(solution)/shard_map/all_to_all | solution.py:368
  69.9 19.5 %collective-permute-start = (bf16[1280,128]{1,0:T(8,128)(2,1)S(1)}, bf16[1280,128]{1,0:T(8,128)(2,1)S(1)}, u32[]{:S(2)}, u32[]{:S(2)}) collective-permute-start(bf16[1280,128]{1,0:T(8,128)(2,1)S(1)} %far.1), channel_id=1, source_target_pairs={{0,32},{16,48},{32,0},{48,16},{1,33},{17,49},{33,1},{49,17},{2,34}... | collective-permute-start | bytes 983048 | tf_op jit(solution)/shard_map/ppermute | solution.py:375
  95.2 20.2 %collective-permute-start.1 = (bf16[1280,128]{1,0:T(8,128)(2,1)S(1)}, bf16[1280,128]{1,0:T(8,128)(2,1)S(1)}, u32[]{:S(2)}, u32[]{:S(2)}) collective-permute-start(bf16[1280,128]{1,0:T(8,128)(2,1)S(1)} %factor.1.factor_ref), channel_id=1, source_target_pairs={{0,32},{16,48},{32,0},{48,16},{1,33},{17,49},{33,1},{49,17},{2,34}... | collective-permute-start | bytes 983048 | tf_op jit(solution)/shard_map/ppermute | solution.py:375
  116.9 34.5 %copy-start.1 = (bf16[1,64,32,512]{3,2,1,0:T(8,128)(2,1)S(1)}, bf16[1,64,32,512]{3,2,1,0:T(8,128)(2,1)}, u32[]{:S(2)}) copy-start(bf16[1,64,32,512]{3,2,1,0:T(8,128)(2,1)} %param.4) | copy-start | bytes 6291460

commit v7 on v6

--- a/solution.py
+++ b/solution.py
@@ -54,7 +54,7 @@
 
 
 def rows_of(peer, away, pair):
-    return peer * 2 + lax.rem(pair + away, 2)
+    return (peer ^ 4) * 2 + 1 - pair if away else peer * 2 + pair
 
 
 def prepare_kernel(pair_ref, slots_ref, grad_hbm, mom_hbm, part_ref, grad_ref, mom_ref, acc_ref, grad_sems, sem):
@@ -333,14 +333,14 @@
     scale = learn_rate * 0.2 * math.sqrt(max(ROWS, COLS))
     pair = pair_ref[0]
 
-    @pl.loop(0, ortho_ref.shape[0] // CHUNK)
+    @pl.loop(0, ortho_ref.shape[0] // (2 * CHUNK))
     def _(chunk):
-        base = chunk * CHUNK
-        for k in range(CHUNK):
+        base = chunk * (2 * CHUNK)
+        for k in range(2 * CHUNK):
             matrix = base + rows_of(k // 2, 1 - k % 2, pair)
             kept = weight_ref[matrix].astype(f32) * (1.0 - learn_rate * weight_decay)
             out_buf[matrix] = (kept - scale * ortho_ref[base + k].astype(f32)).astype(bf16)
-        rows = pl.ds(base, CHUNK)
+        rows = pl.ds(base, 2 * CHUNK)
         pltpu.make_async_copy(out_buf.at[rows], out_hbm.at[rows], sem).start()
 
     pltpu.make_async_copy(out_buf, out_hbm, sem).wait()
@@ -371,8 +371,12 @@
 
 
 def opposite(value):
-    count = lax.axis_size(DEPTH)
-    return lax.ppermute(value, DEPTH, [(k, (k + count // 2) % count) for k in range(count)])
+    moves = []
+    for plane in range(4):
+        for core in range(2):
+            place = (plane - core) % 4
+            moves.append((plane * 2 + core, (3 - place + core) % 4 * 2 + core))
+    return lax.ppermute(value, (DEPTH, CORE), moves)
 
 
 def local(weight, momentum, gradient, assign):

time: 153 us -> 136 us (0.89)
  the two profiles are of different devices: /device:TPU:1 before, /device:TPU:8 now
where the time goes in v7:
time: 136 us; the launch traced here: 134 us
  blocking collectives  60.6 us (45%)
  waiting for transfers between devices  41.6 us (31%)
  Pallas kernels  20.7 us (15%)
  starting transfers between devices  8.37 us (6%)
  local copies, waits for them, and re-layouts  1.97 us (1%)
    all_to_all x1, blocking collectives, across(): lax.all_to_all(value, SPREAD, split_axis=0, concat_axis=0, axis_index_gro...  33.8 us
    all_to_all x1, blocking collectives, local(): lax.all_to_all(partials.reshape(DEVICES, 1, 128), ALL_AXES, split_axis=0,...  26.8 us
    all_to_all x1, waiting for transfers between devices, across(): lax.all_to_all(value, SPREAD, split_axis=0, concat_axis=0, axis_index_gro...  24.7 us
    ppermute x2, waiting for transfers between devices, opposite(): return lax.ppermute(value, (DEPTH, CORE), moves)  16.8 us
    pallas_call x1, Pallas kernels, shared_factor(): pl.pallas_call(factor_kernel, out_shape=jax.ShapeDtypeStruct((len(BLOCKS)...  5.77 us
    all_to_all x1, starting transfers between devices, across(): lax.all_to_all(value, SPREAD, split_axis=0, concat_axis=0, axis_index_gro...  5.1 us
    pallas_call x1, Pallas kernels, momentum_call(): pl.pallas_call(functools.partial(kernel, count), grid_spec=pltpu.Prefetch...  4.88 us
    ppermute x2, starting transfers between devices, opposite(): return lax.ppermute(value, (DEPTH, CORE), moves)  3.27 us
  transfers between devices with their start and end apart: 3, of which 3 were waited for; matrix products, arithmetic and copies ran while one was open for 0% of the time, Pallas kernels for 5%

profile of v7, /device:TPU:8, one launch (start us, length us, event | category | flops | bytes accessed | tf_op | source)
XLA Modules:
  0.0 134.0 jit_solution(1282648912974304466)
XLA Ops:
  0.7 0.0 copy-start.3
  0.7 0.6 copy-done.3
  1.3 2.8 %prepare.1 = (f32[256,128]{1,0:T(8,128)S(1)}, bf16[64,32,512]{2,1,0:T(8,128)(2,1)S(1)}, bf16[64,32,512]{2,1,0:T(8,128)(2,1)S(1)}) custom-call(s32[1]{0:T(128)} %bitcast.pair_ref, s32[64]{0:T(128)S(1)} %bitcast.23, bf16[64,32,512]{2,1,0:T(8,128)(2,1)} %bitcast.24, bf16[64,32,512]{2,1,0:T(8,128)(2,1)} %bitcast.26), custom_call_target="tpu_custom_call" | custom-call | flops 2097152 | bytes 8388608 | tf_op jit(solution)/shard_map/prepare/pallas_call | solution.py:87
  4.1 26.8 %all_to_all.15 = f32[256,1,128]{2,1,0:T(1,128)S(1)} all-to-all(f32[256,1,128]{2,1,0:T(1,128)S(1)} %bitcast.21), channel_id=1, replica_groups=mesh['rows_0'=4,'rows_1'=4,'rows_2'=4,'experts_0'=2,'experts_1'=2] {'row..., dimensions={0} | all-to-all | bytes 262144 | tf_op jit(solution)/shard_map/all_to_all | solution.py:390
  30.9 0.0 copy-start.2
  30.9 1.5 %update.1 = bf16[64,32,512]{2,1,0:T(8,128)(2,1)S(1)} custom-call(f32[256,128]{1,0:T(8,128)S(1)} %bitcast.19, bf16[64,32,512]{2,1,0:T(8,128)(2,1)S(1)} %get-tuple-element.8.grad_ref, bf16[64,32,512]{2,1,0:T(8,128)(2,1)S(1)} %get-tuple-element.9.mom_ref), custom_call_target="tpu_custom_call" | custom-call | flops 6291456 | bytes 6291456 | tf_op jit(solution)/shard_map/update/pallas_call | solution.py:149
  32.4 0.0 copy-done.2
  32.4 0.0 copy-start
  32.4 1.3 copy-done
  33.7 5.1 %all-to-all-start.1 = ((bf16[64,32,512]{2,1,0:T(8,128)(2,1)}), bf16[64,32,512]{2,1,0:T(8,128)(2,1)S(1)}, u32[]{:S(2)}, u32[]{:S(2)}) async-start(bf16[64,32,512]{2,1,0:T(8,128)(2,1)} %copy-done), calls=%async_computation.1 | async-start | bytes 4194304 | tf_op jit(solution)/shard_map/all_to_all | solution.py:368
  38.8 4.9 %state.1 = bf16[64,32,512]{2,1,0:T(8,128)(2,1)} custom-call(s32[64]{0:T(128)} %bitcast.22, f32[256,128]{1,0:T(8,128)} %bitcast.20, bf16[64,32,512]{2,1,0:T(8,128)(2,1)} %bitcast.25, bf16[64,32,512]{2,1,0:T(8,128)(2,1)} %bitcast.27), custom_call_target="tpu_custom_call" | custom-call | flops 6291456 | bytes 6291456 | tf_op jit(solution)/shard_map/state/pallas_call | solution.py:185
  43.7 24.7 %all-to-all-done.1 = bf16[64,32,512]{2,1,0:T(8,128)(2,1)S(1)} async-done(((bf16[64,32,512]{2,1,0:T(8,128)(2,1)}), bf16[64,32,512]{2,1,0:T(8,128)(2,1)S(1)}, u32[]{:S(2)}, u32[]{:S(2)}) %all-to-all-start.1) | async-done | bytes 2097184 | tf_op jit(solution)/shard_map/all_to_all | solution.py:368
  68.4 0.7 far.1
  69.2 0.1 collective-permute-start
  69.3 0.7 own.1.own_ref
  70.0 8.9 %collective-permute-done.part_ref = bf16[1280,128]{1,0:T(8,128)(2,1)S(1)} collective-permute-done((bf16[1280,128]{1,0:T(8,128)(2,1)S(1)}, bf16[1280,128]{1,0:T(8,128)(2,1)S(1)}, u32[]{:S(2)}, u32[]{:S(2)}) %collective-permute-start) | collective-permute-done | bytes 327712 | tf_op jit(solution)/shard_map/ppermute | solution.py:379
  78.9 5.8 %factor.1.factor_ref = bf16[1280,128]{1,0:T(8,128)(2,1)S(1)} custom-call(f32[512,512]{1,0:T(8,128)S(1)} %own.1.own_ref, bf16[1280,128]{1,0:T(8,128)(2,1)S(1)} %collective-permute-done.part_ref), custom_call_target="tpu_custom_call" | custom-call | flops 5000000000 | bytes 1048576 | tf_op jit(solution)/shard_map/factor/pallas_call | solution.py:286
  84.7 3.2 %collective-permute-start.1 = (bf16[1280,128]{1,0:T(8,128)(2,1)S(1)}, bf16[1280,128]{1,0:T(8,128)(2,1)S(1)}, u32[]{:S(2)}, u32[]{:S(2)}) collective-permute-start(bf16[1280,128]{1,0:T(8,128)(2,1)S(1)} %factor.1.factor_ref), channel_id=1, source_target_pairs={{0,48},{1,17},{16,32},{17,1},{32,16},{33,49},{48,0},{49,33},{2,50}... | collective-permute-start | bytes 983048 | tf_op jit(solution)/shard_map/ppermute | solution.py:379
  87.9 1.4 %apply.2.refs_0_ = bf16[32,2,32,512]{3,2,1,0:T(8,128)(2,1)S(1)} custom-call(bf16[32,2,32,512]{3,2,1,0:T(8,128)(2,1)S(1)} %bitcast.15, bf16[1280,128]{1,0:T(8,128)(2,1)S(1)} %factor.1.factor_ref), custom_call_target="tpu_custom_call" | custom-call | flops 536870912 | bytes 3145728 | tf_op jit(solution)/shard_map/apply/pallas_call | solution.py:313
  89.3 7.9 %collective-permute-done.1.factor_ref = bf16[1280,128]{1,0:T(8,128)(2,1)S(1)} collective-permute-done((bf16[1280,128]{1,0:T(8,128)(2,1)S(1)}, bf16[1280,128]{1,0:T(8,128)(2,1)S(1)}, u32[]{:S(2)}, u32[]{:S(2)}) %collective-permute-start.1) | collective-permute-done | bytes 327712 | tf_op jit(solution)/shard_map/ppermute | solution.py:379
  97.2 1.4 %apply.3 = bf16[32,2,32,512]{3,2,1,0:T(8,128)(2,1)S(1)} custom-call(bf16[32,2,32,512]{3,2,1,0:T(8,128)(2,1)S(1)} %bitcast.16, bf16[1280,128]{1,0:T(8,128)(2,1)S(1)} %collective-permute-done.1.factor_ref, bf16[32,2,32,512]{3,2,1,0:T(8,128)(2,1)S(1)} %apply.2.refs_0_), custom_call_target="tpu_custom_call", output_to_operand_aliasing={{}: (2, {})} | custom-call | flops 536870912 | bytes 3145728 | tf_op jit(solution)/shard_map/apply/pallas_call | solution.py:313
  98.6 0.0 copy-start.1
  98.6 33.8 %all_to_all.16.ortho_ref = bf16[64,32,512]{2,1,0:T(8,128)(2,1)S(1)} all-to-all(bf16[64,32,512]{2,1,0:T(8,128)(2,1)S(1)} %bitcast.17), channel_id=1, replica_groups={{0,4,8,12,16,20,24,28,64,68,72,76,80,84,88,92,128,132,136,140,144,148,1..., dimensions={0} | all-to-all | bytes 4194304 | tf_op jit(solution)/shard_map/all_to_all | solution.py:368
  132.4 0.0 copy-done.1
  132.4 1.6 %finish.1 = bf16[64,32,512]{2,1,0:T(8,128)(2,1)} custom-call(s32[1]{0:T(128)} %bitcast.pair_ref, bf16[64,32,512]{2,1,0:T(8,128)(2,1)S(1)} %all_to_all.16.ortho_ref, bf16[64,32,512]{2,1,0:T(8,128)(2,1)S(1)} %bitcast.18), custom_call_target="tpu_custom_call" | custom-call | flops 3145728 | bytes 6291456 | tf_op jit(solution)/shard_map/finish/pallas_call | solution.py:351
Async XLA Ops:
  0.7 0.7 copy-start.3
  30.9 1.5 %copy-start.2 = (f32[256,1,128]{2,1,0:T(1,128)}, f32[256,1,128]{2,1,0:T(1,128)S(1)}, u32[]{:S(2)}) copy-start(f32[256,1,128]{2,1,0:T(1,128)S(1)} %all_to_all.15) | copy-start | bytes 393220
  32.4 1.3 copy-start
  33.7 34.7 %all-to-all-start.1 = ((bf16[64,32,512]{2,1,0:T(8,128)(2,1)}), bf16[64,32,512]{2,1,0:T(8,128)(2,1)S(1)}, u32[]{:S(2)}, u32[]{:S(2)}) async-start(bf16[64,32,512]{2,1,0:T(8,128)(2,1)} %copy-done), calls=%async_computation.1 | async-start | bytes 4194304 | tf_op jit(solution)/shard_map/all_to_all | solution.py:368
  69.2 9.7 %collective-permute-start = (bf16[1280,128]{1,0:T(8,128)(2,1)S(1)}, bf16[1280,128]{1,0:T(8,128)(2,1)S(1)}, u32[]{:S(2)}, u32[]{:S(2)}) collective-permute-start(bf16[1280,128]{1,0:T(8,128)(2,1)S(1)} %far.1), channel_id=1, source_target_pairs={{0,48},{1,17},{16,32},{17,1},{32,16},{33,49},{48,0},{49,33},{2,50}... | collective-permute-start | bytes 983048 | tf_op jit(solution)/shard_map/ppermute | solution.py:379
  84.7 12.5 %collective-permute-start.1 = (bf16[1280,128]{1,0:T(8,128)(2,1)S(1)}, bf16[1280,128]{1,0:T(8,128)(2,1)S(1)}, u32[]{:S(2)}, u32[]{:S(2)}) collective-permute-start(bf16[1280,128]{1,0:T(8,128)(2,1)S(1)} %factor.1.factor_ref), channel_id=1, source_target_pairs={{0,48},{1,17},{16,32},{17,1},{32,16},{33,49},{48,0},{49,33},{2,50}... | collective-permute-start | bytes 983048 | tf_op jit(solution)/shard_map/ppermute | solution.py:379
  98.6 33.8 %copy-start.1 = (bf16[1,64,32,512]{3,2,1,0:T(8,128)(2,1)S(1)}, bf16[1,64,32,512]{3,2,1,0:T(8,128)(2,1)}, u32[]{:S(2)}) copy-start(bf16[1,64,32,512]{3,2,1,0:T(8,128)(2,1)} %param.4) | copy-start | bytes 6291460
